TPU v7x, 32 devices: a whole 2x2x4 slice. The times are simulated.
32 devices in a mesh: dp: 2 (over core), blk: 4 (over y, x), rep: 4 (over z).
Axes of the slice: x: 2, y: 2, z: 4, core: 2. Of those that a mesh axis runs over, the one named last changes fastest.
Arguments:
- feats: bfloat16 [2, 16384, 512], P('dp', ('blk', 'rep')), may hold values from -6 to 6
- weight: bfloat16 [512, 512], replicated, may hold values from -0.25 to 0.25
- cols: int32 [2, 128, 15], P('dp', ('blk', 'rep')), may hold values from -1 to 127, as said below
- vals: bfloat16 [2, 128, 15, 128, 128], P('dp', ('blk', 'rep')), as said below
- cotangent: bfloat16 [2, 16384, 512], P('dp', ('blk', 'rep')), may hold values from -6 to 6
Outputs:
- activ: bfloat16 [2, 16384, 512], P('dp', ('blk', 'rep'))
- feat_grad: bfloat16 [2, 16384, 512], P('dp', ('blk', 'rep'))
- weight_grad: float32 [512, 512], replicated
Inputs may be any that keep to these rules, and one draw needn't show every extreme that they name: `cols`: used slots come first in each row and -1 marks the unused ones. Slot 0 of block row p names p itself; every other used slot names a block at most 7 away from p, each at most once. The relation is symmetric: p names q exactly when q names p. In every scenario some block row uses all 15 slots. `vals`: the block in row p's slot naming q is the transpose of the block in row q's slot naming p (the self block is symmetric); unused slots hold zeros.
All inputs are finite; a program needn't handle non-finite values.
Results may differ from a plain program's by a relative error of at most 0.0061.
Values may be sent and summed in bfloat16 or wider, within the bound.
No kernel may reach another device: no remote copies, remote signals or barrier semaphores. Data moves between devices by JAX's collectives and lax.ppermute only.
A program may use at most 128 MiB of HBM per device.

v0:
```python
import jax
import jax.numpy as jnp
from jax import lax
from jax.sharding import PartitionSpec as P

REACH = 7


def padded(cells, sides, width):
    for axis, dim in sides:
        count = lax.axis_size(axis)
        ends = count - 1
        head = lax.slice_in_dim(cells, 0, width, axis=dim)
        tail = lax.slice_in_dim(cells, cells.shape[dim] - width, cells.shape[dim], axis=dim)
        cells = jnp.concatenate(
            [
                lax.ppermute(tail, axis, [(i, (i + 1) % count) for i in range(ends)]),
                cells,
                lax.ppermute(head, axis, [((i + 1) % count, i) for i in range(ends)]),
            ],
            axis=dim,
        )
    return cells


def spread(extended, row_cols, row_vals, first):
    row_blocks = row_vals.shape[0]
    block_size = row_vals.shape[2]
    width = extended.shape[1]
    ext_blocks = extended.reshape(-1, block_size, width)
    margin = (ext_blocks.shape[0] - row_blocks) // 2
    local_index = jnp.where(row_cols >= 0, row_cols - first + margin, 0)
    picked = ext_blocks[local_index]
    summed = jnp.einsum("rkab,rkbf->raf", row_vals, picked, preferred_element_type=jnp.float32)
    return summed.reshape(-1, width)


def shards(feats, weight, cols, vals, cotangent):
    first = lax.axis_index(("blk", "rep")) * cols.shape[1]
    rim_rows = REACH * vals.shape[3]
    own = feats[0]
    projected = jnp.dot(own, weight, preferred_element_type=jnp.float32).astype(jnp.bfloat16)
    extended = padded(projected, ((("blk", "rep"), 0),), rim_rows)
    agg = spread(extended, cols[0], vals[0], first)
    sig = jax.nn.sigmoid(agg)
    activ_list = [(agg * sig).astype(jnp.bfloat16)]
    dagg = (cotangent[0].astype(jnp.float32) * sig * (1.0 + agg * (1.0 - sig))).astype(jnp.bfloat16)
    grad_ext = padded(dagg, ((("blk", "rep"), 0),), rim_rows)
    dproj = spread(grad_ext, cols[0], vals[0], first).astype(jnp.bfloat16)
    back = lax.dot_general(
        dproj, weight, (((1,), (1,)), ((), ())), preferred_element_type=jnp.float32
    )
    grad_list = [back.astype(jnp.bfloat16)]
    grads = lax.dot_general(
        own, dproj, (((0,), (0,)), ((), ())), preferred_element_type=jnp.float32
    )
    weight_grad = lax.psum(grads, ("dp", "blk", "rep"))
    return (jnp.stack(activ_list), jnp.stack(grad_list), weight_grad)


def solution(mesh):
    placed = (
        P("dp", ("blk", "rep"), None),
        P(),
        P("dp", ("blk", "rep"), None),
        P("dp", ("blk", "rep"), None, None, None),
        P("dp", ("blk", "rep"), None),
    )
    return jax.shard_map(
        shards,
        mesh=mesh,
        in_specs=placed,
        out_specs=(P("dp", ("blk", "rep"), None), P("dp", ("blk", "rep"), None), P()),
        check_vma=False,
    )
```

profile of v0, /device:TPU:0, one launch (start us, length us, event | category | flops | bytes accessed | tf_op | source)
XLA Modules:
  0.0 287.8 jit_solution(11901660477694064899)
XLA Ops:
  7.2 0.0 copy-start
  7.2 0.0 all-reduce.2.cloned.1.call-start
  7.2 1.2 copy-done
  8.4 1.7 convolution_convert_fusion.1
  10.1 1.1 fusion.16
  11.2 5.9 %collective-permute-start = (bf16[896,512]{1,0:T(8,128)(2,1)}, bf16[896,512]{1,0:T(8,128)(2,1)}, u32[]{:S(2)}, u32[]{:S(2)}) collective-permute-start(bf16[896,512]{1,0:T(8,128)(2,1)} %get-tuple-element.8), channel_id=1, source_target_pairs={{0,1},{1,2},{2,3},{3,4},{4,5},{5,6},{6,7},{7,8},{8,9},{9,10},{10,1... | collective-permute-start | bytes 2752520 | tf_op jit(solution)/shard_map/ppermute | solution.py:17
  17.1 1.3 collective-permute-start.1
  18.4 0.1 reshape.102
  18.5 17.5 %collective-permute-done = bf16[896,512]{1,0:T(8,128)(2,1)} collective-permute-done((bf16[896,512]{1,0:T(8,128)(2,1)}, bf16[896,512]{1,0:T(8,128)(2,1)}, u32[]{:S(2)}, u32[]{:S(2)}) %collective-permute-start) | collective-permute-done | bytes 917536 | tf_op jit(solution)/shard_map/ppermute | solution.py:17
  36.1 23.3 %collective-permute-done.1 = bf16[896,512]{1,0:T(8,128)(2,1)} collective-permute-done((bf16[896,512]{1,0:T(8,128)(2,1)S(1)}, bf16[896,512]{1,0:T(8,128)(2,1)}, u32[]{:S(2)}, u32[]{:S(2)}) %collective-permute-start.1) | collective-permute-done | bytes 917536 | tf_op jit(solution)/shard_map/ppermute | solution.py:19
  59.3 3.2 %pad_maximum_fusion = bf16[2816,512]{1,0:T(8,128)(2,1)} fusion(bf16[896,512]{1,0:T(8,128)(2,1)} %collective-permute-done.1, bf16[1024,512]{1,0:T(8,128)(2,1)S(1)} %convolution_convert_fusion.1, bf16[896,512]{1,0:T(8,128)(2,1)} %collective-permute-done), kind=kLoop, calls=%fused_computation.6 | loop fusion | flops 8650752 | bytes 5767168 | tf_op jit(solution)/shard_map/concatenate | solution.py:15
  62.6 9.5 %gather_fusion = bf16[120,128,512]{2,1,0:T(8,128)(2,1)} fusion(bf16[22,128,512]{2,1,0:T(8,128)(2,1)} %bitcast.62, s32[1024]{0:T(1024)S(1)} %pad_clamp_fusion), kind=kCustom, calls=%fused_computation | custom fusion | bytes 31457760 | tf_op jit(solution)/shard_map/gather | solution.py:33
  72.0 8.2 %fusion = f32[8,512,128,1]{1,2,3,0:T(8,128)S(1)} fusion(bf16[8,15,128,512]{3,2,1,0:T(8,128)(2,1)} %bitcast.64, bf16[1,8,15,128,128]{4,3,2,1,0:T(8,128)(2,1)} %param.8), kind=kOutput, calls=%fused_computation.2 | convolution fusion | flops 2013265920 | bytes 21757952 | tf_op jit(solution)/shard_map/rkab,rkbf->raf/dot_general | solution.py:34
  80.3 0.8 fusion.5
  81.1 0.1 fusion.15
  81.2 2.7 collective-permute-start.2
  83.9 1.3 collective-permute-start.3
  85.2 18.5 %collective-permute-done.2 = bf16[896,512]{1,0:T(8,128)(2,1)S(1)} collective-permute-done((bf16[896,512]{1,0:T(8,128)(2,1)S(1)}, bf16[896,512]{1,0:T(8,128)(2,1)S(1)}, u32[]{:S(2)}, u32[]{:S(2)}) %collective-permute-start.2) | collective-permute-done | bytes 917536 | tf_op jit(solution)/shard_map/ppermute | solution.py:17
  103.7 23.8 %collective-permute-done.3 = bf16[896,512]{1,0:T(8,128)(2,1)S(1)} collective-permute-done((bf16[896,512]{1,0:T(8,128)(2,1)S(1)}, bf16[896,512]{1,0:T(8,128)(2,1)S(1)}, u32[]{:S(2)}, u32[]{:S(2)}) %collective-permute-start.3) | collective-permute-done | bytes 917536 | tf_op jit(solution)/shard_map/ppermute | solution.py:19
  127.5 1.8 pad_maximum_fusion.1
  129.3 9.5 %gather_fusion.1 = bf16[120,128,512]{2,1,0:T(8,128)(2,1)} fusion(bf16[22,128,512]{2,1,0:T(8,128)(2,1)} %bitcast.61, s32[1024]{0:T(1024)S(1)} %pad_clamp_fusion), kind=kCustom, calls=%fused_computation.1 | custom fusion | bytes 31457760 | tf_op jit(solution)/shard_map/gather | solution.py:33
  138.8 9.0 %bitcast_convert_fusion = bf16[8,512,128]{1,2,0:T(8,128)(2,1)S(1)} fusion(bf16[8,15,128,512]{3,2,1,0:T(8,128)(2,1)} %bitcast.63, bf16[1,8,15,128,128]{4,3,2,1,0:T(8,128)(2,1)} %param.8), kind=kOutput, calls=%fused_computation.11 | convolution fusion | flops 2013790208 | bytes 20709376 | tf_op jit(solution)/shard_map/rkab,rkbf->raf/dot_general | solution.py:34
  147.8 0.0 copy-start.1
  147.8 1.0 copy-done.1
  148.8 1.7 convolution_bitcast_fusion
  150.5 0.0 all-reduce.2.cloned.1.call-update
  150.6 0.0 copy-start.2
  150.6 0.0 copy-start.5
  150.6 1.5 multiply_convert_fusion
  152.1 1.7 fusion.12
  153.8 124.6 %all-reduce.2.cloned.1.call-done = f32[512,512]{0,1:T(8,128)} async-done(((f32[512,512]{0,1:T(8,128)}), f32[512,512]{0,1:T(8,128)}) %all-reduce.2.cloned.1.call-update) | async-done | bytes 1048592 | tf_op jit(solution)/shard_map/psum | solution.py:57
  278.4 2.5 copy.8
  (8 shorter events, 0.0 us)
Async XLA Ops:
  7.2 1.2 copy-start
  7.2 11.2 %copy-start.4 = (s32[1,8,15]{2,1,0:T(8,128)S(1)}, s32[1,8,15]{2,1,0:T(8,128)}, u32[]{:S(2)}) copy-start(s32[1,8,15]{2,1,0:T(8,128)} %param.7) | copy-start | bytes 1444
  7.2 271.2 %all-reduce.2.cloned.1.call-start = ((), (), s32[]{:S(2)}) async-start(), calls=%async_computation | async-start | bytes 2097152 | tf_op jit(solution)/shard_map/psum | solution.py:57
  11.2 24.8 %collective-permute-start = (bf16[896,512]{1,0:T(8,128)(2,1)}, bf16[896,512]{1,0:T(8,128)(2,1)}, u32[]{:S(2)}, u32[]{:S(2)}) collective-permute-start(bf16[896,512]{1,0:T(8,128)(2,1)} %get-tuple-element.8), channel_id=1, source_target_pairs={{0,1},{1,2},{2,3},{3,4},{4,5},{5,6},{6,7},{7,8},{8,9},{9,10},{10,1... | collective-permute-start | bytes 2752520 | tf_op jit(solution)/shard_map/ppermute | solution.py:17
  17.1 42.2 %collective-permute-start.1 = (bf16[896,512]{1,0:T(8,128)(2,1)S(1)}, bf16[896,512]{1,0:T(8,128)(2,1)}, u32[]{:S(2)}, u32[]{:S(2)}) collective-permute-start(bf16[896,512]{1,0:T(8,128)(2,1)S(1)} %get-tuple-element.9), channel_id=1, source_target_pairs={{1,0},{2,1},{3,2},{4,3},{5,4},{6,5},{7,6},{8,7},{9,8},{10,9},{11,1... | collective-permute-start | bytes 2752520 | tf_op jit(solution)/shard_map/ppermute | solution.py:19
  72.0 8.2 %copy-start.3 = (bf16[1,1024,512]{2,1,0:T(8,128)(2,1)S(1)}, bf16[1,1024,512]{2,1,0:T(8,128)(2,1)}, u32[]{:S(2)}) copy-start(bf16[1,1024,512]{2,1,0:T(8,128)(2,1)} %param.9) | copy-start | bytes 3145732
  81.2 22.5 %collective-permute-start.2 = (bf16[896,512]{1,0:T(8,128)(2,1)S(1)}, bf16[896,512]{1,0:T(8,128)(2,1)S(1)}, u32[]{:S(2)}, u32[]{:S(2)}) collective-permute-start(bf16[896,512]{1,0:T(8,128)(2,1)S(1)} %get-tuple-element.6), channel_id=1, source_target_pairs={{0,1},{1,2},{2,3},{3,4},{4,5},{5,6},{6,7},{7,8},{8,9},{9,10},{10,1... | collective-permute-start | bytes 2752520 | tf_op jit(solution)/shard_map/ppermute | solution.py:17
  83.9 43.6 %collective-permute-start.3 = (bf16[896,512]{1,0:T(8,128)(2,1)S(1)}, bf16[896,512]{1,0:T(8,128)(2,1)S(1)}, u32[]{:S(2)}, u32[]{:S(2)}) collective-permute-start(bf16[896,512]{1,0:T(8,128)(2,1)S(1)} %get-tuple-element.7), channel_id=1, source_target_pairs={{1,0},{2,1},{3,2},{4,3},{5,4},{6,5},{7,6},{8,7},{9,8},{10,9},{11,1... | collective-permute-start | bytes 2752520 | tf_op jit(solution)/shard_map/ppermute | solution.py:19
  147.8 1.0 copy-start.1
  150.6 1.5 copy-start.2
  150.6 1.5 copy-start.5
Sparse Core Ops, SparseCore 0:
  150.7 127.6 all-reduce.1
where the time goes:
time: 288 us
  waiting for transfers between devices  208 us (72%)
  local copies, waits for them, and re-layouts  25 us (9%)
  matrix products  22.4 us (8%)
  between operations  14.2 us (5%)
  starting transfers between devices  11.2 us (4%)
  other arithmetic  7.32 us (3%)
    psum x1, waiting for transfers between devices, shards(): weight_grad = lax.psum(grads, ('dp', 'blk', 'rep'))  125 us
    ppermute x2, waiting for transfers between devices, padded(): lax.ppermute(head, axis, [((i + 1) % count, i) for i in range(ends)])  47.1 us
    ppermute x2, waiting for transfers between devices, padded(): lax.ppermute(tail, axis, [(i, (i + 1) % count) for i in range(ends)])  36 us
    gather x2, local copies, waits for them, and re-layouts, spread(): picked = ext_blocks[local_index]  19 us
    dot_general x2, matrix products, spread(): jnp.einsum('rkab,rkbf->raf', row_vals, picked, preferred_element_type=jnp...  17.2 us
    ppermute x2, starting transfers between devices, padded(): lax.ppermute(tail, axis, [(i, (i + 1) % count) for i in range(ends)])  8.55 us
  transfers between devices with their start and end apart: 5, of which 5 were waited for; matrix products, arithmetic and copies ran while one was open for 1% of the time, Pallas kernels for 0%

commit v1 on v0

v1 whole, which is shorter than its diff:
```python
import functools

import jax
import jax.numpy as jnp
from jax import lax
from jax.experimental import pallas as pl
from jax.experimental.pallas import tpu as pltpu
from jax.sharding import PartitionSpec as P

REACH = 7
PAIR = 2
LINE = ("blk", "rep")
VMEM_BYTES = 40 << 20


def whole():
    return pl.BlockSpec(memory_space=pltpu.VMEM)


def held(x):
    return pltpu.with_memory_space_constraint(x, pltpu.VMEM)


def window(tile, rows):
    start = PAIR * tile
    before = REACH - start if start < REACH else 0
    own = min(rows, start + 2 * REACH + PAIR - REACH) - max(0, start - REACH)
    return start, before, own


def lanes(blocks_ref, tile, positions):
    return jnp.concatenate([blocks_ref[tile, q] for q in positions], axis=1)


def build_kernel(place_ref, vals_ref, feats_ref, band_ref, near_ref, sems):
    rows, slots = place_ref.shape
    tiles, span, height, size = band_ref.shape

    def clear(i, _):
        t, q = i // span, i % span
        band_ref[t, q] = jnp.zeros((height, size), band_ref.dtype)
        return 0

    lax.fori_loop(0, tiles * span, clear, 0)

    def copy(r, k, at):
        return pltpu.make_async_copy(
            vals_ref.at[r, k],
            band_ref.at[r // PAIR, at - PAIR * (r // PAIR), pl.ds((r % PAIR) * size, size)],
            sems.at[r, k],
        )

    for r in range(rows):
        for k in range(slots):
            at = place_ref[r, k]

            @pl.when(at >= 0)
            def _():
                copy(r, k, at).start()

    for t in range(tiles):
        for r in range(PAIR * t, PAIR * (t + 1)):
            for k in range(slots):
                at = place_ref[r, k]

                @pl.when(at >= 0)
                def _():
                    copy(r, k, at).wait()

        near_ref[pl.ds(t * height, height), :] = own_part(band_ref, t, feats_ref[...])


def own_part(band_ref, t, own):
    rows = own.shape[0] // band_ref.shape[3]
    begin = REACH - PAIR * t
    return jnp.dot(
        lanes(band_ref, t, range(begin, begin + rows)), own, preferred_element_type=jnp.float32
    )


def halo_part(band_ref, t, rows, before_ref, after_ref):
    size = band_ref.shape[3]
    span = band_ref.shape[1]
    begin = REACH - PAIR * t
    positions = [*range(begin), *range(begin + rows, span)]
    source = jnp.concatenate(
        [before_ref[PAIR * t * size :, :], after_ref[: (span - begin - rows) * size, :]], axis=0
    )
    return jnp.dot(lanes(band_ref, t, positions), source, preferred_element_type=jnp.float32)


def layer_kernel(band_ref, near_ref, before_ref, after_ref, weight_ref, cot_ref,
                 mixed_ref, activ_ref, low_ref, high_ref):
    tiles, span, height, size = band_ref.shape
    rows = tiles * PAIR
    ends = (rows - REACH) * size
    for t in range(tiles):
        at = pl.ds(t * height, height)
        mixed = near_ref[at, :] + halo_part(band_ref, t, rows, before_ref, after_ref)
        mixed = mixed.astype(jnp.bfloat16)
        mixed_ref[at, :] = mixed
        agg = jnp.dot(mixed, weight_ref[...], preferred_element_type=jnp.float32)
        sig = jax.nn.sigmoid(agg)
        activ_ref[at, :] = (agg * sig).astype(activ_ref.dtype)
        dagg = cot_ref[at, :].astype(jnp.float32) * sig * (1.0 + agg * (1.0 - sig))
        dagg = dagg.astype(jnp.bfloat16)
        skip = max(0, (t + 1) * height - low_ref.shape[0])
        low_ref[pl.ds(t * height, height - skip), :] = dagg[: height - skip]
        skip = max(0, ends - t * height)
        high_ref[pl.ds(t * height + skip - ends, height - skip), :] = dagg[skip:]


def near_kernel(band_ref, low_ref, high_ref, near_ref):
    tiles, span, height, size = band_ref.shape
    missing = tiles * height - low_ref.shape[0]
    own = jnp.concatenate([low_ref[...], high_ref[high_ref.shape[0] - missing :, :]], axis=0)
    for t in range(tiles):
        near_ref[pl.ds(t * height, height), :] = own_part(band_ref, t, own)


def back_kernel(band_ref, near_ref, before_ref, after_ref, weight_ref, out_ref):
    tiles, span, height, size = band_ref.shape
    rows = tiles * PAIR
    for t in range(tiles):
        at = pl.ds(t * height, height)
        dproj = near_ref[at, :] + halo_part(band_ref, t, rows, before_ref, after_ref)
        back = lax.dot_general(
            dproj.astype(jnp.bfloat16), weight_ref[...], (((1,), (1,)), ((), ())),
            preferred_element_type=jnp.float32,
        )
        out_ref[at, :] = back.astype(out_ref.dtype)


def kernel_call(body, outs, flops, traffic, specs, **more):
    return pl.pallas_call(
        body,
        out_shape=outs,
        in_specs=specs,
        out_specs=[whole()] * len(outs),
        compiler_params=pltpu.CompilerParams(vmem_limit_bytes=VMEM_BYTES),
        cost_estimate=pl.CostEstimate(flops=flops, bytes_accessed=traffic, transcendentals=0),
        **more,
    )


def along(x, step):
    count = lax.axis_size(LINE)
    pairs = [(i, i + step) for i in range(count) if 0 <= i + step < count]
    return lax.ppermute(x, LINE, pairs)


def partner(j, d, n):
    return j ^ d if n & (n - 1) == 0 else (j + d) % n


def scatter_sum(x, axis):
    n = lax.axis_size(axis)
    me = lax.axis_index(axis)
    step = x.shape[0] // n
    total = lax.dynamic_slice_in_dim(x, me * step, step)
    arrived = []
    for d in range(1, n):
        part = lax.dynamic_slice_in_dim(x, partner(me, d, n) * step, step)
        arrived.append(lax.ppermute(part, axis, [(j, partner(j, d, n)) for j in range(n)]))
    for part in arrived:
        total = total + part
    return total


def collect(x, axis):
    n = lax.axis_size(axis)
    me = lax.axis_index(axis)
    step = x.shape[0]
    out = jnp.zeros((n * step, x.shape[1]), x.dtype)
    out = lax.dynamic_update_slice_in_dim(out, x, me * step, 0)
    for d in range(1, n):
        part = lax.ppermute(x, axis, [(j, partner(j, d, n)) for j in range(n)])
        origin = me ^ d if n & (n - 1) == 0 else (me - d) % n
        out = lax.dynamic_update_slice_in_dim(out, part, origin * step, 0)
    return out


def shards(feats, weight, cols, vals, cotangent):
    rows, slots = cols.shape[1:]
    size = vals.shape[3]
    width = feats.shape[2]
    zones = rows * size
    tiles = rows // PAIR
    span = 2 * REACH + PAIR
    rim = REACH * size
    own = feats[0]

    before = along(own[zones - rim :], 1)
    after = along(own[:rim], -1)
    first = lax.axis_index(LINE) * rows
    place = jnp.where(cols[0] >= 0, cols[0] - first + REACH, -1)

    product = 2 * zones * zones * width
    band, near = kernel_call(
        build_kernel,
        [pltpu.VMEM((tiles, span, PAIR * size, size), jnp.bfloat16), pltpu.VMEM((zones, width), jnp.float32)],
        product, 8 << 20,
        [pl.BlockSpec(memory_space=pltpu.SMEM), pl.BlockSpec(memory_space=pl.ANY), whole()],
        scratch_shapes=[pltpu.SemaphoreType.DMA((rows, slots))],
    )(place, vals[0], own)

    mixed, activ, low, high = kernel_call(
        layer_kernel,
        [
            jax.ShapeDtypeStruct((zones, width), jnp.bfloat16),
            jax.ShapeDtypeStruct((zones, width), jnp.bfloat16),
            jax.ShapeDtypeStruct((rim, width), jnp.bfloat16),
            jax.ShapeDtypeStruct((rim, width), jnp.bfloat16),
        ],
        product * 3 // 2, 8 << 20, [whole()] * 6,
    )(held(band), held(near), before, after, weight, cotangent[0])

    before = along(high, 1)
    after = along(low, -1)
    near = kernel_call(
        near_kernel, [pltpu.VMEM((zones, width), jnp.float32)], product, 8 << 20, [whole()] * 3
    )(held(band), low, high)[0]
    dagg = jnp.concatenate([low, high[2 * rim - zones :]], axis=0)
    term = lax.dot_general(
        mixed, dagg, (((0,), (0,)), ((), ())), preferred_element_type=jnp.float32
    )
    for axis in ("dp", "blk", "rep"):
        term = scatter_sum(term, axis)
    term = term.astype(jnp.bfloat16)
    for axis in ("rep", "blk", "dp"):
        term = collect(term, axis)
    weight_grad = term.astype(jnp.float32)

    feat_grad = kernel_call(
        back_kernel, [jax.ShapeDtypeStruct((zones, width), jnp.bfloat16)],
        product * 3 // 2, 8 << 20, [whole()] * 5,
    )(held(band), held(near), before, after, weight)[0]
    return activ[None], feat_grad[None], weight_grad


def solution(mesh):
    placed = (
        P("dp", LINE, None),
        P(),
        P("dp", LINE, None),
        P("dp", LINE, None, None, None),
        P("dp", LINE, None),
    )
    return jax.shard_map(
        shards,
        mesh=mesh,
        in_specs=placed,
        out_specs=(P("dp", LINE, None), P("dp", LINE, None), P()),
        check_vma=False,
    )
```

time: 288 us -> 131 us (0.45)
  waiting for transfers between devices: 208 us -> 76.4 us
  matrix products: 22.4 us -> 0.73 us
  local copies, waits for them, and re-layouts: 25 us -> 9.23 us
  Pallas kernels: 0 us -> 15.2 us
  starting transfers between devices: 11.2 us -> 26.2 us
  between operations: 14.2 us -> 0.91 us
  other arithmetic: 7.32 us -> 2.29 us
    psum x1 -> x0, waiting for transfers between devices: 125 us -> none  [shards(): weight_grad = lax.psum(grads, ('dp', 'blk', 'rep'))]
    dot_general x5 -> x1, matrix products: 22.4 us -> 0.73 us  [shards(): lax.dot_general(mixed, dagg, (((0,), (0,)), ((), ())), preferred_element_...]
    gather x2 -> x0, local copies, waits for them, and re-layouts: 19 us -> none  [spread(): picked = ext_blocks[local_index]]
    pallas_call x0 -> x4, Pallas kernels: none -> 15.2 us  [the longest x1 7.39 us: shards(): kernel_call(build_kernel, [pltpu.VMEM((tiles, span, PAIR * size, size), j...]
    ppermute x4 -> x18, starting transfers between devices: 11.1 us -> 26.2 us  [the longest x4 9.51 us: along(): return lax.ppermute(x, LINE, pairs)]
    ppermute x4 -> x18, waiting for transfers between devices: 83.2 us -> 76.4 us  [the longest x7 36.3 us: collect(): part = lax.ppermute(x, axis, [(j, partner(j, d, n)) for j in range(n)])]
    concatenate x2 -> x0, other arithmetic: 4.97 us -> none  [padded(): jnp.concatenate([lax.ppermute(tail, axis, [(i, (i + 1) % count) for i in...]
  transfers between devices with their start and end apart: 5 -> 18, of which waited for: 5 -> 11; matrix products, arithmetic and copies ran while one was open for 1% -> 0% of each run, Pallas kernels for 0% -> 9%
where the time goes in v1:
time: 131 us
  waiting for transfers between devices  76.4 us (58%)
  starting transfers between devices  26.2 us (20%)
  Pallas kernels  15.2 us (12%)
  local copies, waits for them, and re-layouts  9.23 us (7%)
  other arithmetic  2.29 us (2%)
    ppermute x7, waiting for transfers between devices, collect(): part = lax.ppermute(x, axis, [(j, partner(j, d, n)) for j in range(n)])  36.3 us
    ppermute x4, waiting for transfers between devices, along(): return lax.ppermute(x, LINE, pairs)  32.2 us
    ppermute x4, starting transfers between devices, along(): return lax.ppermute(x, LINE, pairs)  9.51 us
    ppermute x7, starting transfers between devices, collect(): part = lax.ppermute(x, axis, [(j, partner(j, d, n)) for j in range(n)])  8.71 us
    ppermute x7, waiting for transfers between devices, scatter_sum(): lax.ppermute(part, axis, [(j, partner(j, d, n)) for j in range(n)])  7.97 us
    ppermute x7, starting transfers between devices, scatter_sum(): lax.ppermute(part, axis, [(j, partner(j, d, n)) for j in range(n)])  7.96 us
    pallas_call x1, Pallas kernels, shards(): kernel_call(build_kernel, [pltpu.VMEM((tiles, span, PAIR * size, size), j...  7.39 us
    unnamed x20, local copies, waits for them, and re-layouts  5.43 us
  transfers between devices with their start and end apart: 18, of which 11 were waited for; matrix products, arithmetic and copies ran while one was open for 0% of the time, Pallas kernels for 9%

profile of v1, /device:TPU:0, one launch (start us, length us, event | category | flops | bytes accessed | tf_op | source)
XLA Modules:
  0.0 130.9 jit_solution(10196059375747552118)
XLA Ops:
  0.6 2.9 %slice_bitcast_fusion = (bf16[896,512]{1,0:T(8,128)(2,1)}, bf16[896,512]{1,0:T(8,128)(2,1)}) fusion(bf16[1,1024,512]{2,1,0:T(8,128)(2,1)} %param.5), kind=kLoop, calls=%fused_computation.4 | loop fusion | bytes 3670016 | tf_op jit(solution)/shard_map/slice | solution.py:194
  3.5 5.0 %collective-permute-start = (bf16[896,512]{1,0:T(8,128)(2,1)}, bf16[896,512]{1,0:T(8,128)(2,1)S(1)}, u32[]{:S(2)}, u32[]{:S(2)}) collective-permute-start(bf16[896,512]{1,0:T(8,128)(2,1)} %get-tuple-element.18), channel_id=1, source_target_pairs={{0,1},{1,2},{2,3},{3,4},{4,5},{5,6},{6,7},{7,8},{8,9},{9,10},{10,1... | collective-permute-start | bytes 2752520 | tf_op jit(solution)/shard_map/ppermute | solution.py:149
  8.5 1.3 collective-permute-start.1
  9.9 2.1 %copy-done.3 = bf16[1,8,15,128,128]{4,3,2,1,0:T(8,128)(2,1)S(1)} copy-done((bf16[1,8,15,128,128]{4,3,2,1,0:T(8,128)(2,1)S(1)}, bf16[1,8,15,128,128]{4,3,2,1,0:T(8,128)(2,1)}, u32[]{:S(2)}) %copy-start.3) | copy-done | bytes 3932184
  12.0 7.4 %shard_map.76 = (bf16[4,16,256,128]{3,2,1,0:T(8,128)(2,1)S(1)}, f32[1024,512]{1,0:T(8,128)S(1)}) custom-call(s32[8,15]{1,0:T(8,128)S(1)} %select_bitcast_fusion.place_ref, bf16[8,15,128,128]{3,2,1,0:T(8,128)(2,1)S(1)} %bitcast.13, bf16[1024,512]{1,0:T(8,128)(2,1)S(1)} %bitcast.12), custom_call_target="tpu_custom_call" | custom-call | flops 1073741824 | bytes 8388608 | tf_op jit(solution)/shard_map/pallas_call | solution.py:199
  19.4 9.0 %collective-permute-done.before_ref = bf16[896,512]{1,0:T(8,128)(2,1)S(1)} collective-permute-done((bf16[896,512]{1,0:T(8,128)(2,1)}, bf16[896,512]{1,0:T(8,128)(2,1)S(1)}, u32[]{:S(2)}, u32[]{:S(2)}) %collective-permute-start) | collective-permute-done | bytes 917536 | tf_op jit(solution)/shard_map/ppermute | solution.py:149
  28.4 23.2 %collective-permute-done.1.after_ref = bf16[896,512]{1,0:T(8,128)(2,1)S(1)} collective-permute-done((bf16[896,512]{1,0:T(8,128)(2,1)}, bf16[896,512]{1,0:T(8,128)(2,1)S(1)}, u32[]{:S(2)}, u32[]{:S(2)}) %collective-permute-start.1) | collective-permute-done | bytes 917536 | tf_op jit(solution)/shard_map/ppermute | solution.py:149
  51.6 3.4 %shard_map.77 = (bf16[1024,512]{1,0:T(8,128)(2,1)S(1)}, bf16[1024,512]{1,0:T(8,128)(2,1)}, bf16[896,512]{1,0:T(8,128)(2,1)S(1)}, bf16[896,512]{1,0:T(8,128)(2,1)S(1)}) custom-call(bf16[4,16,256,128]{3,2,1,0:T(8,128)(2,1)S(1)} %get-tuple-element.9.band_ref, f32[1024,512]{1,0:T(8,128)S(1)} %get-tuple-element.10.near_ref, ...), custom_call_target="tpu_custom_call" | custom-call | flops 1610612736 | bytes 8388608 | tf_op jit(solution)/shard_map/pallas_call | solution.py:207
  56.0 0.9 copy-done.8
  56.9 1.9 %collective-permute-done.4 = f32[256,512]{1,0:T(8,128)S(1)} collective-permute-done((f32[256,512]{1,0:T(8,128)S(1)}, f32[256,512]{1,0:T(8,128)S(1)}, u32[]{:S(2)}, u32[]{:S(2)}) %collective-permute-start.4) | collective-permute-done | bytes 524320 | tf_op jit(solution)/shard_map/ppermute | solution.py:164
  58.8 1.1 dynamic-slice_add_fusion
  60.6 1.5 %collective-permute-start.5 = (f32[64,512]{1,0:T(8,128)}, f32[64,512]{1,0:T(8,128)S(1)}, u32[]{:S(2)}, u32[]{:S(2)}) collective-permute-start(f32[64,512]{1,0:T(8,128)} %get-tuple-element.19), channel_id=1, source_target_pairs={{0,4},{4,0},{8,12},{12,8},{1,5},{5,1},{9,13},{13,9},{2,6},{6,2},{1... | collective-permute-start | bytes 393224 | tf_op jit(solution)/shard_map/ppermute | solution.py:164
  62.2 2.0 %collective-permute-start.7 = (f32[64,512]{1,0:T(8,128)S(1)}, f32[64,512]{1,0:T(8,128)S(1)}, u32[]{:S(2)}, u32[]{:S(2)}) collective-permute-start(f32[64,512]{1,0:T(8,128)S(1)} %get-tuple-element.20), channel_id=1, source_target_pairs={{0,12},{4,8},{8,4},{12,0},{1,13},{5,9},{9,5},{13,1},{2,14},{6,10},... | collective-permute-start | bytes 393224 | tf_op jit(solution)/shard_map/ppermute | solution.py:164
  64.1 2.8 %collective-permute-done.5 = f32[64,512]{1,0:T(8,128)S(1)} collective-permute-done((f32[64,512]{1,0:T(8,128)}, f32[64,512]{1,0:T(8,128)S(1)}, u32[]{:S(2)}, u32[]{:S(2)}) %collective-permute-start.5) | collective-permute-done | bytes 131104 | tf_op jit(solution)/shard_map/ppermute | solution.py:164
  67.0 1.2 collective-permute-done.6
  68.2 2.0 %collective-permute-done.7 = f32[64,512]{1,0:T(8,128)S(1)} collective-permute-done((f32[64,512]{1,0:T(8,128)S(1)}, f32[64,512]{1,0:T(8,128)S(1)}, u32[]{:S(2)}, u32[]{:S(2)}) %collective-permute-start.7) | collective-permute-done | bytes 131104 | tf_op jit(solution)/shard_map/ppermute | solution.py:164
  70.3 1.8 %collective-permute-start.10 = (f32[16,512]{1,0:T(8,128)S(1)}, f32[16,512]{1,0:T(8,128)S(1)}, u32[]{:S(2)}, u32[]{:S(2)}) collective-permute-start(f32[16,512]{1,0:T(8,128)S(1)} %get-tuple-element.23), channel_id=1, source_target_pairs={{0,3},{1,2},{2,1},{3,0},{4,7},{5,6},{6,5},{7,4},{8,11},{9,10},{10,... | collective-permute-start | bytes 98312 | tf_op jit(solution)/shard_map/ppermute | solution.py:164
  72.1 2.7 %collective-permute-start.9 = (f32[16,512]{1,0:T(8,128)S(1)}, f32[16,512]{1,0:T(8,128)S(1)}, u32[]{:S(2)}, u32[]{:S(2)}) collective-permute-start(f32[16,512]{1,0:T(8,128)S(1)} %get-tuple-element.24), channel_id=1, source_target_pairs={{0,2},{1,3},{2,0},{3,1},{4,6},{5,7},{6,4},{7,5},{8,10},{9,11},{10,... | collective-permute-start | bytes 98312 | tf_op jit(solution)/shard_map/ppermute | solution.py:164
  74.7 2.0 %collective-permute-start.2 = (bf16[896,512]{1,0:T(8,128)(2,1)S(1)}, bf16[896,512]{1,0:T(8,128)(2,1)S(1)}, u32[]{:S(2)}, u32[]{:S(2)}) collective-permute-start(bf16[896,512]{1,0:T(8,128)(2,1)S(1)} %get-tuple-element.13.high_ref), channel_id=1, source_target_pairs={{0,1},{1,2},{2,3},{3,4},{4,5},{5,6},{6,7},{7,8},{8,9},{9,10},{10,1... | collective-permute-start | bytes 2752520 | tf_op jit(solution)/shard_map/ppermute | solution.py:149
  76.7 1.3 collective-permute-start.3
  78.1 2.7 %collective-permute-start.11 = (bf16[16,512]{1,0:T(8,128)(2,1)S(1)}, bf16[16,512]{1,0:T(8,128)(2,1)S(1)}, u32[]{:S(2)}, u32[]{:S(2)}) collective-permute-start(bf16[16,512]{1,0:T(8,128)(2,1)S(1)} %get-tuple-element.16), channel_id=1, source_target_pairs={{0,1},{1,0},{2,3},{3,2},{4,5},{5,4},{6,7},{7,6},{8,9},{9,8},{10,11... | collective-permute-start | bytes 49160 | tf_op jit(solution)/shard_map/ppermute | solution.py:177
  80.8 2.2 %copy-done.1 = bf16[4,16,256,128]{3,2,1,0:T(8,128)(2,1)S(1)} copy-done((bf16[4,16,256,128]{3,2,1,0:T(8,128)(2,1)S(1)}, bf16[4,16,256,128]{3,2,1,0:T(8,128)(2,1)}, u32[]{:S(2)}) %copy-start.1) | copy-done | bytes 4194328
  83.0 1.2 shard_map.78.near_ref
  84.2 2.4 %collective-permute-start.12 = (bf16[16,512]{1,0:T(8,128)(2,1)S(1)}, bf16[16,512]{1,0:T(8,128)(2,1)S(1)}, u32[]{:S(2)}, u32[]{:S(2)}) collective-permute-start(bf16[16,512]{1,0:T(8,128)(2,1)S(1)} %get-tuple-element.16), channel_id=1, source_target_pairs={{0,2},{1,3},{2,0},{3,1},{4,6},{5,7},{6,4},{7,5},{8,10},{9,11},{10,... | collective-permute-start | bytes 49160 | tf_op jit(solution)/shard_map/ppermute | solution.py:177
  86.6 32.5 %collective-permute-done.11 = bf16[16,512]{1,0:T(8,128)(2,1)S(1)} collective-permute-done((bf16[16,512]{1,0:T(8,128)(2,1)S(1)}, bf16[16,512]{1,0:T(8,128)(2,1)S(1)}, u32[]{:S(2)}, u32[]{:S(2)}) %collective-permute-start.11) | collective-permute-done | bytes 16416 | tf_op jit(solution)/shard_map/ppermute | solution.py:177
  119.4 1.9 %collective-permute-start.14 = (bf16[64,512]{1,0:T(8,128)(2,1)S(1)}, bf16[64,512]{1,0:T(8,128)(2,1)S(1)}, u32[]{:S(2)}, u32[]{:S(2)}) collective-permute-start(bf16[64,512]{1,0:T(8,128)(2,1)S(1)} %constant_dynamic-update-slice_fusion.6), channel_id=1, source_target_pairs={{0,4},{4,0},{8,12},{12,8},{1,5},{5,1},{9,13},{13,9},{2,6},{6,2},{1... | collective-permute-start | bytes 196616 | tf_op jit(solution)/shard_map/ppermute | solution.py:177
  121.3 1.6 %collective-permute-start.16 = (bf16[64,512]{1,0:T(8,128)(2,1)S(1)}, bf16[64,512]{1,0:T(8,128)(2,1)S(1)}, u32[]{:S(2)}, u32[]{:S(2)}) collective-permute-start(bf16[64,512]{1,0:T(8,128)(2,1)S(1)} %constant_dynamic-update-slice_fusion.6), channel_id=1, source_target_pairs={{0,12},{4,8},{8,4},{12,0},{1,13},{5,9},{9,5},{13,1},{2,14},{6,10},... | collective-permute-start | bytes 196616 | tf_op jit(solution)/shard_map/ppermute | solution.py:177
  123.0 0.8 collective-permute-done.14
  123.8 1.8 %collective-permute-done.15 = bf16[64,512]{1,0:T(8,128)(2,1)S(1)} collective-permute-done((bf16[64,512]{1,0:T(8,128)(2,1)S(1)}, bf16[64,512]{1,0:T(8,128)(2,1)S(1)}, u32[]{:S(2)}, u32[]{:S(2)}) %collective-permute-start.15) | collective-permute-done | bytes 65568 | tf_op jit(solution)/shard_map/ppermute | solution.py:177
  125.6 0.9 collective-permute-done.16
  126.7 3.1 %shard_map.79 = bf16[1024,512]{1,0:T(8,128)(2,1)} custom-call(bf16[4,16,256,128]{3,2,1,0:T(8,128)(2,1)S(1)} %copy-done.1, f32[1024,512]{1,0:T(8,128)S(1)} %shard_map.78.near_ref, bf16[896,512]{1,0:T(8,128)(2,1)S(1)} %collective-permute-done.2.before_ref, bf16[896,512]{1,0:T(8,128)(2,1)S(1)} %collective-permute-done.3.after_ref, bf16[512,512]{1,0:T(8,128)(2,1)S(1)} %copy-done.4), custom_call_target="tpu_custom_call" | custom-call | flops 1610612736 | bytes 8388608 | tf_op jit(solution)/shard_map/pallas_call | solution.py:234
  129.8 1.1 convert_element_type.7
  (51 shorter events, 2.5 us)
Async XLA Ops:
  0.6 9.2 %copy-start.2 = (bf16[1,1024,512]{2,1,0:T(8,128)(2,1)S(1)}, bf16[1,1024,512]{2,1,0:T(8,128)(2,1)}, u32[]{:S(2)}) copy-start(bf16[1,1024,512]{2,1,0:T(8,128)(2,1)} %param.5) | copy-start | bytes 3145732
  0.6 9.2 %copy-start.9 = (s32[1,8,15]{2,1,0:T(8,128)S(1)}, s32[1,8,15]{2,1,0:T(8,128)}, u32[]{:S(2)}) copy-start(s32[1,8,15]{2,1,0:T(8,128)} %param.7) | copy-start | bytes 1444
  3.5 24.8 %collective-permute-start = (bf16[896,512]{1,0:T(8,128)(2,1)}, bf16[896,512]{1,0:T(8,128)(2,1)S(1)}, u32[]{:S(2)}, u32[]{:S(2)}) collective-permute-start(bf16[896,512]{1,0:T(8,128)(2,1)} %get-tuple-element.18), channel_id=1, source_target_pairs={{0,1},{1,2},{2,3},{3,4},{4,5},{5,6},{6,7},{7,8},{8,9},{9,10},{10,1... | collective-permute-start | bytes 2752520 | tf_op jit(solution)/shard_map/ppermute | solution.py:149
  8.5 43.0 %collective-permute-start.1 = (bf16[896,512]{1,0:T(8,128)(2,1)}, bf16[896,512]{1,0:T(8,128)(2,1)S(1)}, u32[]{:S(2)}, u32[]{:S(2)}) collective-permute-start(bf16[896,512]{1,0:T(8,128)(2,1)} %get-tuple-element.17), channel_id=1, source_target_pairs={{1,0},{2,1},{3,2},{4,3},{5,4},{6,5},{7,6},{8,7},{9,8},{10,9},{11,1... | collective-permute-start | bytes 2752520 | tf_op jit(solution)/shard_map/ppermute | solution.py:149
  9.9 2.1 %copy-start.3 = (bf16[1,8,15,128,128]{4,3,2,1,0:T(8,128)(2,1)S(1)}, bf16[1,8,15,128,128]{4,3,2,1,0:T(8,128)(2,1)}, u32[]{:S(2)}) copy-start(bf16[1,8,15,128,128]{4,3,2,1,0:T(8,128)(2,1)} %param.8) | copy-start | bytes 11796484
  12.0 39.6 %copy-start.4 = (bf16[512,512]{1,0:T(8,128)(2,1)S(1)}, bf16[512,512]{1,0:T(8,128)(2,1)}, u32[]{:S(2)}) copy-start(bf16[512,512]{1,0:T(8,128)(2,1)} %weight_ref.3) | copy-start | bytes 1572868
  12.0 39.6 %copy-start.5 = (bf16[1,1024,512]{2,1,0:T(8,128)(2,1)S(1)}, bf16[1,1024,512]{2,1,0:T(8,128)(2,1)}, u32[]{:S(2)}) copy-start(bf16[1,1024,512]{2,1,0:T(8,128)(2,1)} %param.9) | copy-start | bytes 3145732
  19.4 35.6 %copy-start = (bf16[4,16,256,128]{3,2,1,0:T(8,128)(2,1)}, bf16[4,16,256,128]{3,2,1,0:T(8,128)(2,1)S(1)}, u32[]{:S(2)}) copy-start(bf16[4,16,256,128]{3,2,1,0:T(8,128)(2,1)S(1)} %get-tuple-element.9.band_ref) | copy-start | bytes 12582916
  55.0 0.9 copy-start.6
  55.9 1.0 copy-start.8
  56.9 19.8 %copy-start.7 = (bf16[896,512]{1,0:T(8,128)(2,1)S(1)}, bf16[896,512]{1,0:T(8,128)(2,1)}, u32[]{:S(2)}) copy-start(bf16[896,512]{1,0:T(8,128)(2,1)} %copy-done.6) | copy-start | bytes 2752516
  56.9 1.9 %collective-permute-start.4 = (f32[256,512]{1,0:T(8,128)S(1)}, f32[256,512]{1,0:T(8,128)S(1)}, u32[]{:S(2)}, u32[]{:S(2)}) collective-permute-start(f32[256,512]{1,0:T(8,128)S(1)} %constant_dynamic-slice_fusion.6), channel_id=1, source_target_pairs={{0,16},{16,0},{1,17},{17,1},{2,18},{18,2},{3,19},{19,3},{4,20},{20... | collective-permute-start | bytes 1572872 | tf_op jit(solution)/shard_map/ppermute | solution.py:164
  60.6 6.3 %collective-permute-start.5 = (f32[64,512]{1,0:T(8,128)}, f32[64,512]{1,0:T(8,128)S(1)}, u32[]{:S(2)}, u32[]{:S(2)}) collective-permute-start(f32[64,512]{1,0:T(8,128)} %get-tuple-element.19), channel_id=1, source_target_pairs={{0,4},{4,0},{8,12},{12,8},{1,5},{5,1},{9,13},{13,9},{2,6},{6,2},{1... | collective-permute-start | bytes 393224 | tf_op jit(solution)/shard_map/ppermute | solution.py:164
  62.1 6.1 %collective-permute-start.6 = (f32[64,512]{1,0:T(8,128)S(1)}, f32[64,512]{1,0:T(8,128)S(1)}, u32[]{:S(2)}, u32[]{:S(2)}) collective-permute-start(f32[64,512]{1,0:T(8,128)S(1)} %get-tuple-element.21), channel_id=1, source_target_pairs={{0,8},{4,12},{8,0},{12,4},{1,9},{5,13},{9,1},{13,5},{2,10},{6,14},... | collective-permute-start | bytes 393224 | tf_op jit(solution)/shard_map/ppermute | solution.py:164
  62.2 8.0 %collective-permute-start.7 = (f32[64,512]{1,0:T(8,128)S(1)}, f32[64,512]{1,0:T(8,128)S(1)}, u32[]{:S(2)}, u32[]{:S(2)}) collective-permute-start(f32[64,512]{1,0:T(8,128)S(1)} %get-tuple-element.20), channel_id=1, source_target_pairs={{0,12},{4,8},{8,4},{12,0},{1,13},{5,9},{9,5},{13,1},{2,14},{6,10},... | collective-permute-start | bytes 393224 | tf_op jit(solution)/shard_map/ppermute | solution.py:164
  70.3 7.7 %collective-permute-start.10 = (f32[16,512]{1,0:T(8,128)S(1)}, f32[16,512]{1,0:T(8,128)S(1)}, u32[]{:S(2)}, u32[]{:S(2)}) collective-permute-start(f32[16,512]{1,0:T(8,128)S(1)} %get-tuple-element.23), channel_id=1, source_target_pairs={{0,3},{1,2},{2,1},{3,0},{4,7},{5,6},{6,5},{7,4},{8,11},{9,10},{10,... | collective-permute-start | bytes 98312 | tf_op jit(solution)/shard_map/ppermute | solution.py:164
  72.1 5.9 %collective-permute-start.8 = (f32[16,512]{1,0:T(8,128)S(1)}, f32[16,512]{1,0:T(8,128)S(1)}, u32[]{:S(2)}, u32[]{:S(2)}) collective-permute-start(f32[16,512]{1,0:T(8,128)S(1)} %get-tuple-element.22), channel_id=1, source_target_pairs={{0,1},{1,0},{2,3},{3,2},{4,5},{5,4},{6,7},{7,6},{8,9},{9,8},{10,11... | collective-permute-start | bytes 98312 | tf_op jit(solution)/shard_map/ppermute | solution.py:164
  72.1 5.9 %collective-permute-start.9 = (f32[16,512]{1,0:T(8,128)S(1)}, f32[16,512]{1,0:T(8,128)S(1)}, u32[]{:S(2)}, u32[]{:S(2)}) collective-permute-start(f32[16,512]{1,0:T(8,128)S(1)} %get-tuple-element.24), channel_id=1, source_target_pairs={{0,2},{1,3},{2,0},{3,1},{4,6},{5,7},{6,4},{7,5},{8,10},{9,11},{10,... | collective-permute-start | bytes 98312 | tf_op jit(solution)/shard_map/ppermute | solution.py:164
  74.7 51.9 %collective-permute-start.2 = (bf16[896,512]{1,0:T(8,128)(2,1)S(1)}, bf16[896,512]{1,0:T(8,128)(2,1)S(1)}, u32[]{:S(2)}, u32[]{:S(2)}) collective-permute-start(bf16[896,512]{1,0:T(8,128)(2,1)S(1)} %get-tuple-element.13.high_ref), channel_id=1, source_target_pairs={{0,1},{1,2},{2,3},{3,4},{4,5},{5,6},{6,7},{7,8},{8,9},{9,10},{10,1... | collective-permute-start | bytes 2752520 | tf_op jit(solution)/shard_map/ppermute | solution.py:149
  76.7 50.0 %collective-permute-start.3 = (bf16[896,512]{1,0:T(8,128)(2,1)S(1)}, bf16[896,512]{1,0:T(8,128)(2,1)S(1)}, u32[]{:S(2)}, u32[]{:S(2)}) collective-permute-start(bf16[896,512]{1,0:T(8,128)(2,1)S(1)} %copy-done.7), channel_id=1, source_target_pairs={{1,0},{2,1},{3,2},{4,3},{5,4},{6,5},{7,6},{8,7},{9,8},{10,9},{11,1... | collective-permute-start | bytes 2752520 | tf_op jit(solution)/shard_map/ppermute | solution.py:149
  78.1 41.0 %collective-permute-start.11 = (bf16[16,512]{1,0:T(8,128)(2,1)S(1)}, bf16[16,512]{1,0:T(8,128)(2,1)S(1)}, u32[]{:S(2)}, u32[]{:S(2)}) collective-permute-start(bf16[16,512]{1,0:T(8,128)(2,1)S(1)} %get-tuple-element.16), channel_id=1, source_target_pairs={{0,1},{1,0},{2,3},{3,2},{4,5},{5,4},{6,7},{7,6},{8,9},{9,8},{10,11... | collective-permute-start | bytes 49160 | tf_op jit(solution)/shard_map/ppermute | solution.py:177
  80.8 2.2 %copy-start.1 = (bf16[4,16,256,128]{3,2,1,0:T(8,128)(2,1)S(1)}, bf16[4,16,256,128]{3,2,1,0:T(8,128)(2,1)}, u32[]{:S(2)}) copy-start(bf16[4,16,256,128]{3,2,1,0:T(8,128)(2,1)} %copy-done) | copy-start | bytes 12582916
  84.2 34.9 %collective-permute-start.12 = (bf16[16,512]{1,0:T(8,128)(2,1)S(1)}, bf16[16,512]{1,0:T(8,128)(2,1)S(1)}, u32[]{:S(2)}, u32[]{:S(2)}) collective-permute-start(bf16[16,512]{1,0:T(8,128)(2,1)S(1)} %get-tuple-element.16), channel_id=1, source_target_pairs={{0,2},{1,3},{2,0},{3,1},{4,6},{5,7},{6,4},{7,5},{8,10},{9,11},{10,... | collective-permute-start | bytes 49160 | tf_op jit(solution)/shard_map/ppermute | solution.py:177
  86.6 32.9 %collective-permute-start.13 = (bf16[16,512]{1,0:T(8,128)(2,1)S(1)}, bf16[16,512]{1,0:T(8,128)(2,1)S(1)}, u32[]{:S(2)}, u32[]{:S(2)}) collective-permute-start(bf16[16,512]{1,0:T(8,128)(2,1)S(1)} %get-tuple-element.16), channel_id=1, source_target_pairs={{0,3},{1,2},{2,1},{3,0},{4,7},{5,6},{6,5},{7,4},{8,11},{9,10},{10,... | collective-permute-start | bytes 49160 | tf_op jit(solution)/shard_map/ppermute | solution.py:177
  119.4 4.3 %collective-permute-start.14 = (bf16[64,512]{1,0:T(8,128)(2,1)S(1)}, bf16[64,512]{1,0:T(8,128)(2,1)S(1)}, u32[]{:S(2)}, u32[]{:S(2)}) collective-permute-start(bf16[64,512]{1,0:T(8,128)(2,1)S(1)} %constant_dynamic-update-slice_fusion.6), channel_id=1, source_target_pairs={{0,4},{4,0},{8,12},{12,8},{1,5},{5,1},{9,13},{13,9},{2,6},{6,2},{1... | collective-permute-start | bytes 196616 | tf_op jit(solution)/shard_map/ppermute | solution.py:177
  121.3 4.3 %collective-permute-start.15 = (bf16[64,512]{1,0:T(8,128)(2,1)S(1)}, bf16[64,512]{1,0:T(8,128)(2,1)S(1)}, u32[]{:S(2)}, u32[]{:S(2)}) collective-permute-start(bf16[64,512]{1,0:T(8,128)(2,1)S(1)} %constant_dynamic-update-slice_fusion.6), channel_id=1, source_target_pairs={{0,8},{4,12},{8,0},{12,4},{1,9},{5,13},{9,1},{13,5},{2,10},{6,14},... | collective-permute-start | bytes 196616 | tf_op jit(solution)/shard_map/ppermute | solution.py:177
  121.3 5.2 %collective-permute-start.16 = (bf16[64,512]{1,0:T(8,128)(2,1)S(1)}, bf16[64,512]{1,0:T(8,128)(2,1)S(1)}, u32[]{:S(2)}, u32[]{:S(2)}) collective-permute-start(bf16[64,512]{1,0:T(8,128)(2,1)S(1)} %constant_dynamic-update-slice_fusion.6), channel_id=1, source_target_pairs={{0,12},{4,8},{8,4},{12,0},{1,13},{5,9},{9,5},{13,1},{2,14},{6,10},... | collective-permute-start | bytes 196616 | tf_op jit(solution)/shard_map/ppermute | solution.py:177
  126.5 3.3 %collective-permute-start.17 = (bf16[256,512]{1,0:T(8,128)(2,1)S(1)}, bf16[256,512]{1,0:T(8,128)(2,1)S(1)}, u32[]{:S(2)}, u32[]{:S(2)}) collective-permute-start(bf16[256,512]{1,0:T(8,128)(2,1)S(1)} %constant_dynamic-update-slice_fusion.2), channel_id=1, source_target_pairs={{0,16},{16,0},{1,17},{17,1},{2,18},{18,2},{3,19},{19,3},{4,20},{20... | collective-permute-start | bytes 786440 | tf_op jit(solution)/shard_map/ppermute | solution.py:177

commit v2 on v0

v2 whole, which is shorter than its diff:
```python
import jax
import jax.numpy as jnp
from jax import lax
from jax.experimental import pallas as pl
from jax.experimental.pallas import tpu as pltpu
from jax.sharding import PartitionSpec as P

REACH = 7
PAIR = 2
LINE = ("blk", "rep")
LEVEL = ("dp", "blk")
VMEM_BYTES = 14 << 20
BF16, F32 = jnp.bfloat16, jnp.float32


def whole():
    return pl.BlockSpec(memory_space=pltpu.VMEM)


def anywhere():
    return pl.BlockSpec(memory_space=pl.ANY)


def held(*arrays):
    return [pltpu.with_memory_space_constraint(x, pltpu.VMEM) for x in arrays]


def place():
    return lax.axis_index(LINE[0]) * lax.axis_size(LINE[1]) + lax.axis_index(LINE[1])


def is_odd():
    return lax.rem(place(), 2)


def by_parity(body):
    odd = is_odd()

    @pl.when(odd == 0)
    def _():
        body(1, 0)

    @pl.when(odd == 1)
    def _():
        body(0, 1)


def before(blocks):
    return [b - 1 for b in blocks]


def mine(blocks):
    return [REACH + b for b in blocks]


def after(blocks):
    return [2 * REACH + 1 + b for b in blocks]


def banded(band_ref, t, sources):
    size = band_ref.shape[3]
    left, right = [], []
    for indices, ref in sources:
        for i, w in enumerate(indices):
            if 0 <= w - PAIR * t < band_ref.shape[1]:
                left.append(band_ref[t, w - PAIR * t])
                right.append(ref[i * size : (i + 1) * size, :])
    return jnp.dot(
        jnp.concatenate(left, axis=1), jnp.concatenate(right, axis=0), preferred_element_type=F32
    )


def cut_kernel(feats_ref, *refs):
    outs, sems = refs[:-1], refs[-1]
    size = feats_ref.shape[0] // (REACH + 1)
    odd = is_odd()
    copies = []
    for i, (out, even_first, odd_first) in enumerate(zip(outs, (3, 0, 1, 5), (0, 3, 5, 1))):
        first = jnp.where(odd == 0, even_first, odd_first)
        source = feats_ref.at[pl.ds(pl.multiple_of(first * size, size), out.shape[0])]
        copies.append(pltpu.make_async_copy(source, out, sems.at[i]))
        copies[-1].start()
    for copy in copies:
        copy.wait()


def build_kernel(cols_ref, vals_ref, feats_ref, band_ref, near_ref, sems):
    rows, slots = cols_ref.shape
    tiles, span, height, size = band_ref.shape
    first = place() * rows - REACH

    def clear(i, _):
        band_ref[i // span, i % span] = jnp.zeros((height, size), band_ref.dtype)
        return 0

    lax.fori_loop(0, tiles * span, clear, 0)

    def each(r, act):
        for k in range(slots):
            column = cols_ref[r, k]

            @pl.when(column >= 0)
            def _():
                act(
                    pltpu.make_async_copy(
                        vals_ref.at[r, k],
                        band_ref.at[
                            r // PAIR, column - first - PAIR * (r // PAIR), pl.ds((r % PAIR) * size, size)
                        ],
                        sems.at[r, k],
                    )
                )

    for r in range(rows):
        each(r, lambda copy: copy.start())
    for t in range(tiles):
        for r in range(PAIR * t, PAIR * (t + 1)):
            each(r, lambda copy: copy.wait())
        near_ref[pl.ds(t * height, height), :] = banded(
            band_ref, t, [(mine(range(rows)), feats_ref)]
        )


def tile_step(band_ref, near_ref, sources, t, weight_ref, cot_ref):
    height = band_ref.shape[2]
    at = pl.ds(t * height, height)
    mixed = (near_ref[at, :] + banded(band_ref, t, sources)).astype(BF16)
    agg = jnp.dot(mixed, weight_ref[...], preferred_element_type=F32)
    sig = jax.nn.sigmoid(agg)
    dagg = cot_ref[at, :].astype(F32) * sig * (1.0 + agg * (1.0 - sig))
    return mixed, dagg.astype(BF16)


def inner_kernel(band_ref, near_ref, first5_ref, second5_ref, weight_ref, cot_ref,
                 mixed_ref, third_ref, fifth_ref):
    height = band_ref.shape[2]
    five = (first5_ref, second5_ref)

    def body(left, right):
        sources = [(before(range(3, 8)), five[left]), (after(range(5)), five[right])]
        for i, (t, out) in enumerate(((1, third_ref), (2, fifth_ref))):
            mixed, dagg = tile_step(band_ref, near_ref, sources, t, weight_ref, cot_ref)
            mixed_ref[pl.ds(i * height, height), :] = mixed
            out[...] = dagg

    by_parity(body)


def outer_kernel(band_ref, near_ref, first5_ref, second5_ref, first2_ref, second2_ref, weight_ref, cot_ref,
                 mixed_ref, low_ref, high_ref, first3_ref, second3_ref):
    size = band_ref.shape[3]
    height = PAIR * size
    five, two = (first5_ref, second5_ref), (first2_ref, second2_ref)
    three = (first3_ref, second3_ref)

    def body(left, right):
        sources = [
            (before(range(1, 3)), two[left]),
            (before(range(3, 8)), five[left]),
            (after(range(5)), five[right]),
            (after(range(5, 7)), two[right]),
        ]
        mixed, dagg = tile_step(band_ref, near_ref, sources, 0, weight_ref, cot_ref)
        mixed_ref[:height, :] = mixed
        low_ref[...] = dagg
        for out in three:
            out[:size, :] = dagg[size:]
        three[left][2 * size :, :] = dagg[:size]
        mixed, dagg = tile_step(band_ref, near_ref, sources, 3, weight_ref, cot_ref)
        mixed_ref[height:, :] = mixed
        high_ref[...] = dagg
        for out in three:
            out[size : 2 * size, :] = dagg[:size]
        three[right][2 * size :, :] = dagg[size:]

    by_parity(body)


def gather_kernel(band_ref, low_ref, third_ref, fifth_ref, high_ref, first_ref, second_ref,
                  mixed_mid_ref, mixed_end_ref, weight_ref, near_ref, activ_ref):
    tiles, _, height, _ = band_ref.shape
    came = (first_ref, second_ref)

    def body(left, right):
        sources = [
            (before((2, 3)), came[left]),
            (mine((0, 1)), low_ref),
            (mine((2, 3)), third_ref),
            (mine((4, 5)), fifth_ref),
            (mine((6, 7)), high_ref),
            (after((2, 3)), came[right]),
        ]
        for t in range(tiles):
            near_ref[pl.ds(t * height, height), :] = banded(band_ref, t, sources)

    by_parity(body)
    halves = (mixed_end_ref[:height, :], mixed_mid_ref[:height, :], mixed_mid_ref[height:, :], mixed_end_ref[height:, :])
    for t, mixed in enumerate(halves):
        agg = jnp.dot(mixed, weight_ref[...], preferred_element_type=F32)
        activ_ref[pl.ds(t * height, height), :] = (agg * jax.nn.sigmoid(agg)).astype(activ_ref.dtype)


def add_kernel(band_ref, near_ref, first_ref, second_ref, out_ref):
    tiles, _, height, _ = band_ref.shape
    came = (first_ref, second_ref)

    def body(left, right):
        sources = [(before((4, 5)), came[left]), (after((4, 5)), came[right])]
        for t in range(tiles):
            at = pl.ds(t * height, height)
            out_ref[at, :] = near_ref[at, :] + banded(band_ref, t, sources)

    by_parity(body)


def back_kernel(band_ref, near_ref, first3_ref, second3_ref, weight_ref, out_ref, held_ref, sems):
    tiles, _, height, _ = band_ref.shape
    came = (first3_ref, second3_ref)

    def body(left, right):
        sources = [(before((1, 6, 7)), came[left]), (after((1, 6, 0)), came[right])]
        copies = []
        for t in range(tiles):
            at = pl.ds(t * height, height)
            dproj = near_ref[at, :] + banded(band_ref, t, sources)
            held_ref[at, :] = lax.dot_general(
                dproj.astype(BF16), weight_ref[...], (((1,), (1,)), ((), ())), preferred_element_type=F32
            ).astype(BF16)
            copies.append(pltpu.make_async_copy(held_ref.at[at], out_ref.at[at], sems.at[t]))
            copies[-1].start()
        for copy in copies:
            copy.wait()

    by_parity(body)


def kernel_call(body, ins, outs, cost, specs=None, out_specs=None, **more):
    return pl.pallas_call(
        body,
        out_shape=outs,
        in_specs=specs or [whole()] * len(ins),
        out_specs=out_specs or [whole()] * len(outs),
        compiler_params=pltpu.CompilerParams(vmem_limit_bytes=VMEM_BYTES),
        cost_estimate=pl.CostEstimate(flops=cost, bytes_accessed=0, transcendentals=0),
        **more,
    )(*ins)


def swapped(first, second):
    count = lax.axis_size(LINE)
    result = []
    for x, start in ((first, 0), (second, 1)):
        pairs = [(i, i + 1) for i in range(start, count - 1, 2)]
        result.append(lax.ppermute(x, LINE, pairs + [(j, i) for i, j in pairs]))
    return result


def traded(x, axes):
    return lax.all_to_all(x.astype(BF16), axes, 0, 0, tiled=True)


def shared(x, axes):
    return traded(jnp.broadcast_to(x[None], (lax.axis_size(axes), *x.shape)), axes)


def total(parts):
    return jnp.sum(parts.astype(F32), axis=0)


def term_of(mixed, dagg):
    return lax.dot_general(mixed, dagg, (((0,), (0,)), ((), ())), preferred_element_type=F32)


def shards(feats, weight, cols, vals, cotangent):
    rows, slots = cols.shape[1:]
    size = vals.shape[3]
    width = feats.shape[2]
    zones = rows * size
    tiles = rows // PAIR
    height = PAIR * size
    span = 2 * REACH + PAIR
    own = feats[0]
    product = zones * zones * width

    def chip(blocks, dtype=BF16):
        return pltpu.VMEM((blocks * size, width), dtype)

    def plain(blocks, dtype=BF16):
        return jax.ShapeDtypeStruct((blocks * size, width), dtype)

    cut = kernel_call(
        cut_kernel, [pltpu.with_memory_space_constraint(own, pltpu.HBM)],
        [chip(5), chip(5), chip(2), chip(2)], 0, [anywhere()],
        scratch_shapes=[pltpu.SemaphoreType.DMA((4,))],
    )
    five = swapped(*cut[:2])
    two = swapped(*cut[2:])

    band, near = kernel_call(
        build_kernel, [cols[0], vals[0], own],
        [pltpu.VMEM((tiles, span, height, size), BF16), chip(rows, F32)], 4 * product,
        [pl.BlockSpec(memory_space=pltpu.SMEM), anywhere(), whole()],
        scratch_shapes=[pltpu.SemaphoreType.DMA((rows, slots))],
    )
    band, near = held(band, near)
    mixed_mid, third, fifth = kernel_call(
        inner_kernel, [band, near, *five, weight, cotangent[0]], [chip(4), chip(2), chip(2)], product
    )
    came_third = swapped(third, third)
    came_fifth = swapped(fifth, fifth)
    mixed_end, low, high, *three = kernel_call(
        outer_kernel, [band, near, *five, *two, weight, cotangent[0]],
        [chip(4), chip(2), chip(2), chip(3), chip(3)], product,
    )
    near, activ = kernel_call(
        gather_kernel, [band, low, third, fifth, high, *came_third, mixed_mid, mixed_end, weight],
        [chip(rows, F32), plain(rows)], 4 * product,
    )
    term = term_of(mixed_mid, jnp.concatenate([third, fifth])) + term_of(mixed_end, jnp.concatenate([low, high]))
    term = traded(term.reshape(lax.axis_size(LEVEL), -1, width), LEVEL)
    term, near = lax.optimization_barrier((term, near))
    term = total(term)
    term, *three = lax.optimization_barrier((term, *three))
    term = shared(term, ("rep",))
    three = swapped(*three)
    near = kernel_call(add_kernel, [band, near, *came_fifth], [chip(rows, F32)], 12 * product)[0]
    term, near = lax.optimization_barrier((term, near))
    term = shared(total(term), LEVEL)
    feat_grad = kernel_call(
        back_kernel, [band, near, *three, weight], [plain(rows)], 4 * product,
        out_specs=[anywhere()],
        scratch_shapes=[pltpu.VMEM((zones, width), BF16), pltpu.SemaphoreType.DMA((tiles,))],
    )[0]
    term, feat_grad = lax.optimization_barrier((term, feat_grad))
    weight_grad = term.reshape(-1, width).astype(F32)
    return activ[None], feat_grad[None], weight_grad


def solution(mesh):
    placed = (
        P("dp", LINE, None),
        P(),
        P("dp", LINE, None),
        P("dp", LINE, None, None, None),
        P("dp", LINE, None),
    )
    return jax.shard_map(
        shards,
        mesh=mesh,
        in_specs=placed,
        out_specs=(P("dp", LINE, None), P("dp", LINE, None), P()),
        check_vma=False,
    )
```

time: 288 us -> 111 us (0.39)
  the two profiles are of different devices: /device:TPU:0 before, /device:TPU:7 now
where the time goes in v2:
time: 111 us; the launch traced here: 110 us
  starting transfers between devices  45.1 us (41%)
  waiting for transfers between devices  21.5 us (19%)
  Pallas kernels  19.7 us (18%)
  local copies, waits for them, and re-layouts  16.7 us (15%)
  other arithmetic  4.25 us (4%)
  matrix products  1.72 us (2%)
    ppermute x10, starting transfers between devices, swapped(): result.append(lax.ppermute(x, LINE, pairs + [(j, i) for i, j in pairs]))  28.9 us
    pallas_call x7, Pallas kernels, kernel_call(): pl.pallas_call(body, out_shape=outs, in_specs=specs or [whole()] * len(in...  19.7 us
    ppermute x10, waiting for transfers between devices, swapped(): result.append(lax.ppermute(x, LINE, pairs + [(j, i) for i, j in pairs]))  18.8 us
    all_to_all x3, starting transfers between devices, traded(): return lax.all_to_all(x.astype(BF16), axes, 0, 0, tiled=True)  16.2 us
    unnamed x26, local copies, waits for them, and re-layouts  15.2 us
    all_to_all x3, waiting for transfers between devices, traded(): return lax.all_to_all(x.astype(BF16), axes, 0, 0, tiled=True)  2.65 us
  transfers between devices with their start and end apart: 13, of which 4 were waited for; matrix products, arithmetic and copies ran while one was open for 5% of the time, Pallas kernels for 17%

profile of v2, /device:TPU:7, one launch (start us, length us, event | category | flops | bytes accessed | tf_op | source)
XLA Modules:
  0.0 109.9 jit_solution(1422972761261538128)
XLA Ops:
  0.6 1.5 %shard_map.77 = (bf16[640,512]{1,0:T(8,128)(2,1)S(1)}, bf16[640,512]{1,0:T(8,128)(2,1)S(1)}, bf16[256,512]{1,0:T(8,128)(2,1)S(1)}, bf16[256,512]{1,0:T(8,128)(2,1)S(1)}) custom-call(bf16[1024,512]{1,0:T(8,128)(2,1)} %bitcast.14), custom_call_target="tpu_custom_call" | custom-call | tf_op jit(solution)/shard_map/pallas_call | solution.py:238
  2.1 1.4 %collective-permute-start = (bf16[640,512]{1,0:T(8,128)(2,1)S(1)}, bf16[640,512]{1,0:T(8,128)(2,1)S(1)}, u32[]{:S(2)}, u32[]{:S(2)}) collective-permute-start(bf16[640,512]{1,0:T(8,128)(2,1)S(1)} %get-tuple-element.30), channel_id=1, source_target_pairs={{0,1},{2,3},{4,5},{6,7},{8,9},{10,11},{12,13},{14,15},{1,0},{3,2},... | collective-permute-start | bytes 1966088 | tf_op jit(solution)/shard_map/ppermute | solution.py:254
  3.5 4.1 %collective-permute-start.1 = (bf16[640,512]{1,0:T(8,128)(2,1)S(1)}, bf16[640,512]{1,0:T(8,128)(2,1)S(1)}, u32[]{:S(2)}, u32[]{:S(2)}) collective-permute-start(bf16[640,512]{1,0:T(8,128)(2,1)S(1)} %get-tuple-element.31), channel_id=1, source_target_pairs={{1,2},{3,4},{5,6},{7,8},{9,10},{11,12},{13,14},{2,1},{4,3},{6,5},{... | collective-permute-start | bytes 1966088 | tf_op jit(solution)/shard_map/ppermute | solution.py:254
  8.0 3.5 %collective-permute-start.3 = (bf16[256,512]{1,0:T(8,128)(2,1)S(1)}, bf16[256,512]{1,0:T(8,128)(2,1)S(1)}, u32[]{:S(2)}, u32[]{:S(2)}) collective-permute-start(bf16[256,512]{1,0:T(8,128)(2,1)S(1)} %get-tuple-element.33), channel_id=1, source_target_pairs={{1,2},{3,4},{5,6},{7,8},{9,10},{11,12},{13,14},{2,1},{4,3},{6,5},{... | collective-permute-start | bytes 786440 | tf_op jit(solution)/shard_map/ppermute | solution.py:254
  11.5 1.2 %copy-done.6 = bf16[1,1024,512]{2,1,0:T(8,128)(2,1)S(1)} copy-done((bf16[1,1024,512]{2,1,0:T(8,128)(2,1)S(1)}, bf16[1,1024,512]{2,1,0:T(8,128)(2,1)}, u32[]{:S(2)}) %copy-start.6) | copy-done | bytes 1048600
  12.8 2.1 %copy-done.7 = bf16[1,8,15,128,128]{4,3,2,1,0:T(8,128)(2,1)S(1)} copy-done((bf16[1,8,15,128,128]{4,3,2,1,0:T(8,128)(2,1)S(1)}, bf16[1,8,15,128,128]{4,3,2,1,0:T(8,128)(2,1)}, u32[]{:S(2)}) %copy-start.7) | copy-done | bytes 3932184
  15.6 7.9 %shard_map.76 = (bf16[4,16,256,128]{3,2,1,0:T(8,128)(2,1)S(1)}, f32[1024,512]{1,0:T(8,128)S(1)}) custom-call(s32[8,15]{1,0:T(8,128)S(1)} %bitcast.17, bf16[8,15,128,128]{3,2,1,0:T(8,128)(2,1)S(1)} %bitcast.16, bf16[1024,512]{1,0:T(8,128)(2,1)S(1)} %bitcast.15), custom_call_target="tpu_custom_call" | custom-call | flops 2147483648 | tf_op jit(solution)/shard_map/pallas_call | solution.py:238
  23.5 10.4 %collective-permute-done.1.second5_ref = bf16[640,512]{1,0:T(8,128)(2,1)S(1)} collective-permute-done((bf16[640,512]{1,0:T(8,128)(2,1)S(1)}, bf16[640,512]{1,0:T(8,128)(2,1)S(1)}, u32[]{:S(2)}, u32[]{:S(2)}) %collective-permute-start.1) | collective-permute-done | bytes 655392 | tf_op jit(solution)/shard_map/ppermute | solution.py:254
  33.9 1.3 %shard_map.79 = (bf16[512,512]{1,0:T(8,128)(2,1)S(1)}, bf16[256,512]{1,0:T(8,128)(2,1)S(1)}, bf16[256,512]{1,0:T(8,128)(2,1)S(1)}) custom-call(bf16[4,16,256,128]{3,2,1,0:T(8,128)(2,1)S(1)} %get-tuple-element.28.band_ref, f32[1024,512]{1,0:T(8,128)S(1)} %get-tuple-element.29.near_ref, bf16[640,512]{1,0:T(8,128)(2,1)S(1)} %collective-permute-done.first5_ref, ...), custom_call_target="tpu_custom_call" | custom-call | flops 536870912 | tf_op jit(solution)/shard_map/pallas_call | solution.py:238
  35.2 1.1 %collective-permute-start.4 = (bf16[256,512]{1,0:T(8,128)(2,1)S(1)}, bf16[256,512]{1,0:T(8,128)(2,1)S(1)}, u32[]{:S(2)}, u32[]{:S(2)}) collective-permute-start(bf16[256,512]{1,0:T(8,128)(2,1)S(1)} %get-tuple-element.35.third_ref), channel_id=1, source_target_pairs={{0,1},{2,3},{4,5},{6,7},{8,9},{10,11},{12,13},{14,15},{1,0},{3,2},... | collective-permute-start | bytes 786440 | tf_op jit(solution)/shard_map/ppermute | solution.py:254
  36.3 5.1 %collective-permute-start.5 = (bf16[256,512]{1,0:T(8,128)(2,1)S(1)}, bf16[256,512]{1,0:T(8,128)(2,1)S(1)}, u32[]{:S(2)}, u32[]{:S(2)}) collective-permute-start(bf16[256,512]{1,0:T(8,128)(2,1)S(1)} %get-tuple-element.35.third_ref), channel_id=1, source_target_pairs={{1,2},{3,4},{5,6},{7,8},{9,10},{11,12},{13,14},{2,1},{4,3},{6,5},{... | collective-permute-start | bytes 786440 | tf_op jit(solution)/shard_map/ppermute | solution.py:254
  41.4 3.7 %collective-permute-done.3.second2_ref = bf16[256,512]{1,0:T(8,128)(2,1)S(1)} collective-permute-done((bf16[256,512]{1,0:T(8,128)(2,1)S(1)}, bf16[256,512]{1,0:T(8,128)(2,1)S(1)}, u32[]{:S(2)}, u32[]{:S(2)}) %collective-permute-start.3) | collective-permute-done | bytes 262176 | tf_op jit(solution)/shard_map/ppermute | solution.py:254
  45.1 2.2 %shard_map.78 = (bf16[512,512]{1,0:T(8,128)(2,1)S(1)}, bf16[256,512]{1,0:T(8,128)(2,1)S(1)}, bf16[256,512]{1,0:T(8,128)(2,1)S(1)}, bf16[384,512]{1,0:T(8,128)(2,1)}, bf16[384,512]{1,0:T(8,128)(2,1)}) custom-call(bf16[4,16,256,128]{3,2,1,0:T(8,128)(2,1)S(1)} %get-tuple-element.28.band_ref, f32[1024,512]{1,0:T(8,128)S(1)} %get-tuple-element.29.near_ref, ...), custom_call_target="tpu_custom_call" | custom-call | flops 536870912 | tf_op jit(solution)/shard_map/pallas_call | solution.py:238
  47.8 1.3 %fusion = bf16[512,512]{1,0:T(8,128)(2,1)} fusion(f32[512,512]{1,0:T(8,128)S(1)} %fusion.4, bf16[512,512]{1,0:T(8,128)(2,1)S(1)} %get-tuple-element.38.mixed_mid_ref, bf16[256,512]{1,0:T(8,128)(2,1)S(1)} %get-tuple-element.36.fifth_ref, bf16[256,512]{1,0:T(8,128)(2,1)S(1)} %get-tuple-element.35.third_ref), kind=kOutput, calls=%fused_computation.1 | convolution fusion | flops 270008320 | bytes 2621440 | tf_op jit(solution)/shard_map/dot_general | solution.py:271
  49.0 6.5 %all-to-all-start = ((bf16[8,64,512]{2,1,0:T(8,128)(2,1)}), bf16[8,64,512]{2,1,0:T(8,128)(2,1)}, u32[]{:S(2)}, u32[]{:S(2)}) async-start(bf16[8,64,512]{2,1,0:T(8,128)(2,1)} %bitcast.18), calls=%async_computation | async-start | bytes 1048576 | tf_op jit(solution)/shard_map/all_to_all | solution.py:259
  55.6 2.6 %collective-permute-start.6 = (bf16[256,512]{1,0:T(8,128)(2,1)S(1)}, bf16[256,512]{1,0:T(8,128)(2,1)S(1)}, u32[]{:S(2)}, u32[]{:S(2)}) collective-permute-start(bf16[256,512]{1,0:T(8,128)(2,1)S(1)} %get-tuple-element.36.fifth_ref), channel_id=1, source_target_pairs={{0,1},{2,3},{4,5},{6,7},{8,9},{10,11},{12,13},{14,15},{1,0},{3,2},... | collective-permute-start | bytes 786440 | tf_op jit(solution)/shard_map/ppermute | solution.py:254
  58.1 4.4 %collective-permute-start.7 = (bf16[256,512]{1,0:T(8,128)(2,1)S(1)}, bf16[256,512]{1,0:T(8,128)(2,1)}, u32[]{:S(2)}, u32[]{:S(2)}) collective-permute-start(bf16[256,512]{1,0:T(8,128)(2,1)S(1)} %get-tuple-element.36.fifth_ref), channel_id=1, source_target_pairs={{1,2},{3,4},{5,6},{7,8},{9,10},{11,12},{13,14},{2,1},{4,3},{6,5},{... | collective-permute-start | bytes 786440 | tf_op jit(solution)/shard_map/ppermute | solution.py:254
  62.6 2.2 %copy-done.1 = bf16[4,16,256,128]{3,2,1,0:T(8,128)(2,1)S(1)} copy-done((bf16[4,16,256,128]{3,2,1,0:T(8,128)(2,1)S(1)}, bf16[4,16,256,128]{3,2,1,0:T(8,128)(2,1)}, u32[]{:S(2)}) %copy-start.1) | copy-done | bytes 4194328
  64.8 3.2 %shard_map.80 = (f32[1024,512]{1,0:T(8,128)S(1)}, bf16[1024,512]{1,0:T(8,128)(2,1)}) custom-call(bf16[4,16,256,128]{3,2,1,0:T(8,128)(2,1)S(1)} %copy-done.1, bf16[256,512]{1,0:T(8,128)(2,1)S(1)} %get-tuple-element.34.low_ref, bf16[256,512]{1,0:T(8,128)(2,1)S(1)} %get-tuple-element.35.third_ref, bf16[256,512]{1,0:T(8,128)(2,1)S(1)} %get-tuple-element.36.fifth_ref, ...), custom_call_target="tpu_custom_call" | custom-call | flops 2147483648 | tf_op jit(solution)/shard_map/pallas_call | solution.py:238
  68.0 1.3 %copy-done.11 = f32[1024,512]{1,0:T(8,128)} copy-done((f32[1024,512]{1,0:T(8,128)}, f32[1024,512]{1,0:T(8,128)S(1)}, u32[]{:S(2)}) %copy-start.11) | copy-done | bytes 2097176
  71.2 4.1 %all-to-all-start.1 = ((bf16[4,64,512]{2,1,0:T(8,128)(2,1)}), bf16[4,64,512]{2,1,0:T(8,128)(2,1)}, u32[]{:S(2)}, u32[]{:S(2)}) async-start(bf16[4,64,512]{2,1,0:T(8,128)(2,1)} %broadcast_in_dim.9), calls=%async_computation.1 | async-start | bytes 524288 | tf_op jit(solution)/shard_map/all_to_all | solution.py:259
  75.3 1.4 %collective-permute-start.8 = (bf16[384,512]{1,0:T(8,128)(2,1)}, bf16[384,512]{1,0:T(8,128)(2,1)S(1)}, u32[]{:S(2)}, u32[]{:S(2)}) collective-permute-start(bf16[384,512]{1,0:T(8,128)(2,1)} %get-tuple-element.49), channel_id=1, source_target_pairs={{0,1},{2,3},{4,5},{6,7},{8,9},{10,11},{12,13},{14,15},{1,0},{3,2},... | collective-permute-start | bytes 1179656 | tf_op jit(solution)/shard_map/ppermute | solution.py:254
  76.7 4.9 %collective-permute-start.9 = (bf16[384,512]{1,0:T(8,128)(2,1)}, bf16[384,512]{1,0:T(8,128)(2,1)S(1)}, u32[]{:S(2)}, u32[]{:S(2)}) collective-permute-start(bf16[384,512]{1,0:T(8,128)(2,1)} %get-tuple-element.50), channel_id=1, source_target_pairs={{1,2},{3,4},{5,6},{7,8},{9,10},{11,12},{13,14},{2,1},{4,3},{6,5},{... | collective-permute-start | bytes 1179656 | tf_op jit(solution)/shard_map/ppermute | solution.py:254
  82.3 2.2 %copy-done.2 = bf16[4,16,256,128]{3,2,1,0:T(8,128)(2,1)S(1)} copy-done((bf16[4,16,256,128]{3,2,1,0:T(8,128)(2,1)S(1)}, bf16[4,16,256,128]{3,2,1,0:T(8,128)(2,1)}, u32[]{:S(2)}) %copy-start.2) | copy-done | bytes 4194328
  85.4 1.6 %copy-done.12 = f32[1024,512]{1,0:T(8,128)S(1)} copy-done((f32[1024,512]{1,0:T(8,128)S(1)}, f32[1024,512]{1,0:T(8,128)}, u32[]{:S(2)}) %copy-start.12) | copy-done | bytes 2097176
  87.0 1.4 %shard_map.81.near_ref = f32[1024,512]{1,0:T(8,128)S(1)} custom-call(bf16[4,16,256,128]{3,2,1,0:T(8,128)(2,1)S(1)} %copy-done.2, f32[1024,512]{1,0:T(8,128)S(1)} %copy-done.12, bf16[256,512]{1,0:T(8,128)(2,1)S(1)} %copy-done.9, bf16[256,512]{1,0:T(8,128)(2,1)} %collective-permute-done.7.second_ref), custom_call_target="tpu_custom_call" | custom-call | flops 6442450944 | tf_op jit(solution)/shard_map/pallas_call | solution.py:238
  90.3 5.6 %all-to-all-start.2 = ((bf16[8,64,512]{2,1,0:T(8,128)(2,1)}), bf16[8,64,512]{2,1,0:T(8,128)(2,1)}, u32[]{:S(2)}, u32[]{:S(2)}) async-start(bf16[8,64,512]{2,1,0:T(8,128)(2,1)} %broadcast_in_dim.20), calls=%async_computation.2 | async-start | bytes 1048576 | tf_op jit(solution)/shard_map/all_to_all | solution.py:259
  95.9 4.7 %collective-permute-done.9.second3_ref = bf16[384,512]{1,0:T(8,128)(2,1)S(1)} collective-permute-done((bf16[384,512]{1,0:T(8,128)(2,1)}, bf16[384,512]{1,0:T(8,128)(2,1)S(1)}, u32[]{:S(2)}, u32[]{:S(2)}) %collective-permute-start.9) | collective-permute-done | bytes 393248 | tf_op jit(solution)/shard_map/ppermute | solution.py:254
  100.6 2.2 %copy-done.3 = bf16[4,16,256,128]{3,2,1,0:T(8,128)(2,1)S(1)} copy-done((bf16[4,16,256,128]{3,2,1,0:T(8,128)(2,1)S(1)}, bf16[4,16,256,128]{3,2,1,0:T(8,128)(2,1)}, u32[]{:S(2)}) %copy-start.3) | copy-done | bytes 4194328
  102.7 2.3 %shard_map.82 = bf16[1024,512]{1,0:T(8,128)(2,1)} custom-call(bf16[4,16,256,128]{3,2,1,0:T(8,128)(2,1)S(1)} %copy-done.3, f32[1024,512]{1,0:T(8,128)S(1)} %shard_map.81.near_ref, bf16[384,512]{1,0:T(8,128)(2,1)S(1)} %collective-permute-done.8.first3_ref, bf16[384,512]{1,0:T(8,128)(2,1)S(1)} %collective-permute-done.9.second3_ref, bf16[512,512]{1,0:T(8,128)(2,1)S(1)} %copy-done.4), custom_call_target="tpu_custom_call" | custom-call | flops 2147483648 | tf_op jit(solution)/shard_map/pallas_call | solution.py:238
  105.1 2.6 %all-to-all-done.2 = bf16[8,64,512]{2,1,0:T(8,128)(2,1)} async-done(((bf16[8,64,512]{2,1,0:T(8,128)(2,1)}), bf16[8,64,512]{2,1,0:T(8,128)(2,1)}, u32[]{:S(2)}, u32[]{:S(2)}) %all-to-all-start.2) | async-done | bytes 524320 | tf_op jit(solution)/shard_map/all_to_all | solution.py:259
  107.7 2.1 %bitcast_convert_fusion = f32[512,512]{1,0:T(8,128)} fusion(bf16[8,64,512]{2,1,0:T(8,128)(2,1)} %all-to-all-done.2), kind=kLoop, calls=%fused_computation.10 | loop fusion | flops 262144 | bytes 1572864 | tf_op jit(solution)/shard_map/convert_element_type | solution.py:335
  (34 shorter events, 7.0 us)
Async XLA Ops:
  2.1 21.4 %collective-permute-start = (bf16[640,512]{1,0:T(8,128)(2,1)S(1)}, bf16[640,512]{1,0:T(8,128)(2,1)S(1)}, u32[]{:S(2)}, u32[]{:S(2)}) collective-permute-start(bf16[640,512]{1,0:T(8,128)(2,1)S(1)} %get-tuple-element.30), channel_id=1, source_target_pairs={{0,1},{2,3},{4,5},{6,7},{8,9},{10,11},{12,13},{14,15},{1,0},{3,2},... | collective-permute-start | bytes 1966088 | tf_op jit(solution)/shard_map/ppermute | solution.py:254
  3.5 30.4 %collective-permute-start.1 = (bf16[640,512]{1,0:T(8,128)(2,1)S(1)}, bf16[640,512]{1,0:T(8,128)(2,1)S(1)}, u32[]{:S(2)}, u32[]{:S(2)}) collective-permute-start(bf16[640,512]{1,0:T(8,128)(2,1)S(1)} %get-tuple-element.31), channel_id=1, source_target_pairs={{1,2},{3,4},{5,6},{7,8},{9,10},{11,12},{13,14},{2,1},{4,3},{6,5},{... | collective-permute-start | bytes 1966088 | tf_op jit(solution)/shard_map/ppermute | solution.py:254
  7.5 33.9 %collective-permute-start.2 = (bf16[256,512]{1,0:T(8,128)(2,1)S(1)}, bf16[256,512]{1,0:T(8,128)(2,1)S(1)}, u32[]{:S(2)}, u32[]{:S(2)}) collective-permute-start(bf16[256,512]{1,0:T(8,128)(2,1)S(1)} %get-tuple-element.32), channel_id=1, source_target_pairs={{0,1},{2,3},{4,5},{6,7},{8,9},{10,11},{12,13},{14,15},{1,0},{3,2},... | collective-permute-start | bytes 786440 | tf_op jit(solution)/shard_map/ppermute | solution.py:254
  8.0 37.1 %collective-permute-start.3 = (bf16[256,512]{1,0:T(8,128)(2,1)S(1)}, bf16[256,512]{1,0:T(8,128)(2,1)S(1)}, u32[]{:S(2)}, u32[]{:S(2)}) collective-permute-start(bf16[256,512]{1,0:T(8,128)(2,1)S(1)} %get-tuple-element.33), channel_id=1, source_target_pairs={{1,2},{3,4},{5,6},{7,8},{9,10},{11,12},{13,14},{2,1},{4,3},{6,5},{... | collective-permute-start | bytes 786440 | tf_op jit(solution)/shard_map/ppermute | solution.py:254
  11.5 1.2 %copy-start.6 = (bf16[1,1024,512]{2,1,0:T(8,128)(2,1)S(1)}, bf16[1,1024,512]{2,1,0:T(8,128)(2,1)}, u32[]{:S(2)}) copy-start(bf16[1,1024,512]{2,1,0:T(8,128)(2,1)} %param.5) | copy-start | bytes 3145732
  12.8 2.1 %copy-start.7 = (bf16[1,8,15,128,128]{4,3,2,1,0:T(8,128)(2,1)S(1)}, bf16[1,8,15,128,128]{4,3,2,1,0:T(8,128)(2,1)}, u32[]{:S(2)}) copy-start(bf16[1,8,15,128,128]{4,3,2,1,0:T(8,128)(2,1)} %param.8) | copy-start | bytes 11796484
  14.9 0.7 copy-start.10
  15.6 18.3 %copy-start.4 = (bf16[512,512]{1,0:T(8,128)(2,1)S(1)}, bf16[512,512]{1,0:T(8,128)(2,1)}, u32[]{:S(2)}) copy-start(bf16[512,512]{1,0:T(8,128)(2,1)} %weight_ref.7) | copy-start | bytes 1572868
  15.6 18.3 %copy-start.5 = (bf16[1,1024,512]{2,1,0:T(8,128)(2,1)S(1)}, bf16[1,1024,512]{2,1,0:T(8,128)(2,1)}, u32[]{:S(2)}) copy-start(bf16[1,1024,512]{2,1,0:T(8,128)(2,1)} %param.9) | copy-start | bytes 3145732
  23.5 21.7 %copy-start = (bf16[4,16,256,128]{3,2,1,0:T(8,128)(2,1)}, bf16[4,16,256,128]{3,2,1,0:T(8,128)(2,1)S(1)}, u32[]{:S(2)}) copy-start(bf16[4,16,256,128]{3,2,1,0:T(8,128)(2,1)S(1)} %get-tuple-element.28.band_ref) | copy-start | bytes 12582916
  35.2 27.4 %collective-permute-start.4 = (bf16[256,512]{1,0:T(8,128)(2,1)S(1)}, bf16[256,512]{1,0:T(8,128)(2,1)S(1)}, u32[]{:S(2)}, u32[]{:S(2)}) collective-permute-start(bf16[256,512]{1,0:T(8,128)(2,1)S(1)} %get-tuple-element.35.third_ref), channel_id=1, source_target_pairs={{0,1},{2,3},{4,5},{6,7},{8,9},{10,11},{12,13},{14,15},{1,0},{3,2},... | collective-permute-start | bytes 786440 | tf_op jit(solution)/shard_map/ppermute | solution.py:254
  36.3 26.3 %collective-permute-start.5 = (bf16[256,512]{1,0:T(8,128)(2,1)S(1)}, bf16[256,512]{1,0:T(8,128)(2,1)S(1)}, u32[]{:S(2)}, u32[]{:S(2)}) collective-permute-start(bf16[256,512]{1,0:T(8,128)(2,1)S(1)} %get-tuple-element.35.third_ref), channel_id=1, source_target_pairs={{1,2},{3,4},{5,6},{7,8},{9,10},{11,12},{13,14},{2,1},{4,3},{6,5},{... | collective-permute-start | bytes 786440 | tf_op jit(solution)/shard_map/ppermute | solution.py:254
  49.0 20.3 %all-to-all-start = ((bf16[8,64,512]{2,1,0:T(8,128)(2,1)}), bf16[8,64,512]{2,1,0:T(8,128)(2,1)}, u32[]{:S(2)}, u32[]{:S(2)}) async-start(bf16[8,64,512]{2,1,0:T(8,128)(2,1)} %bitcast.18), calls=%async_computation | async-start | bytes 1048576 | tf_op jit(solution)/shard_map/all_to_all | solution.py:259
  55.6 26.0 %collective-permute-start.6 = (bf16[256,512]{1,0:T(8,128)(2,1)S(1)}, bf16[256,512]{1,0:T(8,128)(2,1)S(1)}, u32[]{:S(2)}, u32[]{:S(2)}) collective-permute-start(bf16[256,512]{1,0:T(8,128)(2,1)S(1)} %get-tuple-element.36.fifth_ref), channel_id=1, source_target_pairs={{0,1},{2,3},{4,5},{6,7},{8,9},{10,11},{12,13},{14,15},{1,0},{3,2},... | collective-permute-start | bytes 786440 | tf_op jit(solution)/shard_map/ppermute | solution.py:254
  58.1 24.1 %collective-permute-start.7 = (bf16[256,512]{1,0:T(8,128)(2,1)S(1)}, bf16[256,512]{1,0:T(8,128)(2,1)}, u32[]{:S(2)}, u32[]{:S(2)}) collective-permute-start(bf16[256,512]{1,0:T(8,128)(2,1)S(1)} %get-tuple-element.36.fifth_ref), channel_id=1, source_target_pairs={{1,2},{3,4},{5,6},{7,8},{9,10},{11,12},{13,14},{2,1},{4,3},{6,5},{... | collective-permute-start | bytes 786440 | tf_op jit(solution)/shard_map/ppermute | solution.py:254
  62.6 2.2 %copy-start.1 = (bf16[4,16,256,128]{3,2,1,0:T(8,128)(2,1)S(1)}, bf16[4,16,256,128]{3,2,1,0:T(8,128)(2,1)}, u32[]{:S(2)}) copy-start(bf16[4,16,256,128]{3,2,1,0:T(8,128)(2,1)} %copy-done) | copy-start | bytes 12582916
  68.0 1.4 %copy-start.11 = (f32[1024,512]{1,0:T(8,128)}, f32[1024,512]{1,0:T(8,128)S(1)}, u32[]{:S(2)}) copy-start(f32[1024,512]{1,0:T(8,128)S(1)} %get-tuple-element.46.near_ref) | copy-start | bytes 6291460
  71.2 17.2 %all-to-all-start.1 = ((bf16[4,64,512]{2,1,0:T(8,128)(2,1)}), bf16[4,64,512]{2,1,0:T(8,128)(2,1)}, u32[]{:S(2)}, u32[]{:S(2)}) async-start(bf16[4,64,512]{2,1,0:T(8,128)(2,1)} %broadcast_in_dim.9), calls=%async_computation.1 | async-start | bytes 524288 | tf_op jit(solution)/shard_map/all_to_all | solution.py:259
  75.3 20.6 %collective-permute-start.8 = (bf16[384,512]{1,0:T(8,128)(2,1)}, bf16[384,512]{1,0:T(8,128)(2,1)S(1)}, u32[]{:S(2)}, u32[]{:S(2)}) collective-permute-start(bf16[384,512]{1,0:T(8,128)(2,1)} %get-tuple-element.49), channel_id=1, source_target_pairs={{0,1},{2,3},{4,5},{6,7},{8,9},{10,11},{12,13},{14,15},{1,0},{3,2},... | collective-permute-start | bytes 1179656 | tf_op jit(solution)/shard_map/ppermute | solution.py:254
  76.7 23.9 %collective-permute-start.9 = (bf16[384,512]{1,0:T(8,128)(2,1)}, bf16[384,512]{1,0:T(8,128)(2,1)S(1)}, u32[]{:S(2)}, u32[]{:S(2)}) collective-permute-start(bf16[384,512]{1,0:T(8,128)(2,1)} %get-tuple-element.50), channel_id=1, source_target_pairs={{1,2},{3,4},{5,6},{7,8},{9,10},{11,12},{13,14},{2,1},{4,3},{6,5},{... | collective-permute-start | bytes 1179656 | tf_op jit(solution)/shard_map/ppermute | solution.py:254
  81.6 0.7 copy-start.8
  82.3 2.2 %copy-start.2 = (bf16[4,16,256,128]{3,2,1,0:T(8,128)(2,1)S(1)}, bf16[4,16,256,128]{3,2,1,0:T(8,128)(2,1)}, u32[]{:S(2)}) copy-start(bf16[4,16,256,128]{3,2,1,0:T(8,128)(2,1)} %copy-done) | copy-start | bytes 12582916
  84.5 0.9 copy-start.9
  85.4 1.6 %copy-start.12 = (f32[1024,512]{1,0:T(8,128)S(1)}, f32[1024,512]{1,0:T(8,128)}, u32[]{:S(2)}) copy-start(f32[1024,512]{1,0:T(8,128)} %copy-done.11) | copy-start | bytes 6291460
  90.3 17.5 %all-to-all-start.2 = ((bf16[8,64,512]{2,1,0:T(8,128)(2,1)}), bf16[8,64,512]{2,1,0:T(8,128)(2,1)}, u32[]{:S(2)}, u32[]{:S(2)}) async-start(bf16[8,64,512]{2,1,0:T(8,128)(2,1)} %broadcast_in_dim.20), calls=%async_computation.2 | async-start | bytes 1048576 | tf_op jit(solution)/shard_map/all_to_all | solution.py:259
  100.6 2.2 %copy-start.3 = (bf16[4,16,256,128]{3,2,1,0:T(8,128)(2,1)S(1)}, bf16[4,16,256,128]{3,2,1,0:T(8,128)(2,1)}, u32[]{:S(2)}) copy-start(bf16[4,16,256,128]{3,2,1,0:T(8,128)(2,1)} %copy-done) | copy-start | bytes 12582916

commit v3 on v2

--- a/solution.py
+++ b/solution.py
@@ -1,3 +1,5 @@
+import functools
+
 import jax
 import jax.numpy as jnp
 from jax import lax
@@ -10,6 +12,7 @@
 LINE = ("blk", "rep")
 LEVEL = ("dp", "blk")
 VMEM_BYTES = 14 << 20
+LONG = 12
 BF16, F32 = jnp.bfloat16, jnp.float32
 
 
@@ -131,23 +134,23 @@
     return mixed, dagg.astype(BF16)
 
 
-def inner_kernel(band_ref, near_ref, first5_ref, second5_ref, weight_ref, cot_ref,
-                 mixed_ref, third_ref, fifth_ref):
+def inner_kernel(band_ref, near_ref, first5_ref, second5_ref, weight_ref, cot_ref, mixed_ref, mid_ref):
     height = band_ref.shape[2]
     five = (first5_ref, second5_ref)
 
     def body(left, right):
         sources = [(before(range(3, 8)), five[left]), (after(range(5)), five[right])]
-        for i, (t, out) in enumerate(((1, third_ref), (2, fifth_ref))):
+        for i, t in enumerate((1, 2)):
             mixed, dagg = tile_step(band_ref, near_ref, sources, t, weight_ref, cot_ref)
-            mixed_ref[pl.ds(i * height, height), :] = mixed
-            out[...] = dagg
+            at = pl.ds(i * height, height)
+            mixed_ref[at, :] = mixed
+            mid_ref[at, :] = dagg
 
     by_parity(body)
 
 
-def outer_kernel(band_ref, near_ref, first5_ref, second5_ref, first2_ref, second2_ref, weight_ref, cot_ref,
-                 mixed_ref, low_ref, high_ref, first3_ref, second3_ref):
+def outer_kernel(band_ref, near_ref, first5_ref, second5_ref, first2_ref, second2_ref, weight_ref, cot_ref, mid_ref,
+                 mixed_ref, end_ref, first3_ref, second3_ref, all7_ref):
     size = band_ref.shape[3]
     height = PAIR * size
     five, two = (first5_ref, second5_ref), (first2_ref, second2_ref)
@@ -162,50 +165,51 @@
         ]
         mixed, dagg = tile_step(band_ref, near_ref, sources, 0, weight_ref, cot_ref)
         mixed_ref[:height, :] = mixed
-        low_ref[...] = dagg
+        end_ref[:height, :] = dagg
         for out in three:
             out[:size, :] = dagg[size:]
         three[left][2 * size :, :] = dagg[:size]
         mixed, dagg = tile_step(band_ref, near_ref, sources, 3, weight_ref, cot_ref)
         mixed_ref[height:, :] = mixed
-        high_ref[...] = dagg
+        end_ref[height:, :] = dagg
         for out in three:
             out[size : 2 * size, :] = dagg[:size]
         three[right][2 * size :, :] = dagg[size:]
+        all7_ref[: 4 * size, :] = mid_ref[...]
+        all7_ref[4 * size :, :] = second3_ref[...]
 
     by_parity(body)
 
 
-def gather_kernel(band_ref, low_ref, third_ref, fifth_ref, high_ref, first_ref, second_ref,
-                  mixed_mid_ref, mixed_end_ref, weight_ref, near_ref, activ_ref):
+def own_kernel(band_ref, mid_ref, end_ref, near_ref):
     tiles, _, height, _ = band_ref.shape
-    came = (first_ref, second_ref)
-
-    def body(left, right):
-        sources = [
-            (before((2, 3)), came[left]),
-            (mine((0, 1)), low_ref),
-            (mine((2, 3)), third_ref),
-            (mine((4, 5)), fifth_ref),
-            (mine((6, 7)), high_ref),
-            (after((2, 3)), came[right]),
-        ]
-        for t in range(tiles):
-            near_ref[pl.ds(t * height, height), :] = banded(band_ref, t, sources)
-
-    by_parity(body)
+    sources = [
+        (mine((0, 1)), end_ref.at[:height]),
+        (mine((2, 3, 4, 5)), mid_ref),
+        (mine((6, 7)), end_ref.at[height:]),
+    ]
+    for t in range(tiles):
+        near_ref[pl.ds(t * height, height), :] = banded(band_ref, t, sources)
+
+
+def mark_kernel(near_ref, out_ref):
+    out_ref[...] = near_ref[: out_ref.shape[0], : out_ref.shape[1]]
+
+
+def activ_kernel(mixed_mid_ref, mixed_end_ref, weight_ref, _, activ_ref):
+    height = mixed_mid_ref.shape[0] // 2
     halves = (mixed_end_ref[:height, :], mixed_mid_ref[:height, :], mixed_mid_ref[height:, :], mixed_end_ref[height:, :])
     for t, mixed in enumerate(halves):
         agg = jnp.dot(mixed, weight_ref[...], preferred_element_type=F32)
         activ_ref[pl.ds(t * height, height), :] = (agg * jax.nn.sigmoid(agg)).astype(activ_ref.dtype)
 
 
-def add_kernel(band_ref, near_ref, first_ref, second_ref, out_ref):
+def add_kernel(left_rows, right_rows, band_ref, near_ref, first_ref, second_ref, out_ref):
     tiles, _, height, _ = band_ref.shape
     came = (first_ref, second_ref)
 
     def body(left, right):
-        sources = [(before((4, 5)), came[left]), (after((4, 5)), came[right])]
+        sources = [(before(left_rows), came[left]), (after(right_rows), came[right])]
         for t in range(tiles):
             at = pl.ds(t * height, height)
             out_ref[at, :] = near_ref[at, :] + banded(band_ref, t, sources)
@@ -213,12 +217,14 @@
     by_parity(body)
 
 
-def back_kernel(band_ref, near_ref, first3_ref, second3_ref, weight_ref, out_ref, held_ref, sems):
+def back_kernel(band_ref, near_ref, all7_ref, weight_ref, out_ref, held_ref, sems):
     tiles, _, height, _ = band_ref.shape
-    came = (first3_ref, second3_ref)
 
     def body(left, right):
-        sources = [(before((1, 6, 7)), came[left]), (after((1, 6, 0)), came[right])]
+        if left:
+            sources = [(before((2, 3, 4, 5, 1, 6, 7)), all7_ref)]
+        else:
+            sources = [(after((2, 3, 4, 5, 1, 6, 0)), all7_ref)]
         copies = []
         for t in range(tiles):
             at = pl.ds(t * height, height)
@@ -246,25 +252,65 @@
     )(*ins)
 
 
-def swapped(first, second):
-    count = lax.axis_size(LINE)
-    result = []
-    for x, start in ((first, 0), (second, 1)):
-        pairs = [(i, i + 1) for i in range(start, count - 1, 2)]
-        result.append(lax.ppermute(x, LINE, pairs + [(j, i) for i, j in pairs]))
-    return result
-
-
-def traded(x, axes):
-    return lax.all_to_all(x.astype(BF16), axes, 0, 0, tiled=True)
-
-
-def shared(x, axes):
-    return traded(jnp.broadcast_to(x[None], (lax.axis_size(axes), *x.shape)), axes)
-
-
-def total(parts):
-    return jnp.sum(parts.astype(F32), axis=0)
+def swap_pairs(start, across):
+    count, run = lax.axis_size(LINE), lax.axis_size(LINE[1])
+    pairs = [(i, i + 1) for i in range(start, count - 1, 2)]
+    pairs = [(i, j) for i, j in pairs if across is None or (j % run == 0) == across]
+    return pairs + [(j, i) for i, j in pairs]
+
+
+def swapped(first, second, across=None):
+    return [lax.ppermute(x, LINE, swap_pairs(start, across)) for x, start in ((first, 0), (second, 1))]
+
+
+def partner(j, d, n):
+    return j ^ d if n & (n - 1) == 0 else (j + d) % n
+
+
+def from_all(parts, axis):
+    n = lax.axis_size(axis)
+    return [
+        lax.ppermute(parts(d), axis, [(j, partner(j, d, n)) for j in range(n)]) for d in range(1, n)
+    ]
+
+
+def scatter(x, axis, dtype):
+    n = lax.axis_size(axis)
+    me = lax.axis_index(axis)
+    step = x.shape[0] // n
+
+    def part(d):
+        return lax.dynamic_slice_in_dim(x, partner(me, d, n) * step, step)
+
+    return part(0) if n & (n - 1) == 0 else lax.dynamic_slice_in_dim(x, me * step, step), from_all(
+        lambda d: part(d).astype(dtype), axis
+    )
+
+
+def add_all(kept, came):
+    for part in came:
+        kept = kept + part.astype(F32)
+    return kept
+
+
+def pairwise(parts):
+    parts = [part.astype(F32) for part in parts]
+    while len(parts) > 1:
+        parts = [parts[i] + parts[i + 1] for i in range(0, len(parts), 2)]
+    return parts[0]
+
+
+def join_kernel(*refs):
+    *parts, out_ref = refs
+    n = lax.axis_size(LEVEL[1])
+    me = lax.axis_index(LEVEL[1])
+    halves = lax.axis_size(LEVEL[0])
+    step = parts[0].shape[0] // halves
+    for d, part in enumerate(parts):
+        origin = me ^ d if n & (n - 1) == 0 else lax.rem(me - d + n, n)
+        for h in range(halves):
+            first = pl.multiple_of(h * n * step + origin * step, step)
+            out_ref[pl.ds(first, step), :] = part[h * step : (h + 1) * step, :].astype(out_ref.dtype)
 
 
 def term_of(mixed, dagg):
@@ -303,36 +349,52 @@
         scratch_shapes=[pltpu.SemaphoreType.DMA((rows, slots))],
     )
     band, near = held(band, near)
-    mixed_mid, third, fifth = kernel_call(
-        inner_kernel, [band, near, *five, weight, cotangent[0]], [chip(4), chip(2), chip(2)], product
-    )
-    came_third = swapped(third, third)
-    came_fifth = swapped(fifth, fifth)
-    mixed_end, low, high, *three = kernel_call(
-        outer_kernel, [band, near, *five, *two, weight, cotangent[0]],
-        [chip(4), chip(2), chip(2), chip(3), chip(3)], product,
-    )
-    near, activ = kernel_call(
-        gather_kernel, [band, low, third, fifth, high, *came_third, mixed_mid, mixed_end, weight],
-        [chip(rows, F32), plain(rows)], 4 * product,
-    )
-    term = term_of(mixed_mid, jnp.concatenate([third, fifth])) + term_of(mixed_end, jnp.concatenate([low, high]))
-    term = traded(term.reshape(lax.axis_size(LEVEL), -1, width), LEVEL)
-    term, near = lax.optimization_barrier((term, near))
-    term = total(term)
-    term, *three = lax.optimization_barrier((term, *three))
-    term = shared(term, ("rep",))
-    three = swapped(*three)
-    near = kernel_call(add_kernel, [band, near, *came_fifth], [chip(rows, F32)], 12 * product)[0]
-    term, near = lax.optimization_barrier((term, near))
-    term = shared(total(term), LEVEL)
+    mixed_mid, mid = kernel_call(
+        inner_kernel, [band, near, *five, weight, cotangent[0]], [chip(4), chip(4)], product
+    )
+    four = swapped(mid, mid, across=False)
+    mixed_end, end, *three, all7 = kernel_call(
+        outer_kernel, [band, near, *five, *two, weight, cotangent[0], mid],
+        [chip(4), chip(4), chip(3), chip(3), chip(7)], product,
+    )
+    three = swapped(*three, across=False)
+    full = [chip(rows, F32)]
+    term = term_of(mixed_mid, mid) + term_of(mixed_end, end)
+    kept, came = scatter(term, LEVEL[0], F32)
+    near = kernel_call(own_kernel, [band, mid, end], full, LONG * product)[0]
+    came, near = lax.optimization_barrier((came, near))
+    kept, came = scatter(add_all(kept, came), LEVEL[1], BF16)
+    near = kernel_call(
+        functools.partial(add_kernel, (2, 3, 4, 5), (2, 3, 4, 5)), [band, *held(near), *four], full, LONG * product
+    )[0]
+    came, near = lax.optimization_barrier((came, near))
+    term = add_all(kept, came).astype(BF16)
+    parts = [term, *from_all(lambda d: term, "rep")]
+    mark = kernel_call(mark_kernel, held(near), [pltpu.VMEM((8, 128), F32)], LONG * product)[0]
+    *parts, all7, mark = lax.optimization_barrier((*parts, all7, mark))
+    all7 = lax.ppermute(all7, LINE, swap_pairs(1, True))
+    term = pairwise(parts).astype(BF16)
+    other, = from_all(lambda d: term, LEVEL[0])
+    activ = kernel_call(
+        activ_kernel, [mixed_mid, mixed_end, weight, *held(mark)], [plain(rows)], LONG * product
+    )[0]
+    other, activ = lax.optimization_barrier((other, activ))
+    term = jnp.where(lax.axis_index(LEVEL[0]) == 0, jnp.stack([term, other]), jnp.stack([other, term]))
+    term = term.reshape(-1, width)
+    parts = [term, *from_all(lambda d: term, LEVEL[1])]
+    near = kernel_call(
+        functools.partial(add_kernel, (1, 6, 7), (1, 6, 0)), [band, *held(near), *three], full, LONG * product
+    )[0]
+    parts, near = lax.optimization_barrier((parts, near))
     feat_grad = kernel_call(
-        back_kernel, [band, near, *three, weight], [plain(rows)], 4 * product,
+        back_kernel, [band, *held(near), all7, weight], [plain(rows)], LONG * product,
         out_specs=[anywhere()],
         scratch_shapes=[pltpu.VMEM((zones, width), BF16), pltpu.SemaphoreType.DMA((tiles,))],
     )[0]
-    term, feat_grad = lax.optimization_barrier((term, feat_grad))
-    weight_grad = term.reshape(-1, width).astype(F32)
+    parts, feat_grad = lax.optimization_barrier((parts, feat_grad))
+    weight_grad = kernel_call(
+        join_kernel, parts, [jax.ShapeDtypeStruct((width, width), F32)], 0
+    )[0]
     return activ[None], feat_grad[None], weight_grad
 
 

time: 111 us -> 113 us (1.018)
  the two profiles are of different devices: /device:TPU:7 before, /device:TPU:0 now
where the time goes in v3:
time: 113 us
  starting transfers between devices  57 us (50%)
  waiting for transfers between devices  29.6 us (26%)
  Pallas kernels  20.2 us (18%)
  local copies, waits for them, and re-layouts  4.11 us (4%)
    ppermute x8, starting transfers between devices, swapped(): lax.ppermute(x, LINE, swap_pairs(start, across))  36.9 us
    ppermute x11, waiting for transfers between devices, from_all(): lax.ppermute(parts(d), axis, [(j, partner(j, d, n)) for j in range(n)])  29.4 us
    pallas_call x11, Pallas kernels, kernel_call(): pl.pallas_call(body, out_shape=outs, in_specs=specs or [whole()] * len(in...  20.2 us
    ppermute x11, starting transfers between devices, from_all(): lax.ppermute(parts(d), axis, [(j, partner(j, d, n)) for j in range(n)])  19.4 us
    unnamed x10, local copies, waits for them, and re-layouts  4.03 us
  transfers between devices with their start and end apart: 20, of which 7 were waited for; matrix products, arithmetic and copies ran while one was open for 1% of the time, Pallas kernels for 13%

profile of v3, /device:TPU:0, one launch (start us, length us, event | category | flops | bytes accessed | tf_op | source)
XLA Modules:
  0.0 113.0 jit_solution(2409903515925837362)
XLA Ops:
  0.6 2.2 %shard_map.77 = (bf16[640,512]{1,0:T(8,128)(2,1)S(1)}, bf16[640,512]{1,0:T(8,128)(2,1)S(1)}, bf16[256,512]{1,0:T(8,128)(2,1)}, bf16[256,512]{1,0:T(8,128)(2,1)S(1)}) custom-call(bf16[1024,512]{1,0:T(8,128)(2,1)} %bitcast.15), custom_call_target="tpu_custom_call" | custom-call | tf_op jit(solution)/shard_map/pallas_call | solution.py:244
  2.8 3.1 %collective-permute-start = (bf16[640,512]{1,0:T(8,128)(2,1)S(1)}, bf16[640,512]{1,0:T(8,128)(2,1)S(1)}, u32[]{:S(2)}, u32[]{:S(2)}) collective-permute-start(bf16[640,512]{1,0:T(8,128)(2,1)S(1)} %get-tuple-element.42), channel_id=1, source_target_pairs={{0,1},{2,3},{4,5},{6,7},{8,9},{10,11},{12,13},{14,15},{1,0},{3,2},... | collective-permute-start | bytes 1966088 | tf_op jit(solution)/shard_map/ppermute | solution.py:263
  5.9 0.7 collective-permute-start.1
  6.6 4.4 %collective-permute-start.2 = (bf16[256,512]{1,0:T(8,128)(2,1)}, bf16[256,512]{1,0:T(8,128)(2,1)S(1)}, u32[]{:S(2)}, u32[]{:S(2)}) collective-permute-start(bf16[256,512]{1,0:T(8,128)(2,1)} %get-tuple-element.46), channel_id=1, source_target_pairs={{0,1},{2,3},{4,5},{6,7},{8,9},{10,11},{12,13},{14,15},{1,0},{3,2},... | collective-permute-start | bytes 786440 | tf_op jit(solution)/shard_map/ppermute | solution.py:263
  11.7 1.2 %copy-done.2 = bf16[1,1024,512]{2,1,0:T(8,128)(2,1)S(1)} copy-done((bf16[1,1024,512]{2,1,0:T(8,128)(2,1)S(1)}, bf16[1,1024,512]{2,1,0:T(8,128)(2,1)}, u32[]{:S(2)}) %copy-start.2) | copy-done | bytes 1048600
  13.0 2.1 %copy-done.3 = bf16[1,8,15,128,128]{4,3,2,1,0:T(8,128)(2,1)S(1)} copy-done((bf16[1,8,15,128,128]{4,3,2,1,0:T(8,128)(2,1)S(1)}, bf16[1,8,15,128,128]{4,3,2,1,0:T(8,128)(2,1)}, u32[]{:S(2)}) %copy-start.3) | copy-done | bytes 3932184
  15.8 7.4 %shard_map.76 = (bf16[4,16,256,128]{3,2,1,0:T(8,128)(2,1)S(1)}, f32[1024,512]{1,0:T(8,128)S(1)}) custom-call(s32[8,15]{1,0:T(8,128)S(1)} %bitcast.22, bf16[8,15,128,128]{3,2,1,0:T(8,128)(2,1)S(1)} %bitcast.21, bf16[1024,512]{1,0:T(8,128)(2,1)S(1)} %bitcast.16), custom_call_target="tpu_custom_call" | custom-call | flops 2147483648 | tf_op jit(solution)/shard_map/pallas_call | solution.py:244
  23.2 1.3 %shard_map.78 = (bf16[512,512]{1,0:T(8,128)(2,1)S(1)}, bf16[512,512]{1,0:T(8,128)(2,1)S(1)}) custom-call(bf16[4,16,256,128]{3,2,1,0:T(8,128)(2,1)S(1)} %get-tuple-element.40.band_ref, f32[1024,512]{1,0:T(8,128)S(1)} %get-tuple-element.41.near_ref, bf16[640,512]{1,0:T(8,128)(2,1)S(1)} %collective-permute-done.first5_ref, ...), custom_call_target="tpu_custom_call" | custom-call | flops 536870912 | tf_op jit(solution)/shard_map/pallas_call | solution.py:244
  24.5 0.7 collective-permute-start.9
  25.2 18.6 %collective-permute-start.8 = (bf16[512,512]{1,0:T(8,128)(2,1)S(1)}, bf16[512,512]{1,0:T(8,128)(2,1)S(1)}, u32[]{:S(2)}, u32[]{:S(2)}) collective-permute-start(bf16[512,512]{1,0:T(8,128)(2,1)S(1)} %get-tuple-element.45.mid_ref), channel_id=1, source_target_pairs={{0,1},{2,3},{4,5},{6,7},{8,9},{10,11},{12,13},{14,15},{1,0},{3,2},... | collective-permute-start | bytes 1572872 | tf_op jit(solution)/shard_map/ppermute | solution.py:263
  43.9 1.3 %shard_map.79 = (bf16[512,512]{1,0:T(8,128)(2,1)S(1)}, bf16[512,512]{1,0:T(8,128)(2,1)S(1)}, bf16[384,512]{1,0:T(8,128)(2,1)S(1)}, bf16[384,512]{1,0:T(8,128)(2,1)S(1)}, bf16[896,512]{1,0:T(8,128)(2,1)S(1)}) custom-call(bf16[4,16,256,128]{3,2,1,0:T(8,128)(2,1)S(1)} %get-tuple-element.40.band_ref, f32[1024,512]{1,0:T(8,128)S(1)} %get-tuple-element.41.near_ref, ...), custom_call_target="tpu_custom_call" | custom-call | flops 536870912 | tf_op jit(solution)/shard_map/pallas_call | solution.py:244
  46.3 1.2 %shard_map.80.near_ref = f32[1024,512]{1,0:T(8,128)S(1)} custom-call(bf16[4,16,256,128]{3,2,1,0:T(8,128)(2,1)S(1)} %get-tuple-element.40.band_ref, bf16[512,512]{1,0:T(8,128)(2,1)S(1)} %get-tuple-element.45.mid_ref, bf16[512,512]{1,0:T(8,128)(2,1)S(1)} %get-tuple-element.49.end_ref), custom_call_target="tpu_custom_call" | custom-call | flops 6442450944 | tf_op jit(solution)/shard_map/pallas_call | solution.py:244
  47.5 8.0 %collective-permute-start.17 = (bf16[384,512]{1,0:T(8,128)(2,1)S(1)}, bf16[384,512]{1,0:T(8,128)(2,1)S(1)}, u32[]{:S(2)}, u32[]{:S(2)}) collective-permute-start(bf16[384,512]{1,0:T(8,128)(2,1)S(1)} %get-tuple-element.64), channel_id=1, source_target_pairs={{0,1},{2,3},{4,5},{6,7},{8,9},{10,11},{12,13},{14,15},{1,0},{3,2},... | collective-permute-start | bytes 1179656 | tf_op jit(solution)/shard_map/ppermute | solution.py:263
  56.4 2.1 %collective-permute-start.7 = (bf16[64,512]{1,0:T(8,128)(2,1)S(1)}, bf16[64,512]{1,0:T(8,128)(2,1)S(1)}, u32[]{:S(2)}, u32[]{:S(2)}) collective-permute-start(bf16[64,512]{1,0:T(8,128)(2,1)S(1)} %get-tuple-element.77), channel_id=1, source_target_pairs={{0,12},{4,8},{8,4},{12,0},{1,13},{5,9},{9,5},{13,1},{2,14},{6,10},... | collective-permute-start | bytes 196616 | tf_op jit(solution)/shard_map/ppermute | solution.py:273
  58.4 0.9 collective-permute-start.6
  59.6 1.7 %collective-permute-start.5 = (bf16[64,512]{1,0:T(8,128)(2,1)S(1)}, bf16[64,512]{1,0:T(8,128)(2,1)S(1)}, u32[]{:S(2)}, u32[]{:S(2)}) collective-permute-start(bf16[64,512]{1,0:T(8,128)(2,1)S(1)} %get-tuple-element.79), channel_id=1, source_target_pairs={{0,4},{4,0},{8,12},{12,8},{1,5},{5,1},{9,13},{13,9},{2,6},{6,2},{1... | collective-permute-start | bytes 196616 | tf_op jit(solution)/shard_map/ppermute | solution.py:273
  61.3 0.7 shard_map.81.near_ref
  62.1 0.9 collective-permute-done.6
  63.0 0.9 collective-permute-done.5
  63.9 2.8 %collective-permute-start.12 = (bf16[64,512]{1,0:T(8,128)(2,1)S(1)}, bf16[64,512]{1,0:T(8,128)(2,1)S(1)}, u32[]{:S(2)}, u32[]{:S(2)}) collective-permute-start(bf16[64,512]{1,0:T(8,128)(2,1)S(1)} %add_convert_fusion.1), channel_id=1, source_target_pairs={{0,3},{1,2},{2,1},{3,0},{4,7},{5,6},{6,5},{7,4},{8,11},{9,10},{10,... | collective-permute-start | bytes 196616 | tf_op jit(solution)/shard_map/ppermute | solution.py:273
  66.7 3.6 %collective-permute-start.11 = (bf16[64,512]{1,0:T(8,128)(2,1)S(1)}, bf16[64,512]{1,0:T(8,128)(2,1)S(1)}, u32[]{:S(2)}, u32[]{:S(2)}) collective-permute-start(bf16[64,512]{1,0:T(8,128)(2,1)S(1)} %add_convert_fusion.1), channel_id=1, source_target_pairs={{0,2},{1,3},{2,0},{3,1},{4,6},{5,7},{6,4},{7,5},{8,10},{9,11},{10,... | collective-permute-start | bytes 196616 | tf_op jit(solution)/shard_map/ppermute | solution.py:273
  70.6 4.8 %collective-permute-done.11 = bf16[64,512]{1,0:T(8,128)(2,1)S(1)} collective-permute-done((bf16[64,512]{1,0:T(8,128)(2,1)S(1)}, bf16[64,512]{1,0:T(8,128)(2,1)S(1)}, u32[]{:S(2)}, u32[]{:S(2)}) %collective-permute-start.11) | collective-permute-done | bytes 65568 | tf_op jit(solution)/shard_map/ppermute | solution.py:273
  75.5 0.7 collective-permute-start.19
  76.2 1.7 %shard_map.83 = bf16[1024,512]{1,0:T(8,128)(2,1)} custom-call(bf16[512,512]{1,0:T(8,128)(2,1)S(1)} %get-tuple-element.44.mixed_mid_ref, bf16[512,512]{1,0:T(8,128)(2,1)S(1)} %get-tuple-element.48.mixed_end_ref, bf16[512,512]{1,0:T(8,128)(2,1)S(1)} %copy-done.1, f32[8,128]{1,0:T(8,128)S(1)} %shard_map.82._), custom_call_target="tpu_custom_call" | custom-call | flops 6442450944 | tf_op jit(solution)/shard_map/pallas_call | solution.py:244
  78.0 6.3 %collective-permute-start.16 = (bf16[128,512]{1,0:T(8,128)(2,1)S(1)}, bf16[128,512]{1,0:T(8,128)(2,1)S(1)}, u32[]{:S(2)}, u32[]{:S(2)}) collective-permute-start(bf16[128,512]{1,0:T(8,128)(2,1)S(1)} %bitcast.17), channel_id=1, source_target_pairs={{0,12},{4,8},{8,4},{12,0},{1,13},{5,9},{9,5},{13,1},{2,14},{6,10},... | collective-permute-start | bytes 393224 | tf_op jit(solution)/shard_map/ppermute | solution.py:273
  84.4 1.4 %collective-permute-start.14 = (bf16[128,512]{1,0:T(8,128)(2,1)S(1)}, bf16[128,512]{1,0:T(8,128)(2,1)S(1)}, u32[]{:S(2)}, u32[]{:S(2)}) collective-permute-start(bf16[128,512]{1,0:T(8,128)(2,1)S(1)} %bitcast.19), channel_id=1, source_target_pairs={{0,4},{4,0},{8,12},{12,8},{1,5},{5,1},{9,13},{13,9},{2,6},{6,2},{1... | collective-permute-start | bytes 393224 | tf_op jit(solution)/shard_map/ppermute | solution.py:273
  85.8 0.9 shard_map.84.near_ref
  86.7 18.0 %collective-permute-done.16.refs_3_ = bf16[128,512]{1,0:T(8,128)(2,1)S(1)} collective-permute-done((bf16[128,512]{1,0:T(8,128)(2,1)S(1)}, bf16[128,512]{1,0:T(8,128)(2,1)S(1)}, u32[]{:S(2)}, u32[]{:S(2)}) %collective-permute-start.16) | collective-permute-done | bytes 131104 | tf_op jit(solution)/shard_map/ppermute | solution.py:273
  104.7 3.7 %collective-permute-done.15.refs_2_ = bf16[128,512]{1,0:T(8,128)(2,1)S(1)} collective-permute-done((bf16[128,512]{1,0:T(8,128)(2,1)S(1)}, bf16[128,512]{1,0:T(8,128)(2,1)S(1)}, u32[]{:S(2)}, u32[]{:S(2)}) %collective-permute-start.15) | collective-permute-done | bytes 131104 | tf_op jit(solution)/shard_map/ppermute | solution.py:273
  108.4 1.1 collective-permute-done.14.refs_1_
  109.5 2.4 %shard_map.85 = bf16[1024,512]{1,0:T(8,128)(2,1)} custom-call(bf16[4,16,256,128]{3,2,1,0:T(8,128)(2,1)S(1)} %get-tuple-element.40.band_ref, f32[1024,512]{1,0:T(8,128)S(1)} %shard_map.84.near_ref, bf16[896,512]{1,0:T(8,128)(2,1)S(1)} %collective-permute-done.19.all7_ref, bf16[512,512]{1,0:T(8,128)(2,1)S(1)} %copy-done.1), custom_call_target="tpu_custom_call" | custom-call | flops 6442450944 | tf_op jit(solution)/shard_map/pallas_call | solution.py:244
  111.9 1.1 shard_map.86
  (37 shorter events, 4.1 us)
Async XLA Ops:
  2.8 20.4 %collective-permute-start = (bf16[640,512]{1,0:T(8,128)(2,1)S(1)}, bf16[640,512]{1,0:T(8,128)(2,1)S(1)}, u32[]{:S(2)}, u32[]{:S(2)}) collective-permute-start(bf16[640,512]{1,0:T(8,128)(2,1)S(1)} %get-tuple-element.42), channel_id=1, source_target_pairs={{0,1},{2,3},{4,5},{6,7},{8,9},{10,11},{12,13},{14,15},{1,0},{3,2},... | collective-permute-start | bytes 1966088 | tf_op jit(solution)/shard_map/ppermute | solution.py:263
  5.9 17.3 %collective-permute-start.1 = (bf16[640,512]{1,0:T(8,128)(2,1)S(1)}, bf16[640,512]{1,0:T(8,128)(2,1)S(1)}, u32[]{:S(2)}, u32[]{:S(2)}) collective-permute-start(bf16[640,512]{1,0:T(8,128)(2,1)S(1)} %get-tuple-element.43), channel_id=1, source_target_pairs={{1,2},{3,4},{5,6},{7,8},{9,10},{11,12},{13,14},{2,1},{4,3},{6,5},{... | collective-permute-start | bytes 1966088 | tf_op jit(solution)/shard_map/ppermute | solution.py:263
  6.6 37.3 %collective-permute-start.2 = (bf16[256,512]{1,0:T(8,128)(2,1)}, bf16[256,512]{1,0:T(8,128)(2,1)S(1)}, u32[]{:S(2)}, u32[]{:S(2)}) collective-permute-start(bf16[256,512]{1,0:T(8,128)(2,1)} %get-tuple-element.46), channel_id=1, source_target_pairs={{0,1},{2,3},{4,5},{6,7},{8,9},{10,11},{12,13},{14,15},{1,0},{3,2},... | collective-permute-start | bytes 786440 | tf_op jit(solution)/shard_map/ppermute | solution.py:263
  11.0 32.9 %collective-permute-start.3 = (bf16[256,512]{1,0:T(8,128)(2,1)S(1)}, bf16[256,512]{1,0:T(8,128)(2,1)S(1)}, u32[]{:S(2)}, u32[]{:S(2)}) collective-permute-start(bf16[256,512]{1,0:T(8,128)(2,1)S(1)} %get-tuple-element.47), channel_id=1, source_target_pairs={{1,2},{3,4},{5,6},{7,8},{9,10},{11,12},{13,14},{2,1},{4,3},{6,5},{... | collective-permute-start | bytes 786440 | tf_op jit(solution)/shard_map/ppermute | solution.py:263
  11.7 1.2 %copy-start.2 = (bf16[1,1024,512]{2,1,0:T(8,128)(2,1)S(1)}, bf16[1,1024,512]{2,1,0:T(8,128)(2,1)}, u32[]{:S(2)}) copy-start(bf16[1,1024,512]{2,1,0:T(8,128)(2,1)} %param.5) | copy-start | bytes 3145732
  13.0 2.1 %copy-start.3 = (bf16[1,8,15,128,128]{4,3,2,1,0:T(8,128)(2,1)S(1)}, bf16[1,8,15,128,128]{4,3,2,1,0:T(8,128)(2,1)}, u32[]{:S(2)}) copy-start(bf16[1,8,15,128,128]{4,3,2,1,0:T(8,128)(2,1)} %param.8) | copy-start | bytes 11796484
  15.1 0.7 copy-start.4
  15.8 7.4 %copy-start = (bf16[1,1024,512]{2,1,0:T(8,128)(2,1)S(1)}, bf16[1,1024,512]{2,1,0:T(8,128)(2,1)}, u32[]{:S(2)}) copy-start(bf16[1,1024,512]{2,1,0:T(8,128)(2,1)} %param.9) | copy-start | bytes 3145732
  15.8 7.4 %copy-start.1 = (bf16[512,512]{1,0:T(8,128)(2,1)S(1)}, bf16[512,512]{1,0:T(8,128)(2,1)}, u32[]{:S(2)}) copy-start(bf16[512,512]{1,0:T(8,128)(2,1)} %weight_ref.7) | copy-start | bytes 1572868
  24.5 33.9 %collective-permute-start.9 = (bf16[512,512]{1,0:T(8,128)(2,1)S(1)}, bf16[512,512]{1,0:T(8,128)(2,1)S(1)}, u32[]{:S(2)}, u32[]{:S(2)}) collective-permute-start(bf16[512,512]{1,0:T(8,128)(2,1)S(1)} %get-tuple-element.45.mid_ref), channel_id=1, source_target_pairs={{1,2},{5,6},{9,10},{13,14},{2,1},{6,5},{10,9},{14,13},{17,18},{21,... | collective-permute-start | bytes 1572872 | tf_op jit(solution)/shard_map/ppermute | solution.py:263
  25.2 34.4 %collective-permute-start.8 = (bf16[512,512]{1,0:T(8,128)(2,1)S(1)}, bf16[512,512]{1,0:T(8,128)(2,1)S(1)}, u32[]{:S(2)}, u32[]{:S(2)}) collective-permute-start(bf16[512,512]{1,0:T(8,128)(2,1)S(1)} %get-tuple-element.45.mid_ref), channel_id=1, source_target_pairs={{0,1},{2,3},{4,5},{6,7},{8,9},{10,11},{12,13},{14,15},{1,0},{3,2},... | collective-permute-start | bytes 1572872 | tf_op jit(solution)/shard_map/ppermute | solution.py:263
  46.2 10.0 %collective-permute-start.4 = (f32[256,512]{1,0:T(8,128)S(1)}, f32[256,512]{1,0:T(8,128)S(1)}, u32[]{:S(2)}, u32[]{:S(2)}) collective-permute-start(f32[256,512]{1,0:T(8,128)S(1)} %constant_dynamic-slice_fusion), channel_id=1, source_target_pairs={{0,16},{16,0},{1,17},{17,1},{2,18},{18,2},{3,19},{19,3},{4,20},{20... | collective-permute-start | bytes 1572872 | tf_op jit(solution)/shard_map/ppermute | solution.py:273
  47.5 36.9 %collective-permute-start.17 = (bf16[384,512]{1,0:T(8,128)(2,1)S(1)}, bf16[384,512]{1,0:T(8,128)(2,1)S(1)}, u32[]{:S(2)}, u32[]{:S(2)}) collective-permute-start(bf16[384,512]{1,0:T(8,128)(2,1)S(1)} %get-tuple-element.64), channel_id=1, source_target_pairs={{0,1},{2,3},{4,5},{6,7},{8,9},{10,11},{12,13},{14,15},{1,0},{3,2},... | collective-permute-start | bytes 1179656 | tf_op jit(solution)/shard_map/ppermute | solution.py:263
  55.5 30.3 %collective-permute-start.18 = (bf16[384,512]{1,0:T(8,128)(2,1)S(1)}, bf16[384,512]{1,0:T(8,128)(2,1)S(1)}, u32[]{:S(2)}, u32[]{:S(2)}) collective-permute-start(bf16[384,512]{1,0:T(8,128)(2,1)S(1)} %get-tuple-element.65), channel_id=1, source_target_pairs={{1,2},{5,6},{9,10},{13,14},{2,1},{6,5},{10,9},{14,13},{17,18},{21,... | collective-permute-start | bytes 1179656 | tf_op jit(solution)/shard_map/ppermute | solution.py:263
  56.4 5.7 %collective-permute-start.7 = (bf16[64,512]{1,0:T(8,128)(2,1)S(1)}, bf16[64,512]{1,0:T(8,128)(2,1)S(1)}, u32[]{:S(2)}, u32[]{:S(2)}) collective-permute-start(bf16[64,512]{1,0:T(8,128)(2,1)S(1)} %get-tuple-element.77), channel_id=1, source_target_pairs={{0,12},{4,8},{8,4},{12,0},{1,13},{5,9},{9,5},{13,1},{2,14},{6,10},... | collective-permute-start | bytes 196616 | tf_op jit(solution)/shard_map/ppermute | solution.py:273
  58.4 4.6 %collective-permute-start.6 = (bf16[64,512]{1,0:T(8,128)(2,1)S(1)}, bf16[64,512]{1,0:T(8,128)(2,1)S(1)}, u32[]{:S(2)}, u32[]{:S(2)}) collective-permute-start(bf16[64,512]{1,0:T(8,128)(2,1)S(1)} %get-tuple-element.78), channel_id=1, source_target_pairs={{0,8},{4,12},{8,0},{12,4},{1,9},{5,13},{9,1},{13,5},{2,10},{6,14},... | collective-permute-start | bytes 196616 | tf_op jit(solution)/shard_map/ppermute | solution.py:273
  59.6 4.3 %collective-permute-start.5 = (bf16[64,512]{1,0:T(8,128)(2,1)S(1)}, bf16[64,512]{1,0:T(8,128)(2,1)S(1)}, u32[]{:S(2)}, u32[]{:S(2)}) collective-permute-start(bf16[64,512]{1,0:T(8,128)(2,1)S(1)} %get-tuple-element.79), channel_id=1, source_target_pairs={{0,4},{4,0},{8,12},{12,8},{1,5},{5,1},{9,13},{13,9},{2,6},{6,2},{1... | collective-permute-start | bytes 196616 | tf_op jit(solution)/shard_map/ppermute | solution.py:273
  63.9 6.7 %collective-permute-start.12 = (bf16[64,512]{1,0:T(8,128)(2,1)S(1)}, bf16[64,512]{1,0:T(8,128)(2,1)S(1)}, u32[]{:S(2)}, u32[]{:S(2)}) collective-permute-start(bf16[64,512]{1,0:T(8,128)(2,1)S(1)} %add_convert_fusion.1), channel_id=1, source_target_pairs={{0,3},{1,2},{2,1},{3,0},{4,7},{5,6},{6,5},{7,4},{8,11},{9,10},{10,... | collective-permute-start | bytes 196616 | tf_op jit(solution)/shard_map/ppermute | solution.py:273
  66.7 8.7 %collective-permute-start.11 = (bf16[64,512]{1,0:T(8,128)(2,1)S(1)}, bf16[64,512]{1,0:T(8,128)(2,1)S(1)}, u32[]{:S(2)}, u32[]{:S(2)}) collective-permute-start(bf16[64,512]{1,0:T(8,128)(2,1)S(1)} %add_convert_fusion.1), channel_id=1, source_target_pairs={{0,2},{1,3},{2,0},{3,1},{4,6},{5,7},{6,4},{7,5},{8,10},{9,11},{10,... | collective-permute-start | bytes 196616 | tf_op jit(solution)/shard_map/ppermute | solution.py:273
  70.3 5.1 %collective-permute-start.10 = (bf16[64,512]{1,0:T(8,128)(2,1)S(1)}, bf16[64,512]{1,0:T(8,128)(2,1)S(1)}, u32[]{:S(2)}, u32[]{:S(2)}) collective-permute-start(bf16[64,512]{1,0:T(8,128)(2,1)S(1)} %add_convert_fusion.1), channel_id=1, source_target_pairs={{0,1},{1,0},{2,3},{3,2},{4,5},{5,4},{6,7},{7,6},{8,9},{9,8},{10,11... | collective-permute-start | bytes 196616 | tf_op jit(solution)/shard_map/ppermute | solution.py:273
  75.4 2.5 %collective-permute-start.13 = (bf16[64,512]{1,0:T(8,128)(2,1)S(1)}, bf16[64,512]{1,0:T(8,128)(2,1)S(1)}, u32[]{:S(2)}, u32[]{:S(2)}) collective-permute-start(bf16[64,512]{1,0:T(8,128)(2,1)S(1)} %add_convert_fusion), channel_id=1, source_target_pairs={{0,16},{16,0},{1,17},{17,1},{2,18},{18,2},{3,19},{19,3},{4,20},{20... | collective-permute-start | bytes 196616 | tf_op jit(solution)/shard_map/ppermute | solution.py:273
  75.5 34.0 %collective-permute-start.19 = (bf16[896,512]{1,0:T(8,128)(2,1)S(1)}, bf16[896,512]{1,0:T(8,128)(2,1)S(1)}, u32[]{:S(2)}, u32[]{:S(2)}) collective-permute-start(bf16[896,512]{1,0:T(8,128)(2,1)S(1)} %get-tuple-element.71), channel_id=1, source_target_pairs={{3,4},{7,8},{11,12},{4,3},{8,7},{12,11},{19,20},{23,24},{27,28},{2... | collective-permute-start | bytes 2752520 | tf_op jit(solution)/shard_map/ppermute | solution.py:375
  78.0 26.8 %collective-permute-start.16 = (bf16[128,512]{1,0:T(8,128)(2,1)S(1)}, bf16[128,512]{1,0:T(8,128)(2,1)S(1)}, u32[]{:S(2)}, u32[]{:S(2)}) collective-permute-start(bf16[128,512]{1,0:T(8,128)(2,1)S(1)} %bitcast.17), channel_id=1, source_target_pairs={{0,12},{4,8},{8,4},{12,0},{1,13},{5,9},{9,5},{13,1},{2,14},{6,10},... | collective-permute-start | bytes 393224 | tf_op jit(solution)/shard_map/ppermute | solution.py:273
  84.3 24.1 %collective-permute-start.15 = (bf16[128,512]{1,0:T(8,128)(2,1)S(1)}, bf16[128,512]{1,0:T(8,128)(2,1)S(1)}, u32[]{:S(2)}, u32[]{:S(2)}) collective-permute-start(bf16[128,512]{1,0:T(8,128)(2,1)S(1)} %bitcast.18), channel_id=1, source_target_pairs={{0,8},{4,12},{8,0},{12,4},{1,9},{5,13},{9,1},{13,5},{2,10},{6,14},... | collective-permute-start | bytes 393224 | tf_op jit(solution)/shard_map/ppermute | solution.py:273
  84.4 25.0 %collective-permute-start.14 = (bf16[128,512]{1,0:T(8,128)(2,1)S(1)}, bf16[128,512]{1,0:T(8,128)(2,1)S(1)}, u32[]{:S(2)}, u32[]{:S(2)}) collective-permute-start(bf16[128,512]{1,0:T(8,128)(2,1)S(1)} %bitcast.19), channel_id=1, source_target_pairs={{0,4},{4,0},{8,12},{12,8},{1,5},{5,1},{9,13},{13,9},{2,6},{6,2},{1... | collective-permute-start | bytes 393224 | tf_op jit(solution)/shard_map/ppermute | solution.py:273

commit v4 on v3

--- a/solution.py
+++ b/solution.py
@@ -1,5 +1,3 @@
-import functools
-
 import jax
 import jax.numpy as jnp
 from jax import lax
@@ -12,7 +10,6 @@
 LINE = ("blk", "rep")
 LEVEL = ("dp", "blk")
 VMEM_BYTES = 14 << 20
-LONG = 12
 BF16, F32 = jnp.bfloat16, jnp.float32
 
 
@@ -149,8 +146,8 @@
     by_parity(body)
 
 
-def outer_kernel(band_ref, near_ref, first5_ref, second5_ref, first2_ref, second2_ref, weight_ref, cot_ref, mid_ref,
-                 mixed_ref, end_ref, first3_ref, second3_ref, all7_ref):
+def outer_kernel(band_ref, near_ref, first5_ref, second5_ref, first2_ref, second2_ref, weight_ref, cot_ref,
+                 mixed_ref, end_ref, first3_ref, second3_ref):
     size = band_ref.shape[3]
     height = PAIR * size
     five, two = (first5_ref, second5_ref), (first2_ref, second2_ref)
@@ -175,41 +172,41 @@
         for out in three:
             out[size : 2 * size, :] = dagg[:size]
         three[right][2 * size :, :] = dagg[size:]
-        all7_ref[: 4 * size, :] = mid_ref[...]
-        all7_ref[4 * size :, :] = second3_ref[...]
 
     by_parity(body)
 
 
-def own_kernel(band_ref, mid_ref, end_ref, near_ref):
+def own_kernel(band_ref, mid_ref, end_ref, mixed_mid_ref, mixed_end_ref, weight_ref, near_ref, activ_ref):
     tiles, _, height, _ = band_ref.shape
     sources = [
         (mine((0, 1)), end_ref.at[:height]),
         (mine((2, 3, 4, 5)), mid_ref),
         (mine((6, 7)), end_ref.at[height:]),
     ]
-    for t in range(tiles):
-        near_ref[pl.ds(t * height, height), :] = banded(band_ref, t, sources)
-
-
-def mark_kernel(near_ref, out_ref):
-    out_ref[...] = near_ref[: out_ref.shape[0], : out_ref.shape[1]]
-
-
-def activ_kernel(mixed_mid_ref, mixed_end_ref, weight_ref, _, activ_ref):
-    height = mixed_mid_ref.shape[0] // 2
     halves = (mixed_end_ref[:height, :], mixed_mid_ref[:height, :], mixed_mid_ref[height:, :], mixed_end_ref[height:, :])
     for t, mixed in enumerate(halves):
+        at = pl.ds(t * height, height)
+        near_ref[at, :] = banded(band_ref, t, sources)
         agg = jnp.dot(mixed, weight_ref[...], preferred_element_type=F32)
-        activ_ref[pl.ds(t * height, height), :] = (agg * jax.nn.sigmoid(agg)).astype(activ_ref.dtype)
-
-
-def add_kernel(left_rows, right_rows, band_ref, near_ref, first_ref, second_ref, out_ref):
-    tiles, _, height, _ = band_ref.shape
-    came = (first_ref, second_ref)
+        activ_ref[at, :] = (agg * jax.nn.sigmoid(agg)).astype(activ_ref.dtype)
+
+
+LAST = before((1, 6, 7)) + after((1, 6, 0))
+
+
+def last_of(t, span):
+    return [i for i, w in enumerate(LAST) if 0 <= w - PAIR * t < span]
+
+
+def add_kernel(band_ref, near_ref, first4_ref, second4_ref, out_ref, last_ref):
+    tiles, span, height, _ = band_ref.shape
+    for t in range(tiles):
+        for i, which in enumerate(last_of(t, span)):
+            last_ref[t, i] = band_ref[t, LAST[which] - PAIR * t]
+    four = (first4_ref, second4_ref)
 
     def body(left, right):
-        sources = [(before(left_rows), came[left]), (after(right_rows), came[right])]
+        sources = [(before(range(2, 6)), four[left]), (after(range(2, 6)), four[right])]
         for t in range(tiles):
             at = pl.ds(t * height, height)
             out_ref[at, :] = near_ref[at, :] + banded(band_ref, t, sources)
@@ -217,18 +214,22 @@
     by_parity(body)
 
 
-def back_kernel(band_ref, near_ref, all7_ref, weight_ref, out_ref, held_ref, sems):
-    tiles, _, height, _ = band_ref.shape
+def back_kernel(last_ref, near_ref, first3_ref, second3_ref, weight_ref, out_ref, held_ref, sems):
+    tiles, _, height, size = last_ref.shape
+    three = (first3_ref, second3_ref)
 
     def body(left, right):
-        if left:
-            sources = [(before((2, 3, 4, 5, 1, 6, 7)), all7_ref)]
-        else:
-            sources = [(after((2, 3, 4, 5, 1, 6, 0)), all7_ref)]
+        sources = [(side, i * size) for side in (left, right) for i in range(3)]
         copies = []
         for t in range(tiles):
             at = pl.ds(t * height, height)
-            dproj = near_ref[at, :] + banded(band_ref, t, sources)
+            met = last_of(t, 2 * REACH + PAIR)
+            blocks = [three[side][first : first + size, :] for side, first in (sources[i] for i in met)]
+            dproj = near_ref[at, :] + jnp.dot(
+                jnp.concatenate([last_ref[t, i] for i in range(len(met))], axis=1),
+                jnp.concatenate(blocks, axis=0),
+                preferred_element_type=F32,
+            )
             held_ref[at, :] = lax.dot_general(
                 dproj.astype(BF16), weight_ref[...], (((1,), (1,)), ((), ())), preferred_element_type=F32
             ).astype(BF16)
@@ -252,15 +253,13 @@
     )(*ins)
 
 
-def swap_pairs(start, across):
-    count, run = lax.axis_size(LINE), lax.axis_size(LINE[1])
-    pairs = [(i, i + 1) for i in range(start, count - 1, 2)]
-    pairs = [(i, j) for i, j in pairs if across is None or (j % run == 0) == across]
-    return pairs + [(j, i) for i, j in pairs]
-
-
-def swapped(first, second, across=None):
-    return [lax.ppermute(x, LINE, swap_pairs(start, across)) for x, start in ((first, 0), (second, 1))]
+def swapped(first, second):
+    count = lax.axis_size(LINE)
+    result = []
+    for x, start in ((first, 0), (second, 1)):
+        pairs = [(i, i + 1) for i in range(start, count - 1, 2)]
+        result.append(lax.ppermute(x, LINE, pairs + [(j, i) for i, j in pairs]))
+    return result
 
 
 def partner(j, d, n):
@@ -272,25 +271,6 @@
     return [
         lax.ppermute(parts(d), axis, [(j, partner(j, d, n)) for j in range(n)]) for d in range(1, n)
     ]
-
-
-def scatter(x, axis, dtype):
-    n = lax.axis_size(axis)
-    me = lax.axis_index(axis)
-    step = x.shape[0] // n
-
-    def part(d):
-        return lax.dynamic_slice_in_dim(x, partner(me, d, n) * step, step)
-
-    return part(0) if n & (n - 1) == 0 else lax.dynamic_slice_in_dim(x, me * step, step), from_all(
-        lambda d: part(d).astype(dtype), axis
-    )
-
-
-def add_all(kept, came):
-    for part in came:
-        kept = kept + part.astype(F32)
-    return kept
 
 
 def pairwise(parts):
@@ -352,46 +332,38 @@
     mixed_mid, mid = kernel_call(
         inner_kernel, [band, near, *five, weight, cotangent[0]], [chip(4), chip(4)], product
     )
-    four = swapped(mid, mid, across=False)
-    mixed_end, end, *three, all7 = kernel_call(
-        outer_kernel, [band, near, *five, *two, weight, cotangent[0], mid],
-        [chip(4), chip(4), chip(3), chip(3), chip(7)], product,
-    )
-    three = swapped(*three, across=False)
-    full = [chip(rows, F32)]
+    four = swapped(mid, mid)
+    mixed_end, end, *sent = kernel_call(
+        outer_kernel, [band, near, *five, *two, weight, cotangent[0]],
+        [chip(4), chip(4), chip(3), chip(3)], product,
+    )
+    three = swapped(*sent)
+    near, activ = kernel_call(
+        own_kernel, [band, mid, end, mixed_mid, mixed_end, weight], [chip(rows, F32), plain(rows)], product
+    )
+    near, last = kernel_call(
+        add_kernel, [band, held(near)[0], *four],
+        [chip(rows, F32), pltpu.VMEM((tiles, len(last_of(0, span)), height, size), BF16)], 12 * product,
+    )
     term = term_of(mixed_mid, mid) + term_of(mixed_end, end)
-    kept, came = scatter(term, LEVEL[0], F32)
-    near = kernel_call(own_kernel, [band, mid, end], full, LONG * product)[0]
-    came, near = lax.optimization_barrier((came, near))
-    kept, came = scatter(add_all(kept, came), LEVEL[1], BF16)
-    near = kernel_call(
-        functools.partial(add_kernel, (2, 3, 4, 5), (2, 3, 4, 5)), [band, *held(near), *four], full, LONG * product
-    )[0]
-    came, near = lax.optimization_barrier((came, near))
-    term = add_all(kept, came).astype(BF16)
+    term = lax.all_to_all(
+        term.astype(BF16).reshape(lax.axis_size(LEVEL), -1, width), LEVEL, 0, 0, tiled=True
+    )
+    term, near = lax.optimization_barrier((term, near))
+    term = jnp.sum(term.astype(F32), axis=0)
+    term = term.astype(BF16)
     parts = [term, *from_all(lambda d: term, "rep")]
-    mark = kernel_call(mark_kernel, held(near), [pltpu.VMEM((8, 128), F32)], LONG * product)[0]
-    *parts, all7, mark = lax.optimization_barrier((*parts, all7, mark))
-    all7 = lax.ppermute(all7, LINE, swap_pairs(1, True))
-    term = pairwise(parts).astype(BF16)
-    other, = from_all(lambda d: term, LEVEL[0])
-    activ = kernel_call(
-        activ_kernel, [mixed_mid, mixed_end, weight, *held(mark)], [plain(rows)], LONG * product
-    )[0]
-    other, activ = lax.optimization_barrier((other, activ))
-    term = jnp.where(lax.axis_index(LEVEL[0]) == 0, jnp.stack([term, other]), jnp.stack([other, term]))
-    term = term.reshape(-1, width)
-    parts = [term, *from_all(lambda d: term, LEVEL[1])]
-    near = kernel_call(
-        functools.partial(add_kernel, (1, 6, 7), (1, 6, 0)), [band, *held(near), *three], full, LONG * product
-    )[0]
-    parts, near = lax.optimization_barrier((parts, near))
     feat_grad = kernel_call(
-        back_kernel, [band, *held(near), all7, weight], [plain(rows)], LONG * product,
+        back_kernel, [*held(last, near), *three, weight], [plain(rows)], 12 * product,
         out_specs=[anywhere()],
         scratch_shapes=[pltpu.VMEM((zones, width), BF16), pltpu.SemaphoreType.DMA((tiles,))],
     )[0]
     parts, feat_grad = lax.optimization_barrier((parts, feat_grad))
+    term = pairwise(parts).astype(BF16)
+    other, = from_all(lambda d: term, LEVEL[0])
+    term = jnp.where(lax.axis_index(LEVEL[0]) == 0, jnp.stack([term, other]), jnp.stack([other, term]))
+    term = term.reshape(-1, width)
+    parts = [term, *from_all(lambda d: term, LEVEL[1])]
     weight_grad = kernel_call(
         join_kernel, parts, [jax.ShapeDtypeStruct((width, width), F32)], 0
     )[0]

time: 113 us -> 108 us (0.956)
  the two profiles are of different devices: /device:TPU:0 before, /device:TPU:16 now
where the time goes in v4:
time: 108 us
  waiting for transfers between devices  42 us (39%)
  starting transfers between devices  31.6 us (29%)
  Pallas kernels  21.4 us (20%)
  local copies, waits for them, and re-layouts  9.15 us (8%)
  matrix products  1.72 us (2%)
  other arithmetic  1.17 us (1%)
    ppermute x8, waiting for transfers between devices, swapped(): result.append(lax.ppermute(x, LINE, pairs + [(j, i) for i, j in pairs]))  34.2 us
    pallas_call x8, Pallas kernels, kernel_call(): pl.pallas_call(body, out_shape=outs, in_specs=specs or [whole()] * len(in...  21.4 us
    ppermute x8, starting transfers between devices, swapped(): result.append(lax.ppermute(x, LINE, pairs + [(j, i) for i, j in pairs]))  15.1 us
    ppermute x7, starting transfers between devices, from_all(): lax.ppermute(parts(d), axis, [(j, partner(j, d, n)) for j in range(n)])  10.3 us
    unnamed x20, local copies, waits for them, and re-layouts  9.15 us
    ppermute x7, waiting for transfers between devices, from_all(): lax.ppermute(parts(d), axis, [(j, partner(j, d, n)) for j in range(n)])  7.79 us
    all_to_all x1, starting transfers between devices, shards(): lax.all_to_all(term.astype(BF16).reshape(lax.axis_size(LEVEL), -1, width)...  6.23 us
  transfers between devices with their start and end apart: 16, of which 7 were waited for; matrix products, arithmetic and copies ran while one was open for 3% of the time, Pallas kernels for 17%

profile of v4, /device:TPU:16, one launch (start us, length us, event | category | flops | bytes accessed | tf_op | source)
XLA Modules:
  0.0 107.9 jit_solution(6370945924199140605)
XLA Ops:
  0.6 1.5 %shard_map.77 = (bf16[640,512]{1,0:T(8,128)(2,1)S(1)}, bf16[640,512]{1,0:T(8,128)(2,1)S(1)}, bf16[256,512]{1,0:T(8,128)(2,1)S(1)}, bf16[256,512]{1,0:T(8,128)(2,1)S(1)}) custom-call(bf16[1024,512]{1,0:T(8,128)(2,1)} %bitcast.16), custom_call_target="tpu_custom_call" | custom-call | tf_op jit(solution)/shard_map/pallas_call | solution.py:245
  2.1 1.6 %collective-permute-start = (bf16[640,512]{1,0:T(8,128)(2,1)S(1)}, bf16[640,512]{1,0:T(8,128)(2,1)S(1)}, u32[]{:S(2)}, u32[]{:S(2)}) collective-permute-start(bf16[640,512]{1,0:T(8,128)(2,1)S(1)} %get-tuple-element.28), channel_id=1, source_target_pairs={{0,1},{2,3},{4,5},{6,7},{8,9},{10,11},{12,13},{14,15},{1,0},{3,2},... | collective-permute-start | bytes 1966088 | tf_op jit(solution)/shard_map/ppermute | solution.py:261
  3.8 1.9 %collective-permute-start.1 = (bf16[640,512]{1,0:T(8,128)(2,1)S(1)}, bf16[640,512]{1,0:T(8,128)(2,1)S(1)}, u32[]{:S(2)}, u32[]{:S(2)}) collective-permute-start(bf16[640,512]{1,0:T(8,128)(2,1)S(1)} %get-tuple-element.29), channel_id=1, source_target_pairs={{1,2},{3,4},{5,6},{7,8},{9,10},{11,12},{13,14},{2,1},{4,3},{6,5},{... | collective-permute-start | bytes 1966088 | tf_op jit(solution)/shard_map/ppermute | solution.py:261
  5.7 2.8 %collective-permute-start.2 = (bf16[256,512]{1,0:T(8,128)(2,1)S(1)}, bf16[256,512]{1,0:T(8,128)(2,1)S(1)}, u32[]{:S(2)}, u32[]{:S(2)}) collective-permute-start(bf16[256,512]{1,0:T(8,128)(2,1)S(1)} %get-tuple-element.31), channel_id=1, source_target_pairs={{0,1},{2,3},{4,5},{6,7},{8,9},{10,11},{12,13},{14,15},{1,0},{3,2},... | collective-permute-start | bytes 786440 | tf_op jit(solution)/shard_map/ppermute | solution.py:261
  8.5 1.9 %collective-permute-start.3 = (bf16[256,512]{1,0:T(8,128)(2,1)S(1)}, bf16[256,512]{1,0:T(8,128)(2,1)S(1)}, u32[]{:S(2)}, u32[]{:S(2)}) collective-permute-start(bf16[256,512]{1,0:T(8,128)(2,1)S(1)} %get-tuple-element.32), channel_id=1, source_target_pairs={{1,2},{3,4},{5,6},{7,8},{9,10},{11,12},{13,14},{2,1},{4,3},{6,5},{... | collective-permute-start | bytes 786440 | tf_op jit(solution)/shard_map/ppermute | solution.py:261
  10.4 1.2 %copy-done.4 = bf16[1,1024,512]{2,1,0:T(8,128)(2,1)S(1)} copy-done((bf16[1,1024,512]{2,1,0:T(8,128)(2,1)S(1)}, bf16[1,1024,512]{2,1,0:T(8,128)(2,1)}, u32[]{:S(2)}) %copy-start.4) | copy-done | bytes 1048600
  11.6 2.1 %copy-done.5 = bf16[1,8,15,128,128]{4,3,2,1,0:T(8,128)(2,1)S(1)} copy-done((bf16[1,8,15,128,128]{4,3,2,1,0:T(8,128)(2,1)S(1)}, bf16[1,8,15,128,128]{4,3,2,1,0:T(8,128)(2,1)}, u32[]{:S(2)}) %copy-start.5) | copy-done | bytes 3932184
  14.4 8.3 %shard_map.76 = (bf16[4,16,256,128]{3,2,1,0:T(8,128)(2,1)S(1)}, f32[1024,512]{1,0:T(8,128)S(1)}) custom-call(s32[8,15]{1,0:T(8,128)S(1)} %bitcast.23, bf16[8,15,128,128]{3,2,1,0:T(8,128)(2,1)S(1)} %bitcast.22, bf16[1024,512]{1,0:T(8,128)(2,1)S(1)} %bitcast.17), custom_call_target="tpu_custom_call" | custom-call | flops 2147483648 | tf_op jit(solution)/shard_map/pallas_call | solution.py:245
  22.7 12.1 %collective-permute-done.1.second5_ref = bf16[640,512]{1,0:T(8,128)(2,1)S(1)} collective-permute-done((bf16[640,512]{1,0:T(8,128)(2,1)S(1)}, bf16[640,512]{1,0:T(8,128)(2,1)S(1)}, u32[]{:S(2)}, u32[]{:S(2)}) %collective-permute-start.1) | collective-permute-done | bytes 655392 | tf_op jit(solution)/shard_map/ppermute | solution.py:261
  34.8 1.3 %shard_map.78 = (bf16[512,512]{1,0:T(8,128)(2,1)S(1)}, bf16[512,512]{1,0:T(8,128)(2,1)S(1)}) custom-call(bf16[4,16,256,128]{3,2,1,0:T(8,128)(2,1)S(1)} %get-tuple-element.26.band_ref, f32[1024,512]{1,0:T(8,128)S(1)} %get-tuple-element.27.near_ref, bf16[640,512]{1,0:T(8,128)(2,1)S(1)} %collective-permute-done.first5_ref, ...), custom_call_target="tpu_custom_call" | custom-call | flops 536870912 | tf_op jit(solution)/shard_map/pallas_call | solution.py:245
  36.1 1.4 %collective-permute-start.4 = (bf16[512,512]{1,0:T(8,128)(2,1)S(1)}, bf16[512,512]{1,0:T(8,128)(2,1)S(1)}, u32[]{:S(2)}, u32[]{:S(2)}) collective-permute-start(bf16[512,512]{1,0:T(8,128)(2,1)S(1)} %get-tuple-element.30.mid_ref), channel_id=1, source_target_pairs={{0,1},{2,3},{4,5},{6,7},{8,9},{10,11},{12,13},{14,15},{1,0},{3,2},... | collective-permute-start | bytes 1572872 | tf_op jit(solution)/shard_map/ppermute | solution.py:261
  37.5 3.1 %collective-permute-start.5 = (bf16[512,512]{1,0:T(8,128)(2,1)S(1)}, bf16[512,512]{1,0:T(8,128)(2,1)}, u32[]{:S(2)}, u32[]{:S(2)}) collective-permute-start(bf16[512,512]{1,0:T(8,128)(2,1)S(1)} %get-tuple-element.30.mid_ref), channel_id=1, source_target_pairs={{1,2},{3,4},{5,6},{7,8},{9,10},{11,12},{13,14},{2,1},{4,3},{6,5},{... | collective-permute-start | bytes 1572872 | tf_op jit(solution)/shard_map/ppermute | solution.py:261
  40.6 5.5 %collective-permute-done.3.second2_ref = bf16[256,512]{1,0:T(8,128)(2,1)S(1)} collective-permute-done((bf16[256,512]{1,0:T(8,128)(2,1)S(1)}, bf16[256,512]{1,0:T(8,128)(2,1)S(1)}, u32[]{:S(2)}, u32[]{:S(2)}) %collective-permute-start.3) | collective-permute-done | bytes 262176 | tf_op jit(solution)/shard_map/ppermute | solution.py:261
  46.1 1.3 %shard_map.79 = (bf16[512,512]{1,0:T(8,128)(2,1)S(1)}, bf16[512,512]{1,0:T(8,128)(2,1)S(1)}, bf16[384,512]{1,0:T(8,128)(2,1)S(1)}, bf16[384,512]{1,0:T(8,128)(2,1)S(1)}) custom-call(bf16[4,16,256,128]{3,2,1,0:T(8,128)(2,1)S(1)} %get-tuple-element.26.band_ref, f32[1024,512]{1,0:T(8,128)S(1)} %get-tuple-element.27.near_ref, ...), custom_call_target="tpu_custom_call" | custom-call | flops 536870912 | tf_op jit(solution)/shard_map/pallas_call | solution.py:245
  47.8 1.3 %fusion = bf16[512,512]{1,0:T(8,128)(2,1)} fusion(f32[512,512]{1,0:T(8,128)S(1)} %fusion.1, bf16[512,512]{1,0:T(8,128)(2,1)S(1)} %get-tuple-element.34.mixed_mid_ref, bf16[512,512]{1,0:T(8,128)(2,1)S(1)} %get-tuple-element.30.mid_ref), kind=kOutput, calls=%fused_computation.1 | convolution fusion | flops 268959744 | bytes 2621440 | tf_op jit(solution)/shard_map/dot_general | solution.py:297
  49.1 6.2 %all-to-all-start = ((bf16[8,64,512]{2,1,0:T(8,128)(2,1)}), bf16[8,64,512]{2,1,0:T(8,128)(2,1)}, u32[]{:S(2)}, u32[]{:S(2)}) async-start(bf16[8,64,512]{2,1,0:T(8,128)(2,1)} %bitcast.24), calls=%async_computation | async-start | bytes 1048576 | tf_op jit(solution)/shard_map/all_to_all | solution.py:349
  55.3 2.4 %collective-permute-start.10 = (bf16[384,512]{1,0:T(8,128)(2,1)S(1)}, bf16[384,512]{1,0:T(8,128)(2,1)}, u32[]{:S(2)}, u32[]{:S(2)}) collective-permute-start(bf16[384,512]{1,0:T(8,128)(2,1)S(1)} %get-tuple-element.43), channel_id=1, source_target_pairs={{1,2},{3,4},{5,6},{7,8},{9,10},{11,12},{13,14},{2,1},{4,3},{6,5},{... | collective-permute-start | bytes 1179656 | tf_op jit(solution)/shard_map/ppermute | solution.py:261
  57.7 2.2 %copy-done.1 = bf16[4,16,256,128]{3,2,1,0:T(8,128)(2,1)S(1)} copy-done((bf16[4,16,256,128]{3,2,1,0:T(8,128)(2,1)S(1)}, bf16[4,16,256,128]{3,2,1,0:T(8,128)(2,1)}, u32[]{:S(2)}) %copy-start.1) | copy-done | bytes 4194328
  59.9 2.8 %shard_map.80 = (f32[1024,512]{1,0:T(8,128)S(1)}, bf16[1024,512]{1,0:T(8,128)(2,1)}) custom-call(bf16[4,16,256,128]{3,2,1,0:T(8,128)(2,1)S(1)} %copy-done.1, bf16[512,512]{1,0:T(8,128)(2,1)S(1)} %get-tuple-element.30.mid_ref, bf16[512,512]{1,0:T(8,128)(2,1)S(1)} %get-tuple-element.33.end_ref, bf16[512,512]{1,0:T(8,128)(2,1)S(1)} %get-tuple-element.34.mixed_mid_ref, ...), custom_call_target="tpu_custom_call" | custom-call | flops 536870912 | tf_op jit(solution)/shard_map/pallas_call | solution.py:245
  62.7 5.9 %collective-permute-done.5.second4_ref = bf16[512,512]{1,0:T(8,128)(2,1)} collective-permute-done((bf16[512,512]{1,0:T(8,128)(2,1)S(1)}, bf16[512,512]{1,0:T(8,128)(2,1)}, u32[]{:S(2)}, u32[]{:S(2)}) %collective-permute-start.5) | collective-permute-done | bytes 524320 | tf_op jit(solution)/shard_map/ppermute | solution.py:261
  68.5 1.8 %shard_map.81 = (f32[1024,512]{1,0:T(8,128)S(1)}, bf16[4,4,256,128]{3,2,1,0:T(8,128)(2,1)S(1)}) custom-call(bf16[4,16,256,128]{3,2,1,0:T(8,128)(2,1)S(1)} %copy-done.1, f32[1024,512]{1,0:T(8,128)S(1)} %get-tuple-element.37.near_ref, bf16[512,512]{1,0:T(8,128)(2,1)S(1)} %collective-permute-done.4.first4_ref, bf16[512,512]{1,0:T(8,128)(2,1)} %collective-permute-done.5.second4_ref), custom_call_target="tpu_custom_call" | custom-call | flops 6442450944 | tf_op jit(solution)/shard_map/pallas_call | solution.py:245
  70.4 1.3 %copy-done.8 = f32[1024,512]{1,0:T(8,128)} copy-done((f32[1024,512]{1,0:T(8,128)}, f32[1024,512]{1,0:T(8,128)S(1)}, u32[]{:S(2)}) %copy-start.8) | copy-done | bytes 2097176
  71.7 1.1 %reduce_sum.12 = bf16[64,512]{1,0:T(8,128)(2,1)S(1)} reduce(bf16[8,64,512]{2,1,0:T(8,128)(2,1)} %all-to-all-done, bf16[]{:T(256)} %constant.3.clone.1), dimensions={0}, to_apply=%region_0.0 | reduce | flops 229376 | bytes 589826 | tf_op jit(solution)/shard_map/reduce_sum | solution.py:353
  72.8 3.0 %collective-permute-start.6 = (bf16[64,512]{1,0:T(8,128)(2,1)S(1)}, bf16[64,512]{1,0:T(8,128)(2,1)S(1)}, u32[]{:S(2)}, u32[]{:S(2)}) collective-permute-start(bf16[64,512]{1,0:T(8,128)(2,1)S(1)} %reduce_sum.12), channel_id=1, source_target_pairs={{0,1},{1,0},{2,3},{3,2},{4,5},{5,4},{6,7},{7,6},{8,9},{9,8},{10,11... | collective-permute-start | bytes 196616 | tf_op jit(solution)/shard_map/ppermute | solution.py:272
  77.4 10.8 %collective-permute-done.10.second3_ref = bf16[384,512]{1,0:T(8,128)(2,1)} collective-permute-done((bf16[384,512]{1,0:T(8,128)(2,1)S(1)}, bf16[384,512]{1,0:T(8,128)(2,1)}, u32[]{:S(2)}, u32[]{:S(2)}) %collective-permute-start.10) | collective-permute-done | bytes 393248 | tf_op jit(solution)/shard_map/ppermute | solution.py:261
  88.2 1.6 %copy-done.9 = f32[1024,512]{1,0:T(8,128)S(1)} copy-done((f32[1024,512]{1,0:T(8,128)S(1)}, f32[1024,512]{1,0:T(8,128)}, u32[]{:S(2)}) %copy-start.9) | copy-done | bytes 2097176
  89.8 3.4 %shard_map.82 = bf16[1024,512]{1,0:T(8,128)(2,1)} custom-call(bf16[4,4,256,128]{3,2,1,0:T(8,128)(2,1)S(1)} %get-tuple-element.40.last_ref, f32[1024,512]{1,0:T(8,128)S(1)} %copy-done.9, bf16[384,512]{1,0:T(8,128)(2,1)} %collective-permute-done.9.first3_ref, bf16[384,512]{1,0:T(8,128)(2,1)} %collective-permute-done.10.second3_ref, bf16[512,512]{1,0:T(8,128)(2,1)S(1)} %copy-done.2), custom_call_target="tpu_custom_call" | custom-call | flops 6442450944 | tf_op jit(solution)/shard_map/pallas_call | solution.py:245
  93.4 1.2 %collective-permute-done.11 = bf16[64,512]{1,0:T(8,128)(2,1)S(1)} collective-permute-done((bf16[64,512]{1,0:T(8,128)(2,1)S(1)}, bf16[64,512]{1,0:T(8,128)(2,1)S(1)}, u32[]{:S(2)}, u32[]{:S(2)}) %collective-permute-start.11) | collective-permute-done | bytes 65568 | tf_op jit(solution)/shard_map/ppermute | solution.py:272
  94.6 4.1 %collective-permute-start.12 = (bf16[128,512]{1,0:T(8,128)(2,1)S(1)}, bf16[128,512]{1,0:T(8,128)(2,1)S(1)}, u32[]{:S(2)}, u32[]{:S(2)}) collective-permute-start(bf16[128,512]{1,0:T(8,128)(2,1)S(1)} %bitcast.18), channel_id=1, source_target_pairs={{0,4},{4,0},{8,12},{12,8},{1,5},{5,1},{9,13},{13,9},{2,6},{6,2},{1... | collective-permute-start | bytes 393224 | tf_op jit(solution)/shard_map/ppermute | solution.py:272
  98.8 1.5 %collective-permute-start.13 = (bf16[128,512]{1,0:T(8,128)(2,1)S(1)}, bf16[128,512]{1,0:T(8,128)(2,1)S(1)}, u32[]{:S(2)}, u32[]{:S(2)}) collective-permute-start(bf16[128,512]{1,0:T(8,128)(2,1)S(1)} %bitcast.19), channel_id=1, source_target_pairs={{0,8},{4,12},{8,0},{12,4},{1,9},{5,13},{9,1},{13,5},{2,10},{6,14},... | collective-permute-start | bytes 393224 | tf_op jit(solution)/shard_map/ppermute | solution.py:272
  100.3 2.4 %collective-permute-done.12.refs_1_ = bf16[128,512]{1,0:T(8,128)(2,1)S(1)} collective-permute-done((bf16[128,512]{1,0:T(8,128)(2,1)S(1)}, bf16[128,512]{1,0:T(8,128)(2,1)S(1)}, u32[]{:S(2)}, u32[]{:S(2)}) %collective-permute-start.12) | collective-permute-done | bytes 131104 | tf_op jit(solution)/shard_map/ppermute | solution.py:272
  102.7 4.2 %collective-permute-done.13.refs_2_ = bf16[128,512]{1,0:T(8,128)(2,1)S(1)} collective-permute-done((bf16[128,512]{1,0:T(8,128)(2,1)S(1)}, bf16[128,512]{1,0:T(8,128)(2,1)S(1)}, u32[]{:S(2)}, u32[]{:S(2)}) %collective-permute-start.13) | collective-permute-done | bytes 131104 | tf_op jit(solution)/shard_map/ppermute | solution.py:272
  (33 shorter events, 3.9 us)
Async XLA Ops:
  2.1 20.6 %collective-permute-start = (bf16[640,512]{1,0:T(8,128)(2,1)S(1)}, bf16[640,512]{1,0:T(8,128)(2,1)S(1)}, u32[]{:S(2)}, u32[]{:S(2)}) collective-permute-start(bf16[640,512]{1,0:T(8,128)(2,1)S(1)} %get-tuple-element.28), channel_id=1, source_target_pairs={{0,1},{2,3},{4,5},{6,7},{8,9},{10,11},{12,13},{14,15},{1,0},{3,2},... | collective-permute-start | bytes 1966088 | tf_op jit(solution)/shard_map/ppermute | solution.py:261
  3.8 31.1 %collective-permute-start.1 = (bf16[640,512]{1,0:T(8,128)(2,1)S(1)}, bf16[640,512]{1,0:T(8,128)(2,1)S(1)}, u32[]{:S(2)}, u32[]{:S(2)}) collective-permute-start(bf16[640,512]{1,0:T(8,128)(2,1)S(1)} %get-tuple-element.29), channel_id=1, source_target_pairs={{1,2},{3,4},{5,6},{7,8},{9,10},{11,12},{13,14},{2,1},{4,3},{6,5},{... | collective-permute-start | bytes 1966088 | tf_op jit(solution)/shard_map/ppermute | solution.py:261
  5.7 34.9 %collective-permute-start.2 = (bf16[256,512]{1,0:T(8,128)(2,1)S(1)}, bf16[256,512]{1,0:T(8,128)(2,1)S(1)}, u32[]{:S(2)}, u32[]{:S(2)}) collective-permute-start(bf16[256,512]{1,0:T(8,128)(2,1)S(1)} %get-tuple-element.31), channel_id=1, source_target_pairs={{0,1},{2,3},{4,5},{6,7},{8,9},{10,11},{12,13},{14,15},{1,0},{3,2},... | collective-permute-start | bytes 786440 | tf_op jit(solution)/shard_map/ppermute | solution.py:261
  8.5 37.6 %collective-permute-start.3 = (bf16[256,512]{1,0:T(8,128)(2,1)S(1)}, bf16[256,512]{1,0:T(8,128)(2,1)S(1)}, u32[]{:S(2)}, u32[]{:S(2)}) collective-permute-start(bf16[256,512]{1,0:T(8,128)(2,1)S(1)} %get-tuple-element.32), channel_id=1, source_target_pairs={{1,2},{3,4},{5,6},{7,8},{9,10},{11,12},{13,14},{2,1},{4,3},{6,5},{... | collective-permute-start | bytes 786440 | tf_op jit(solution)/shard_map/ppermute | solution.py:261
  10.4 1.2 %copy-start.4 = (bf16[1,1024,512]{2,1,0:T(8,128)(2,1)S(1)}, bf16[1,1024,512]{2,1,0:T(8,128)(2,1)}, u32[]{:S(2)}) copy-start(bf16[1,1024,512]{2,1,0:T(8,128)(2,1)} %param.5) | copy-start | bytes 3145732
  11.6 2.1 %copy-start.5 = (bf16[1,8,15,128,128]{4,3,2,1,0:T(8,128)(2,1)S(1)}, bf16[1,8,15,128,128]{4,3,2,1,0:T(8,128)(2,1)}, u32[]{:S(2)}) copy-start(bf16[1,8,15,128,128]{4,3,2,1,0:T(8,128)(2,1)} %param.8) | copy-start | bytes 11796484
  13.7 0.7 copy-start.7
  14.4 20.4 %copy-start.2 = (bf16[512,512]{1,0:T(8,128)(2,1)S(1)}, bf16[512,512]{1,0:T(8,128)(2,1)}, u32[]{:S(2)}) copy-start(bf16[512,512]{1,0:T(8,128)(2,1)} %weight_ref.7) | copy-start | bytes 1572868
  14.4 20.4 %copy-start.3 = (bf16[1,1024,512]{2,1,0:T(8,128)(2,1)S(1)}, bf16[1,1024,512]{2,1,0:T(8,128)(2,1)}, u32[]{:S(2)}) copy-start(bf16[1,1024,512]{2,1,0:T(8,128)(2,1)} %param.9) | copy-start | bytes 3145732
  22.7 23.4 %copy-start = (bf16[4,16,256,128]{3,2,1,0:T(8,128)(2,1)}, bf16[4,16,256,128]{3,2,1,0:T(8,128)(2,1)S(1)}, u32[]{:S(2)}) copy-start(bf16[4,16,256,128]{3,2,1,0:T(8,128)(2,1)S(1)} %get-tuple-element.26.band_ref) | copy-start | bytes 12582916
  36.1 26.6 %collective-permute-start.4 = (bf16[512,512]{1,0:T(8,128)(2,1)S(1)}, bf16[512,512]{1,0:T(8,128)(2,1)S(1)}, u32[]{:S(2)}, u32[]{:S(2)}) collective-permute-start(bf16[512,512]{1,0:T(8,128)(2,1)S(1)} %get-tuple-element.30.mid_ref), channel_id=1, source_target_pairs={{0,1},{2,3},{4,5},{6,7},{8,9},{10,11},{12,13},{14,15},{1,0},{3,2},... | collective-permute-start | bytes 1572872 | tf_op jit(solution)/shard_map/ppermute | solution.py:261
  37.5 31.0 %collective-permute-start.5 = (bf16[512,512]{1,0:T(8,128)(2,1)S(1)}, bf16[512,512]{1,0:T(8,128)(2,1)}, u32[]{:S(2)}, u32[]{:S(2)}) collective-permute-start(bf16[512,512]{1,0:T(8,128)(2,1)S(1)} %get-tuple-element.30.mid_ref), channel_id=1, source_target_pairs={{1,2},{3,4},{5,6},{7,8},{9,10},{11,12},{13,14},{2,1},{4,3},{6,5},{... | collective-permute-start | bytes 1572872 | tf_op jit(solution)/shard_map/ppermute | solution.py:261
  47.4 1.7 %copy-start.6 = (bf16[384,512]{1,0:T(8,128)(2,1)}, bf16[384,512]{1,0:T(8,128)(2,1)S(1)}, u32[]{:S(2)}) copy-start(bf16[384,512]{1,0:T(8,128)(2,1)S(1)} %get-tuple-element.42) | copy-start | bytes 1179652
  49.1 22.6 %all-to-all-start = ((bf16[8,64,512]{2,1,0:T(8,128)(2,1)}), bf16[8,64,512]{2,1,0:T(8,128)(2,1)}, u32[]{:S(2)}, u32[]{:S(2)}) async-start(bf16[8,64,512]{2,1,0:T(8,128)(2,1)} %bitcast.24), calls=%async_computation | async-start | bytes 1048576 | tf_op jit(solution)/shard_map/all_to_all | solution.py:349
  55.3 22.1 %collective-permute-start.9 = (bf16[384,512]{1,0:T(8,128)(2,1)}, bf16[384,512]{1,0:T(8,128)(2,1)}, u32[]{:S(2)}, u32[]{:S(2)}) collective-permute-start(bf16[384,512]{1,0:T(8,128)(2,1)} %copy-done.6), channel_id=1, source_target_pairs={{0,1},{2,3},{4,5},{6,7},{8,9},{10,11},{12,13},{14,15},{1,0},{3,2},... | collective-permute-start | bytes 1179656 | tf_op jit(solution)/shard_map/ppermute | solution.py:261
  55.3 32.9 %collective-permute-start.10 = (bf16[384,512]{1,0:T(8,128)(2,1)S(1)}, bf16[384,512]{1,0:T(8,128)(2,1)}, u32[]{:S(2)}, u32[]{:S(2)}) collective-permute-start(bf16[384,512]{1,0:T(8,128)(2,1)S(1)} %get-tuple-element.43), channel_id=1, source_target_pairs={{1,2},{3,4},{5,6},{7,8},{9,10},{11,12},{13,14},{2,1},{4,3},{6,5},{... | collective-permute-start | bytes 1179656 | tf_op jit(solution)/shard_map/ppermute | solution.py:261
  57.7 2.2 %copy-start.1 = (bf16[4,16,256,128]{3,2,1,0:T(8,128)(2,1)S(1)}, bf16[4,16,256,128]{3,2,1,0:T(8,128)(2,1)}, u32[]{:S(2)}) copy-start(bf16[4,16,256,128]{3,2,1,0:T(8,128)(2,1)} %copy-done) | copy-start | bytes 12582916
  70.4 1.4 %copy-start.8 = (f32[1024,512]{1,0:T(8,128)}, f32[1024,512]{1,0:T(8,128)S(1)}, u32[]{:S(2)}) copy-start(f32[1024,512]{1,0:T(8,128)S(1)} %get-tuple-element.41.near_ref) | copy-start | bytes 6291460
  72.8 20.4 %collective-permute-start.6 = (bf16[64,512]{1,0:T(8,128)(2,1)S(1)}, bf16[64,512]{1,0:T(8,128)(2,1)S(1)}, u32[]{:S(2)}, u32[]{:S(2)}) collective-permute-start(bf16[64,512]{1,0:T(8,128)(2,1)S(1)} %reduce_sum.12), channel_id=1, source_target_pairs={{0,1},{1,0},{2,3},{3,2},{4,5},{5,4},{6,7},{7,6},{8,9},{9,8},{10,11... | collective-permute-start | bytes 196616 | tf_op jit(solution)/shard_map/ppermute | solution.py:272
  75.9 17.4 %collective-permute-start.7 = (bf16[64,512]{1,0:T(8,128)(2,1)S(1)}, bf16[64,512]{1,0:T(8,128)(2,1)S(1)}, u32[]{:S(2)}, u32[]{:S(2)}) collective-permute-start(bf16[64,512]{1,0:T(8,128)(2,1)S(1)} %reduce_sum.12), channel_id=1, source_target_pairs={{0,2},{1,3},{2,0},{3,1},{4,6},{5,7},{6,4},{7,5},{8,10},{9,11},{10,... | collective-permute-start | bytes 196616 | tf_op jit(solution)/shard_map/ppermute | solution.py:272
  77.0 16.3 %collective-permute-start.8 = (bf16[64,512]{1,0:T(8,128)(2,1)S(1)}, bf16[64,512]{1,0:T(8,128)(2,1)S(1)}, u32[]{:S(2)}, u32[]{:S(2)}) collective-permute-start(bf16[64,512]{1,0:T(8,128)(2,1)S(1)} %reduce_sum.12), channel_id=1, source_target_pairs={{0,3},{1,2},{2,1},{3,0},{4,7},{5,6},{6,5},{7,4},{8,11},{9,10},{10,... | collective-permute-start | bytes 196616 | tf_op jit(solution)/shard_map/ppermute | solution.py:272
  88.2 1.6 %copy-start.9 = (f32[1024,512]{1,0:T(8,128)S(1)}, f32[1024,512]{1,0:T(8,128)}, u32[]{:S(2)}) copy-start(f32[1024,512]{1,0:T(8,128)} %copy-done.8) | copy-start | bytes 6291460
  93.3 1.3 %collective-permute-start.11 = (bf16[64,512]{1,0:T(8,128)(2,1)S(1)}, bf16[64,512]{1,0:T(8,128)(2,1)S(1)}, u32[]{:S(2)}, u32[]{:S(2)}) collective-permute-start(bf16[64,512]{1,0:T(8,128)(2,1)S(1)} %add_convert_fusion), channel_id=1, source_target_pairs={{0,16},{16,0},{1,17},{17,1},{2,18},{18,2},{3,19},{19,3},{4,20},{20... | collective-permute-start | bytes 196616 | tf_op jit(solution)/shard_map/ppermute | solution.py:272
  94.6 8.0 %collective-permute-start.12 = (bf16[128,512]{1,0:T(8,128)(2,1)S(1)}, bf16[128,512]{1,0:T(8,128)(2,1)S(1)}, u32[]{:S(2)}, u32[]{:S(2)}) collective-permute-start(bf16[128,512]{1,0:T(8,128)(2,1)S(1)} %bitcast.18), channel_id=1, source_target_pairs={{0,4},{4,0},{8,12},{12,8},{1,5},{5,1},{9,13},{13,9},{2,6},{6,2},{1... | collective-permute-start | bytes 393224 | tf_op jit(solution)/shard_map/ppermute | solution.py:272
  98.8 8.1 %collective-permute-start.13 = (bf16[128,512]{1,0:T(8,128)(2,1)S(1)}, bf16[128,512]{1,0:T(8,128)(2,1)S(1)}, u32[]{:S(2)}, u32[]{:S(2)}) collective-permute-start(bf16[128,512]{1,0:T(8,128)(2,1)S(1)} %bitcast.19), channel_id=1, source_target_pairs={{0,8},{4,12},{8,0},{12,4},{1,9},{5,13},{9,1},{13,5},{2,10},{6,14},... | collective-permute-start | bytes 393224 | tf_op jit(solution)/shard_map/ppermute | solution.py:272
  100.3 6.6 %collective-permute-start.14 = (bf16[128,512]{1,0:T(8,128)(2,1)S(1)}, bf16[128,512]{1,0:T(8,128)(2,1)S(1)}, u32[]{:S(2)}, u32[]{:S(2)}) collective-permute-start(bf16[128,512]{1,0:T(8,128)(2,1)S(1)} %bitcast.20), channel_id=1, source_target_pairs={{0,12},{4,8},{8,4},{12,0},{1,13},{5,9},{9,5},{13,1},{2,14},{6,10},... | collective-permute-start | bytes 393224 | tf_op jit(solution)/shard_map/ppermute | solution.py:272

commit v5 on v3

--- a/solution.py
+++ b/solution.py
@@ -149,8 +149,8 @@
     by_parity(body)
 
 
-def outer_kernel(band_ref, near_ref, first5_ref, second5_ref, first2_ref, second2_ref, weight_ref, cot_ref, mid_ref,
-                 mixed_ref, end_ref, first3_ref, second3_ref, all7_ref):
+def outer_kernel(band_ref, near_ref, first5_ref, second5_ref, first2_ref, second2_ref, weight_ref, cot_ref,
+                 mixed_ref, end_ref, first3_ref, second3_ref):
     size = band_ref.shape[3]
     height = PAIR * size
     five, two = (first5_ref, second5_ref), (first2_ref, second2_ref)
@@ -175,33 +175,27 @@
         for out in three:
             out[size : 2 * size, :] = dagg[:size]
         three[right][2 * size :, :] = dagg[size:]
-        all7_ref[: 4 * size, :] = mid_ref[...]
-        all7_ref[4 * size :, :] = second3_ref[...]
 
     by_parity(body)
 
 
-def own_kernel(band_ref, mid_ref, end_ref, near_ref):
+def own_kernel(band_ref, mid_ref, end_ref, mixed_mid_ref, mixed_end_ref, weight_ref, near_ref, activ_ref):
     tiles, _, height, _ = band_ref.shape
     sources = [
         (mine((0, 1)), end_ref.at[:height]),
         (mine((2, 3, 4, 5)), mid_ref),
         (mine((6, 7)), end_ref.at[height:]),
     ]
-    for t in range(tiles):
-        near_ref[pl.ds(t * height, height), :] = banded(band_ref, t, sources)
+    halves = (mixed_end_ref[:height, :], mixed_mid_ref[:height, :], mixed_mid_ref[height:, :], mixed_end_ref[height:, :])
+    for t, mixed in enumerate(halves):
+        at = pl.ds(t * height, height)
+        near_ref[at, :] = banded(band_ref, t, sources)
+        agg = jnp.dot(mixed, weight_ref[...], preferred_element_type=F32)
+        activ_ref[at, :] = (agg * jax.nn.sigmoid(agg)).astype(activ_ref.dtype)
 
 
 def mark_kernel(near_ref, out_ref):
     out_ref[...] = near_ref[: out_ref.shape[0], : out_ref.shape[1]]
-
-
-def activ_kernel(mixed_mid_ref, mixed_end_ref, weight_ref, _, activ_ref):
-    height = mixed_mid_ref.shape[0] // 2
-    halves = (mixed_end_ref[:height, :], mixed_mid_ref[:height, :], mixed_mid_ref[height:, :], mixed_end_ref[height:, :])
-    for t, mixed in enumerate(halves):
-        agg = jnp.dot(mixed, weight_ref[...], preferred_element_type=F32)
-        activ_ref[pl.ds(t * height, height), :] = (agg * jax.nn.sigmoid(agg)).astype(activ_ref.dtype)
 
 
 def add_kernel(left_rows, right_rows, band_ref, near_ref, first_ref, second_ref, out_ref):
@@ -217,14 +211,12 @@
     by_parity(body)
 
 
-def back_kernel(band_ref, near_ref, all7_ref, weight_ref, out_ref, held_ref, sems):
+def back_kernel(band_ref, near_ref, first3_ref, second3_ref, weight_ref, _, out_ref, held_ref, sems):
     tiles, _, height, _ = band_ref.shape
+    three = (first3_ref, second3_ref)
 
     def body(left, right):
-        if left:
-            sources = [(before((2, 3, 4, 5, 1, 6, 7)), all7_ref)]
-        else:
-            sources = [(after((2, 3, 4, 5, 1, 6, 0)), all7_ref)]
+        sources = [(before((1, 6, 7)), three[left]), (after((1, 6, 0)), three[right])]
         copies = []
         for t in range(tiles):
             at = pl.ds(t * height, height)
@@ -352,46 +344,43 @@
     mixed_mid, mid = kernel_call(
         inner_kernel, [band, near, *five, weight, cotangent[0]], [chip(4), chip(4)], product
     )
-    four = swapped(mid, mid, across=False)
-    mixed_end, end, *three, all7 = kernel_call(
-        outer_kernel, [band, near, *five, *two, weight, cotangent[0], mid],
-        [chip(4), chip(4), chip(3), chip(3), chip(7)], product,
-    )
-    three = swapped(*three, across=False)
+    four = swapped(mid, mid)
+    mixed_end, end, *three = kernel_call(
+        outer_kernel, [band, near, *five, *two, weight, cotangent[0]],
+        [chip(4), chip(4), chip(3), chip(3)], product,
+    )
+    three = swapped(*three)
     full = [chip(rows, F32)]
+
+    def mark(*given):
+        return kernel_call(mark_kernel, held(*given), [pltpu.VMEM((8, 128), F32)], LONG * product)[0]
+
     term = term_of(mixed_mid, mid) + term_of(mixed_end, end)
     kept, came = scatter(term, LEVEL[0], F32)
-    near = kernel_call(own_kernel, [band, mid, end], full, LONG * product)[0]
+    near, activ = kernel_call(
+        own_kernel, [band, mid, end, mixed_mid, mixed_end, weight], [*full, plain(rows)], LONG * product
+    )
     came, near = lax.optimization_barrier((came, near))
-    kept, came = scatter(add_all(kept, came), LEVEL[1], BF16)
     near = kernel_call(
         functools.partial(add_kernel, (2, 3, 4, 5), (2, 3, 4, 5)), [band, *held(near), *four], full, LONG * product
     )[0]
-    came, near = lax.optimization_barrier((came, near))
+    kept, came, near = lax.optimization_barrier((kept, came, near))
+    kept, came = scatter(add_all(kept, came), LEVEL[1], BF16)
+    came, early = lax.optimization_barrier((came, mark(near)))
     term = add_all(kept, came).astype(BF16)
     parts = [term, *from_all(lambda d: term, "rep")]
-    mark = kernel_call(mark_kernel, held(near), [pltpu.VMEM((8, 128), F32)], LONG * product)[0]
-    *parts, all7, mark = lax.optimization_barrier((*parts, all7, mark))
-    all7 = lax.ppermute(all7, LINE, swap_pairs(1, True))
+    *parts, left, right = lax.optimization_barrier((*parts, *three))
+    three = [left, right]
+    feat_grad = kernel_call(
+        back_kernel, [band, *held(near), *three, weight, *held(early)], [plain(rows)], LONG * product,
+        out_specs=[anywhere()],
+        scratch_shapes=[pltpu.VMEM((zones, width), BF16), pltpu.SemaphoreType.DMA((tiles,))],
+    )[0]
     term = pairwise(parts).astype(BF16)
     other, = from_all(lambda d: term, LEVEL[0])
-    activ = kernel_call(
-        activ_kernel, [mixed_mid, mixed_end, weight, *held(mark)], [plain(rows)], LONG * product
-    )[0]
-    other, activ = lax.optimization_barrier((other, activ))
     term = jnp.where(lax.axis_index(LEVEL[0]) == 0, jnp.stack([term, other]), jnp.stack([other, term]))
     term = term.reshape(-1, width)
     parts = [term, *from_all(lambda d: term, LEVEL[1])]
-    near = kernel_call(
-        functools.partial(add_kernel, (1, 6, 7), (1, 6, 0)), [band, *held(near), *three], full, LONG * product
-    )[0]
-    parts, near = lax.optimization_barrier((parts, near))
-    feat_grad = kernel_call(
-        back_kernel, [band, *held(near), all7, weight], [plain(rows)], LONG * product,
-        out_specs=[anywhere()],
-        scratch_shapes=[pltpu.VMEM((zones, width), BF16), pltpu.SemaphoreType.DMA((tiles,))],
-    )[0]
-    parts, feat_grad = lax.optimization_barrier((parts, feat_grad))
     weight_grad = kernel_call(
         join_kernel, parts, [jax.ShapeDtypeStruct((width, width), F32)], 0
     )[0]

time: 113 us -> 109 us (0.965)
  waiting for transfers between devices: 29.6 us -> 15.8 us
  starting transfers between devices: 57 us -> 63.3 us
  local copies, waits for them, and re-layouts: 4.11 us -> 7.93 us
    ppermute x11, waiting for transfers between devices: 29.4 us -> 13.9 us  [from_all(): lax.ppermute(parts(d), axis, [(j, partner(j, d, n)) for j in range(n)])]
    ppermute x11, starting transfers between devices: 19.4 us -> 26.4 us  [from_all(): lax.ppermute(parts(d), axis, [(j, partner(j, d, n)) for j in range(n)])]
    unnamed x10 -> x18, local copies, waits for them, and re-layouts: 4.03 us -> 7.81 us
    ppermute x8, waiting for transfers between devices: 0.24 us -> 1.99 us  [swapped(): lax.ppermute(x, LINE, swap_pairs(start, across))]
    pallas_call x11 -> x9, Pallas kernels: 20.2 us -> 19.2 us  [kernel_call(): pl.pallas_call(body, out_shape=outs, in_specs=specs or [whole()] * len(in...]
  transfers between devices with their start and end apart: 20 -> 19, of which waited for: 7 -> 8; matrix products, arithmetic and copies ran while one was open for 1% -> 1% of each run, Pallas kernels for 13% -> 15%
where the time goes in v5:
time: 109 us; the launch traced here: 108 us
  starting transfers between devices  63.3 us (58%)
  Pallas kernels  19.2 us (18%)
  waiting for transfers between devices  15.8 us (14%)
  local copies, waits for them, and re-layouts  7.93 us (7%)
    ppermute x8, starting transfers between devices, swapped(): lax.ppermute(x, LINE, swap_pairs(start, across))  36.8 us
    ppermute x11, starting transfers between devices, from_all(): lax.ppermute(parts(d), axis, [(j, partner(j, d, n)) for j in range(n)])  26.4 us
    pallas_call x9, Pallas kernels, kernel_call(): pl.pallas_call(body, out_shape=outs, in_specs=specs or [whole()] * len(in...  19.2 us
    ppermute x11, waiting for transfers between devices, from_all(): lax.ppermute(parts(d), axis, [(j, partner(j, d, n)) for j in range(n)])  13.9 us
    unnamed x18, local copies, waits for them, and re-layouts  7.81 us
  transfers between devices with their start and end apart: 19, of which 8 were waited for; matrix products, arithmetic and copies ran while one was open for 1% of the time, Pallas kernels for 15%

profile of v5, /device:TPU:0, one launch (start us, length us, event | category | flops | bytes accessed | tf_op | source)
XLA Modules:
  0.0 108.2 jit_solution(6187629741396758276)
XLA Ops:
  0.6 2.3 %shard_map.77 = (bf16[640,512]{1,0:T(8,128)(2,1)}, bf16[640,512]{1,0:T(8,128)(2,1)S(1)}, bf16[256,512]{1,0:T(8,128)(2,1)S(1)}, bf16[256,512]{1,0:T(8,128)(2,1)S(1)}) custom-call(bf16[1024,512]{1,0:T(8,128)(2,1)} %bitcast.15), custom_call_target="tpu_custom_call" | custom-call | tf_op jit(solution)/shard_map/pallas_call | solution.py:236
  2.9 3.1 %collective-permute-start = (bf16[640,512]{1,0:T(8,128)(2,1)}, bf16[640,512]{1,0:T(8,128)(2,1)S(1)}, u32[]{:S(2)}, u32[]{:S(2)}) collective-permute-start(bf16[640,512]{1,0:T(8,128)(2,1)} %get-tuple-element.34), channel_id=1, source_target_pairs={{0,1},{2,3},{4,5},{6,7},{8,9},{10,11},{12,13},{14,15},{1,0},{3,2},... | collective-permute-start | bytes 1966088 | tf_op jit(solution)/shard_map/ppermute | solution.py:255
  6.0 0.7 collective-permute-start.1
  6.7 4.4 %collective-permute-start.2 = (bf16[256,512]{1,0:T(8,128)(2,1)S(1)}, bf16[256,512]{1,0:T(8,128)(2,1)S(1)}, u32[]{:S(2)}, u32[]{:S(2)}) collective-permute-start(bf16[256,512]{1,0:T(8,128)(2,1)S(1)} %get-tuple-element.37), channel_id=1, source_target_pairs={{0,1},{2,3},{4,5},{6,7},{8,9},{10,11},{12,13},{14,15},{1,0},{3,2},... | collective-permute-start | bytes 786440 | tf_op jit(solution)/shard_map/ppermute | solution.py:255
  11.9 1.2 %copy-done.4 = bf16[1,1024,512]{2,1,0:T(8,128)(2,1)S(1)} copy-done((bf16[1,1024,512]{2,1,0:T(8,128)(2,1)S(1)}, bf16[1,1024,512]{2,1,0:T(8,128)(2,1)}, u32[]{:S(2)}) %copy-start.4) | copy-done | bytes 1048600
  13.1 2.1 %copy-done.5 = bf16[1,8,15,128,128]{4,3,2,1,0:T(8,128)(2,1)S(1)} copy-done((bf16[1,8,15,128,128]{4,3,2,1,0:T(8,128)(2,1)S(1)}, bf16[1,8,15,128,128]{4,3,2,1,0:T(8,128)(2,1)}, u32[]{:S(2)}) %copy-start.5) | copy-done | bytes 3932184
  15.2 0.7 copy-done.6
  15.9 7.4 %shard_map.76 = (bf16[4,16,256,128]{3,2,1,0:T(8,128)(2,1)S(1)}, f32[1024,512]{1,0:T(8,128)S(1)}) custom-call(s32[8,15]{1,0:T(8,128)S(1)} %bitcast.22, bf16[8,15,128,128]{3,2,1,0:T(8,128)(2,1)S(1)} %bitcast.21, bf16[1024,512]{1,0:T(8,128)(2,1)S(1)} %bitcast.16), custom_call_target="tpu_custom_call" | custom-call | flops 2147483648 | tf_op jit(solution)/shard_map/pallas_call | solution.py:236
  23.4 1.3 %shard_map.78 = (bf16[512,512]{1,0:T(8,128)(2,1)S(1)}, bf16[512,512]{1,0:T(8,128)(2,1)S(1)}) custom-call(bf16[4,16,256,128]{3,2,1,0:T(8,128)(2,1)S(1)} %get-tuple-element.32.band_ref, f32[1024,512]{1,0:T(8,128)S(1)} %get-tuple-element.33.near_ref, bf16[640,512]{1,0:T(8,128)(2,1)S(1)} %collective-permute-done.first5_ref, ...), custom_call_target="tpu_custom_call" | custom-call | flops 536870912 | tf_op jit(solution)/shard_map/pallas_call | solution.py:236
  24.7 17.4 %collective-permute-start.5 = (bf16[512,512]{1,0:T(8,128)(2,1)S(1)}, bf16[512,512]{1,0:T(8,128)(2,1)S(1)}, u32[]{:S(2)}, u32[]{:S(2)}) collective-permute-start(bf16[512,512]{1,0:T(8,128)(2,1)S(1)} %get-tuple-element.36.mid_ref), channel_id=1, source_target_pairs={{0,1},{2,3},{4,5},{6,7},{8,9},{10,11},{12,13},{14,15},{1,0},{3,2},... | collective-permute-start | bytes 1572872 | tf_op jit(solution)/shard_map/ppermute | solution.py:255
  42.8 1.3 %shard_map.79 = (bf16[512,512]{1,0:T(8,128)(2,1)S(1)}, bf16[512,512]{1,0:T(8,128)(2,1)S(1)}, bf16[384,512]{1,0:T(8,128)(2,1)S(1)}, bf16[384,512]{1,0:T(8,128)(2,1)S(1)}) custom-call(bf16[4,16,256,128]{3,2,1,0:T(8,128)(2,1)S(1)} %get-tuple-element.32.band_ref, f32[1024,512]{1,0:T(8,128)S(1)} %get-tuple-element.33.near_ref, ...), custom_call_target="tpu_custom_call" | custom-call | flops 536870912 | tf_op jit(solution)/shard_map/pallas_call | solution.py:236
  45.2 9.2 %collective-permute-start.13 = (bf16[384,512]{1,0:T(8,128)(2,1)S(1)}, bf16[384,512]{1,0:T(8,128)(2,1)S(1)}, u32[]{:S(2)}, u32[]{:S(2)}) collective-permute-start(bf16[384,512]{1,0:T(8,128)(2,1)S(1)} %get-tuple-element.52), channel_id=1, source_target_pairs={{0,1},{2,3},{4,5},{6,7},{8,9},{10,11},{12,13},{14,15},{1,0},{3,2},... | collective-permute-start | bytes 1179656 | tf_op jit(solution)/shard_map/ppermute | solution.py:255
  55.1 2.8 %shard_map.80 = (f32[1024,512]{1,0:T(8,128)S(1)}, bf16[1024,512]{1,0:T(8,128)(2,1)}) custom-call(bf16[4,16,256,128]{3,2,1,0:T(8,128)(2,1)S(1)} %get-tuple-element.32.band_ref, bf16[512,512]{1,0:T(8,128)(2,1)S(1)} %get-tuple-element.36.mid_ref, bf16[512,512]{1,0:T(8,128)(2,1)S(1)} %get-tuple-element.39.end_ref, ...), custom_call_target="tpu_custom_call" | custom-call | flops 6442450944 | tf_op jit(solution)/shard_map/pallas_call | solution.py:236
  57.9 2.0 %collective-permute-done.5.first_ref = bf16[512,512]{1,0:T(8,128)(2,1)S(1)} collective-permute-done((bf16[512,512]{1,0:T(8,128)(2,1)S(1)}, bf16[512,512]{1,0:T(8,128)(2,1)S(1)}, u32[]{:S(2)}, u32[]{:S(2)}) %collective-permute-start.5) | collective-permute-done | bytes 524320 | tf_op jit(solution)/shard_map/ppermute | solution.py:255
  59.8 0.7 shard_map.81.near_ref
  60.7 13.9 %collective-permute-start.7 = (bf16[64,512]{1,0:T(8,128)(2,1)S(1)}, bf16[64,512]{1,0:T(8,128)(2,1)S(1)}, u32[]{:S(2)}, u32[]{:S(2)}) collective-permute-start(bf16[64,512]{1,0:T(8,128)(2,1)S(1)} %get-tuple-element.65), channel_id=1, source_target_pairs={{0,4},{4,0},{8,12},{12,8},{1,5},{5,1},{9,13},{13,9},{2,6},{6,2},{1... | collective-permute-start | bytes 196616 | tf_op jit(solution)/shard_map/ppermute | solution.py:265
  74.6 1.5 %collective-permute-start.8 = (bf16[64,512]{1,0:T(8,128)(2,1)S(1)}, bf16[64,512]{1,0:T(8,128)(2,1)S(1)}, u32[]{:S(2)}, u32[]{:S(2)}) collective-permute-start(bf16[64,512]{1,0:T(8,128)(2,1)S(1)} %get-tuple-element.64), channel_id=1, source_target_pairs={{0,8},{4,12},{8,0},{12,4},{1,9},{5,13},{9,1},{13,5},{2,10},{6,14},... | collective-permute-start | bytes 196616 | tf_op jit(solution)/shard_map/ppermute | solution.py:265
  76.1 0.9 collective-permute-start.9
  77.3 1.5 %collective-permute-done.8 = bf16[64,512]{1,0:T(8,128)(2,1)S(1)} collective-permute-done((bf16[64,512]{1,0:T(8,128)(2,1)S(1)}, bf16[64,512]{1,0:T(8,128)(2,1)S(1)}, u32[]{:S(2)}, u32[]{:S(2)}) %collective-permute-start.8) | collective-permute-done | bytes 65568 | tf_op jit(solution)/shard_map/ppermute | solution.py:265
  78.9 2.4 %collective-permute-done.9 = bf16[64,512]{1,0:T(8,128)(2,1)S(1)} collective-permute-done((bf16[64,512]{1,0:T(8,128)(2,1)S(1)}, bf16[64,512]{1,0:T(8,128)(2,1)S(1)}, u32[]{:S(2)}, u32[]{:S(2)}) %collective-permute-start.9) | collective-permute-done | bytes 65568 | tf_op jit(solution)/shard_map/ppermute | solution.py:265
  81.3 1.9 %collective-permute-start.10 = (bf16[64,512]{1,0:T(8,128)(2,1)S(1)}, bf16[64,512]{1,0:T(8,128)(2,1)S(1)}, u32[]{:S(2)}, u32[]{:S(2)}) collective-permute-start(bf16[64,512]{1,0:T(8,128)(2,1)S(1)} %add_convert_fusion.1), channel_id=1, source_target_pairs={{0,1},{1,0},{2,3},{3,2},{4,5},{5,4},{6,7},{7,6},{8,9},{9,8},{10,11... | collective-permute-start | bytes 196616 | tf_op jit(solution)/shard_map/ppermute | solution.py:265
  83.2 2.0 %collective-permute-start.11 = (bf16[64,512]{1,0:T(8,128)(2,1)S(1)}, bf16[64,512]{1,0:T(8,128)(2,1)S(1)}, u32[]{:S(2)}, u32[]{:S(2)}) collective-permute-start(bf16[64,512]{1,0:T(8,128)(2,1)S(1)} %add_convert_fusion.1), channel_id=1, source_target_pairs={{0,2},{1,3},{2,0},{3,1},{4,6},{5,7},{6,4},{7,5},{8,10},{9,11},{10,... | collective-permute-start | bytes 196616 | tf_op jit(solution)/shard_map/ppermute | solution.py:265
  85.2 1.4 %collective-permute-start.12 = (bf16[64,512]{1,0:T(8,128)(2,1)S(1)}, bf16[64,512]{1,0:T(8,128)(2,1)S(1)}, u32[]{:S(2)}, u32[]{:S(2)}) collective-permute-start(bf16[64,512]{1,0:T(8,128)(2,1)S(1)} %add_convert_fusion.1), channel_id=1, source_target_pairs={{0,3},{1,2},{2,1},{3,0},{4,7},{5,6},{6,5},{7,4},{8,11},{9,10},{10,... | collective-permute-start | bytes 196616 | tf_op jit(solution)/shard_map/ppermute | solution.py:265
  86.6 2.6 %collective-permute-done.10 = bf16[64,512]{1,0:T(8,128)(2,1)S(1)} collective-permute-done((bf16[64,512]{1,0:T(8,128)(2,1)S(1)}, bf16[64,512]{1,0:T(8,128)(2,1)S(1)}, u32[]{:S(2)}, u32[]{:S(2)}) %collective-permute-start.10) | collective-permute-done | bytes 65568 | tf_op jit(solution)/shard_map/ppermute | solution.py:265
  89.2 5.3 %collective-permute-done.11 = bf16[64,512]{1,0:T(8,128)(2,1)S(1)} collective-permute-done((bf16[64,512]{1,0:T(8,128)(2,1)S(1)}, bf16[64,512]{1,0:T(8,128)(2,1)S(1)}, u32[]{:S(2)}, u32[]{:S(2)}) %collective-permute-start.11) | collective-permute-done | bytes 65568 | tf_op jit(solution)/shard_map/ppermute | solution.py:265
  94.6 1.2 %collective-permute-done.15 = bf16[64,512]{1,0:T(8,128)(2,1)S(1)} collective-permute-done((bf16[64,512]{1,0:T(8,128)(2,1)S(1)}, bf16[64,512]{1,0:T(8,128)(2,1)S(1)}, u32[]{:S(2)}, u32[]{:S(2)}) %collective-permute-start.15) | collective-permute-done | bytes 65568 | tf_op jit(solution)/shard_map/ppermute | solution.py:265
  95.9 3.2 %collective-permute-start.16 = (bf16[128,512]{1,0:T(8,128)(2,1)S(1)}, bf16[128,512]{1,0:T(8,128)(2,1)S(1)}, u32[]{:S(2)}, u32[]{:S(2)}) collective-permute-start(bf16[128,512]{1,0:T(8,128)(2,1)S(1)} %bitcast.17), channel_id=1, source_target_pairs={{0,4},{4,0},{8,12},{12,8},{1,5},{5,1},{9,13},{13,9},{2,6},{6,2},{1... | collective-permute-start | bytes 393224 | tf_op jit(solution)/shard_map/ppermute | solution.py:265
  99.1 1.5 %collective-permute-start.18 = (bf16[128,512]{1,0:T(8,128)(2,1)S(1)}, bf16[128,512]{1,0:T(8,128)(2,1)S(1)}, u32[]{:S(2)}, u32[]{:S(2)}) collective-permute-start(bf16[128,512]{1,0:T(8,128)(2,1)S(1)} %bitcast.19), channel_id=1, source_target_pairs={{0,12},{4,8},{8,4},{12,0},{1,13},{5,9},{9,5},{13,1},{2,14},{6,10},... | collective-permute-start | bytes 393224 | tf_op jit(solution)/shard_map/ppermute | solution.py:265
  100.6 2.2 %copy-done.1 = bf16[4,16,256,128]{3,2,1,0:T(8,128)(2,1)S(1)} copy-done((bf16[4,16,256,128]{3,2,1,0:T(8,128)(2,1)S(1)}, bf16[4,16,256,128]{3,2,1,0:T(8,128)(2,1)}, u32[]{:S(2)}) %copy-start.1) | copy-done | bytes 4194328
  102.8 1.6 %copy-done.8 = f32[1024,512]{1,0:T(8,128)S(1)} copy-done((f32[1024,512]{1,0:T(8,128)S(1)}, f32[1024,512]{1,0:T(8,128)}, u32[]{:S(2)}) %copy-start.8) | copy-done | bytes 2097176
  104.4 2.3 %shard_map.83 = bf16[1024,512]{1,0:T(8,128)(2,1)} custom-call(bf16[4,16,256,128]{3,2,1,0:T(8,128)(2,1)S(1)} %copy-done.1, f32[1024,512]{1,0:T(8,128)S(1)} %copy-done.8, bf16[384,512]{1,0:T(8,128)(2,1)S(1)} %collective-permute-done.13.first3_ref, bf16[384,512]{1,0:T(8,128)(2,1)S(1)} %collective-permute-done.14.second3_ref, bf16[512,512]{1,0:T(8,128)(2,1)S(1)} %copy-done.3, ...), custom_call_target="tpu_custom_call" | custom-call | flops 6442450944 | tf_op jit(solution)/shard_map/pallas_call | solution.py:236
  107.2 1.1 shard_map.84
  (41 shorter events, 4.2 us)
Async XLA Ops:
  2.9 20.4 %collective-permute-start = (bf16[640,512]{1,0:T(8,128)(2,1)}, bf16[640,512]{1,0:T(8,128)(2,1)S(1)}, u32[]{:S(2)}, u32[]{:S(2)}) collective-permute-start(bf16[640,512]{1,0:T(8,128)(2,1)} %get-tuple-element.34), channel_id=1, source_target_pairs={{0,1},{2,3},{4,5},{6,7},{8,9},{10,11},{12,13},{14,15},{1,0},{3,2},... | collective-permute-start | bytes 1966088 | tf_op jit(solution)/shard_map/ppermute | solution.py:255
  6.0 17.3 %collective-permute-start.1 = (bf16[640,512]{1,0:T(8,128)(2,1)S(1)}, bf16[640,512]{1,0:T(8,128)(2,1)S(1)}, u32[]{:S(2)}, u32[]{:S(2)}) collective-permute-start(bf16[640,512]{1,0:T(8,128)(2,1)S(1)} %get-tuple-element.35), channel_id=1, source_target_pairs={{1,2},{3,4},{5,6},{7,8},{9,10},{11,12},{13,14},{2,1},{4,3},{6,5},{... | collective-permute-start | bytes 1966088 | tf_op jit(solution)/shard_map/ppermute | solution.py:255
  6.7 36.0 %collective-permute-start.2 = (bf16[256,512]{1,0:T(8,128)(2,1)S(1)}, bf16[256,512]{1,0:T(8,128)(2,1)S(1)}, u32[]{:S(2)}, u32[]{:S(2)}) collective-permute-start(bf16[256,512]{1,0:T(8,128)(2,1)S(1)} %get-tuple-element.37), channel_id=1, source_target_pairs={{0,1},{2,3},{4,5},{6,7},{8,9},{10,11},{12,13},{14,15},{1,0},{3,2},... | collective-permute-start | bytes 786440 | tf_op jit(solution)/shard_map/ppermute | solution.py:255
  11.2 31.6 %collective-permute-start.3 = (bf16[256,512]{1,0:T(8,128)(2,1)S(1)}, bf16[256,512]{1,0:T(8,128)(2,1)S(1)}, u32[]{:S(2)}, u32[]{:S(2)}) collective-permute-start(bf16[256,512]{1,0:T(8,128)(2,1)S(1)} %get-tuple-element.38), channel_id=1, source_target_pairs={{1,2},{3,4},{5,6},{7,8},{9,10},{11,12},{13,14},{2,1},{4,3},{6,5},{... | collective-permute-start | bytes 786440 | tf_op jit(solution)/shard_map/ppermute | solution.py:255
  11.9 1.2 %copy-start.4 = (bf16[1,1024,512]{2,1,0:T(8,128)(2,1)S(1)}, bf16[1,1024,512]{2,1,0:T(8,128)(2,1)}, u32[]{:S(2)}) copy-start(bf16[1,1024,512]{2,1,0:T(8,128)(2,1)} %param.5) | copy-start | bytes 3145732
  13.1 2.1 %copy-start.5 = (bf16[1,8,15,128,128]{4,3,2,1,0:T(8,128)(2,1)S(1)}, bf16[1,8,15,128,128]{4,3,2,1,0:T(8,128)(2,1)}, u32[]{:S(2)}) copy-start(bf16[1,8,15,128,128]{4,3,2,1,0:T(8,128)(2,1)} %param.8) | copy-start | bytes 11796484
  15.2 0.7 copy-start.6
  15.9 7.4 %copy-start.2 = (bf16[1,1024,512]{2,1,0:T(8,128)(2,1)S(1)}, bf16[1,1024,512]{2,1,0:T(8,128)(2,1)}, u32[]{:S(2)}) copy-start(bf16[1,1024,512]{2,1,0:T(8,128)(2,1)} %param.9) | copy-start | bytes 3145732
  15.9 7.5 %copy-start.3 = (bf16[512,512]{1,0:T(8,128)(2,1)S(1)}, bf16[512,512]{1,0:T(8,128)(2,1)}, u32[]{:S(2)}) copy-start(bf16[512,512]{1,0:T(8,128)(2,1)} %weight_ref.7) | copy-start | bytes 1572868
  23.3 36.5 %copy-start = (bf16[4,16,256,128]{3,2,1,0:T(8,128)(2,1)}, bf16[4,16,256,128]{3,2,1,0:T(8,128)(2,1)S(1)}, u32[]{:S(2)}) copy-start(bf16[4,16,256,128]{3,2,1,0:T(8,128)(2,1)S(1)} %get-tuple-element.32.band_ref) | copy-start | bytes 12582916
  24.7 35.2 %collective-permute-start.5 = (bf16[512,512]{1,0:T(8,128)(2,1)S(1)}, bf16[512,512]{1,0:T(8,128)(2,1)S(1)}, u32[]{:S(2)}, u32[]{:S(2)}) collective-permute-start(bf16[512,512]{1,0:T(8,128)(2,1)S(1)} %get-tuple-element.36.mid_ref), channel_id=1, source_target_pairs={{0,1},{2,3},{4,5},{6,7},{8,9},{10,11},{12,13},{14,15},{1,0},{3,2},... | collective-permute-start | bytes 1572872 | tf_op jit(solution)/shard_map/ppermute | solution.py:255
  42.1 17.8 %collective-permute-start.6 = (bf16[512,512]{1,0:T(8,128)(2,1)S(1)}, bf16[512,512]{1,0:T(8,128)(2,1)S(1)}, u32[]{:S(2)}, u32[]{:S(2)}) collective-permute-start(bf16[512,512]{1,0:T(8,128)(2,1)S(1)} %get-tuple-element.36.mid_ref), channel_id=1, source_target_pairs={{1,2},{3,4},{5,6},{7,8},{9,10},{11,12},{13,14},{2,1},{4,3},{6,5},{... | collective-permute-start | bytes 1572872 | tf_op jit(solution)/shard_map/ppermute | solution.py:255
  45.1 12.8 %collective-permute-start.4 = (f32[256,512]{1,0:T(8,128)S(1)}, f32[256,512]{1,0:T(8,128)S(1)}, u32[]{:S(2)}, u32[]{:S(2)}) collective-permute-start(f32[256,512]{1,0:T(8,128)S(1)} %get-tuple-element.61), channel_id=1, source_target_pairs={{0,16},{16,0},{1,17},{17,1},{2,18},{18,2},{3,19},{19,3},{4,20},{20... | collective-permute-start | bytes 1572872 | tf_op jit(solution)/shard_map/ppermute | solution.py:265
  45.2 41.4 %collective-permute-start.13 = (bf16[384,512]{1,0:T(8,128)(2,1)S(1)}, bf16[384,512]{1,0:T(8,128)(2,1)S(1)}, u32[]{:S(2)}, u32[]{:S(2)}) collective-permute-start(bf16[384,512]{1,0:T(8,128)(2,1)S(1)} %get-tuple-element.52), channel_id=1, source_target_pairs={{0,1},{2,3},{4,5},{6,7},{8,9},{10,11},{12,13},{14,15},{1,0},{3,2},... | collective-permute-start | bytes 1179656 | tf_op jit(solution)/shard_map/ppermute | solution.py:255
  54.4 32.2 %collective-permute-start.14 = (bf16[384,512]{1,0:T(8,128)(2,1)S(1)}, bf16[384,512]{1,0:T(8,128)(2,1)S(1)}, u32[]{:S(2)}, u32[]{:S(2)}) collective-permute-start(bf16[384,512]{1,0:T(8,128)(2,1)S(1)} %get-tuple-element.53), channel_id=1, source_target_pairs={{1,2},{3,4},{5,6},{7,8},{9,10},{11,12},{13,14},{2,1},{4,3},{6,5},{... | collective-permute-start | bytes 1179656 | tf_op jit(solution)/shard_map/ppermute | solution.py:255
  60.6 16.4 %copy-start.7 = (f32[1024,512]{1,0:T(8,128)}, f32[1024,512]{1,0:T(8,128)S(1)}, u32[]{:S(2)}) copy-start(f32[1024,512]{1,0:T(8,128)S(1)} %shard_map.81.near_ref) | copy-start | bytes 6291460
  60.7 16.6 %collective-permute-start.7 = (bf16[64,512]{1,0:T(8,128)(2,1)S(1)}, bf16[64,512]{1,0:T(8,128)(2,1)S(1)}, u32[]{:S(2)}, u32[]{:S(2)}) collective-permute-start(bf16[64,512]{1,0:T(8,128)(2,1)S(1)} %get-tuple-element.65), channel_id=1, source_target_pairs={{0,4},{4,0},{8,12},{12,8},{1,5},{5,1},{9,13},{13,9},{2,6},{6,2},{1... | collective-permute-start | bytes 196616 | tf_op jit(solution)/shard_map/ppermute | solution.py:265
  74.6 4.3 %collective-permute-start.8 = (bf16[64,512]{1,0:T(8,128)(2,1)S(1)}, bf16[64,512]{1,0:T(8,128)(2,1)S(1)}, u32[]{:S(2)}, u32[]{:S(2)}) collective-permute-start(bf16[64,512]{1,0:T(8,128)(2,1)S(1)} %get-tuple-element.64), channel_id=1, source_target_pairs={{0,8},{4,12},{8,0},{12,4},{1,9},{5,13},{9,1},{13,5},{2,10},{6,14},... | collective-permute-start | bytes 196616 | tf_op jit(solution)/shard_map/ppermute | solution.py:265
  76.1 5.2 %collective-permute-start.9 = (bf16[64,512]{1,0:T(8,128)(2,1)S(1)}, bf16[64,512]{1,0:T(8,128)(2,1)S(1)}, u32[]{:S(2)}, u32[]{:S(2)}) collective-permute-start(bf16[64,512]{1,0:T(8,128)(2,1)S(1)} %get-tuple-element.63), channel_id=1, source_target_pairs={{0,12},{4,8},{8,4},{12,0},{1,13},{5,9},{9,5},{13,1},{2,14},{6,10},... | collective-permute-start | bytes 196616 | tf_op jit(solution)/shard_map/ppermute | solution.py:265
  81.3 7.8 %collective-permute-start.10 = (bf16[64,512]{1,0:T(8,128)(2,1)S(1)}, bf16[64,512]{1,0:T(8,128)(2,1)S(1)}, u32[]{:S(2)}, u32[]{:S(2)}) collective-permute-start(bf16[64,512]{1,0:T(8,128)(2,1)S(1)} %add_convert_fusion.1), channel_id=1, source_target_pairs={{0,1},{1,0},{2,3},{3,2},{4,5},{5,4},{6,7},{7,6},{8,9},{9,8},{10,11... | collective-permute-start | bytes 196616 | tf_op jit(solution)/shard_map/ppermute | solution.py:265
  83.2 11.3 %collective-permute-start.11 = (bf16[64,512]{1,0:T(8,128)(2,1)S(1)}, bf16[64,512]{1,0:T(8,128)(2,1)S(1)}, u32[]{:S(2)}, u32[]{:S(2)}) collective-permute-start(bf16[64,512]{1,0:T(8,128)(2,1)S(1)} %add_convert_fusion.1), channel_id=1, source_target_pairs={{0,2},{1,3},{2,0},{3,1},{4,6},{5,7},{6,4},{7,5},{8,10},{9,11},{10,... | collective-permute-start | bytes 196616 | tf_op jit(solution)/shard_map/ppermute | solution.py:265
  85.2 9.3 %collective-permute-start.12 = (bf16[64,512]{1,0:T(8,128)(2,1)S(1)}, bf16[64,512]{1,0:T(8,128)(2,1)S(1)}, u32[]{:S(2)}, u32[]{:S(2)}) collective-permute-start(bf16[64,512]{1,0:T(8,128)(2,1)S(1)} %add_convert_fusion.1), channel_id=1, source_target_pairs={{0,3},{1,2},{2,1},{3,0},{4,7},{5,6},{6,5},{7,4},{8,11},{9,10},{10,... | collective-permute-start | bytes 196616 | tf_op jit(solution)/shard_map/ppermute | solution.py:265
  94.5 1.3 %collective-permute-start.15 = (bf16[64,512]{1,0:T(8,128)(2,1)S(1)}, bf16[64,512]{1,0:T(8,128)(2,1)S(1)}, u32[]{:S(2)}, u32[]{:S(2)}) collective-permute-start(bf16[64,512]{1,0:T(8,128)(2,1)S(1)} %add_convert_fusion), channel_id=1, source_target_pairs={{0,16},{16,0},{1,17},{17,1},{2,18},{18,2},{3,19},{19,3},{4,20},{20... | collective-permute-start | bytes 196616 | tf_op jit(solution)/shard_map/ppermute | solution.py:265
  95.9 10.9 %collective-permute-start.16 = (bf16[128,512]{1,0:T(8,128)(2,1)S(1)}, bf16[128,512]{1,0:T(8,128)(2,1)S(1)}, u32[]{:S(2)}, u32[]{:S(2)}) collective-permute-start(bf16[128,512]{1,0:T(8,128)(2,1)S(1)} %bitcast.17), channel_id=1, source_target_pairs={{0,4},{4,0},{8,12},{12,8},{1,5},{5,1},{9,13},{13,9},{2,6},{6,2},{1... | collective-permute-start | bytes 393224 | tf_op jit(solution)/shard_map/ppermute | solution.py:265
  99.1 8.1 %collective-permute-start.17 = (bf16[128,512]{1,0:T(8,128)(2,1)S(1)}, bf16[128,512]{1,0:T(8,128)(2,1)S(1)}, u32[]{:S(2)}, u32[]{:S(2)}) collective-permute-start(bf16[128,512]{1,0:T(8,128)(2,1)S(1)} %bitcast.18), channel_id=1, source_target_pairs={{0,8},{4,12},{8,0},{12,4},{1,9},{5,13},{9,1},{13,5},{2,10},{6,14},... | collective-permute-start | bytes 393224 | tf_op jit(solution)/shard_map/ppermute | solution.py:265
  99.1 8.0 %collective-permute-start.18 = (bf16[128,512]{1,0:T(8,128)(2,1)S(1)}, bf16[128,512]{1,0:T(8,128)(2,1)S(1)}, u32[]{:S(2)}, u32[]{:S(2)}) collective-permute-start(bf16[128,512]{1,0:T(8,128)(2,1)S(1)} %bitcast.19), channel_id=1, source_target_pairs={{0,12},{4,8},{8,4},{12,0},{1,13},{5,9},{9,5},{13,1},{2,14},{6,10},... | collective-permute-start | bytes 393224 | tf_op jit(solution)/shard_map/ppermute | solution.py:265
  100.6 2.2 %copy-start.1 = (bf16[4,16,256,128]{3,2,1,0:T(8,128)(2,1)S(1)}, bf16[4,16,256,128]{3,2,1,0:T(8,128)(2,1)}, u32[]{:S(2)}) copy-start(bf16[4,16,256,128]{3,2,1,0:T(8,128)(2,1)} %copy-done) | copy-start | bytes 12582916
  102.8 1.6 %copy-start.8 = (f32[1024,512]{1,0:T(8,128)S(1)}, f32[1024,512]{1,0:T(8,128)}, u32[]{:S(2)}) copy-start(f32[1024,512]{1,0:T(8,128)} %copy-done.7) | copy-start | bytes 6291460

commit v6 on v5

--- a/solution.py
+++ b/solution.py
@@ -198,9 +198,19 @@
     out_ref[...] = near_ref[: out_ref.shape[0], : out_ref.shape[1]]
 
 
-def add_kernel(left_rows, right_rows, band_ref, near_ref, first_ref, second_ref, out_ref):
-    tiles, _, height, _ = band_ref.shape
+LAST = before((1, 6, 7)) + after((1, 6, 0))
+
+
+def last_of(t, span):
+    return [i for i, w in enumerate(LAST) if 0 <= w - PAIR * t < span]
+
+
+def add_kernel(left_rows, right_rows, band_ref, near_ref, first_ref, second_ref, out_ref, last_ref):
+    tiles, span, height, _ = band_ref.shape
     came = (first_ref, second_ref)
+    for t in range(tiles):
+        for i, which in enumerate(last_of(t, span)):
+            last_ref[t, i] = band_ref[t, LAST[which] - PAIR * t]
 
     def body(left, right):
         sources = [(before(left_rows), came[left]), (after(right_rows), came[right])]
@@ -211,16 +221,22 @@
     by_parity(body)
 
 
-def back_kernel(band_ref, near_ref, first3_ref, second3_ref, weight_ref, _, out_ref, held_ref, sems):
-    tiles, _, height, _ = band_ref.shape
+def back_kernel(last_ref, near_ref, first3_ref, second3_ref, weight_ref, _, out_ref, held_ref, sems):
+    tiles, _, height, size = last_ref.shape
     three = (first3_ref, second3_ref)
 
     def body(left, right):
-        sources = [(before((1, 6, 7)), three[left]), (after((1, 6, 0)), three[right])]
+        sources = [(side, i * size) for side in (left, right) for i in range(3)]
         copies = []
         for t in range(tiles):
             at = pl.ds(t * height, height)
-            dproj = near_ref[at, :] + banded(band_ref, t, sources)
+            met = last_of(t, 2 * REACH + PAIR)
+            blocks = [three[side][first : first + size, :] for side, first in (sources[i] for i in met)]
+            dproj = near_ref[at, :] + jnp.dot(
+                jnp.concatenate([last_ref[t, i] for i in range(len(met))], axis=1),
+                jnp.concatenate(blocks, axis=0),
+                preferred_element_type=F32,
+            )
             held_ref[at, :] = lax.dot_general(
                 dproj.astype(BF16), weight_ref[...], (((1,), (1,)), ((), ())), preferred_element_type=F32
             ).astype(BF16)
@@ -361,9 +377,10 @@
         own_kernel, [band, mid, end, mixed_mid, mixed_end, weight], [*full, plain(rows)], LONG * product
     )
     came, near = lax.optimization_barrier((came, near))
-    near = kernel_call(
-        functools.partial(add_kernel, (2, 3, 4, 5), (2, 3, 4, 5)), [band, *held(near), *four], full, LONG * product
-    )[0]
+    near, last = kernel_call(
+        functools.partial(add_kernel, (2, 3, 4, 5), (2, 3, 4, 5)), [band, *held(near), *four],
+        [*full, pltpu.VMEM((tiles, len(last_of(0, span)), height, size), BF16)], LONG * product,
+    )
     kept, came, near = lax.optimization_barrier((kept, came, near))
     kept, came = scatter(add_all(kept, came), LEVEL[1], BF16)
     came, early = lax.optimization_barrier((came, mark(near)))
@@ -372,7 +389,7 @@
     *parts, left, right = lax.optimization_barrier((*parts, *three))
     three = [left, right]
     feat_grad = kernel_call(
-        back_kernel, [band, *held(near), *three, weight, *held(early)], [plain(rows)], LONG * product,
+        back_kernel, [*held(last, near), *three, weight, *held(early)], [plain(rows)], LONG * product,
         out_specs=[anywhere()],
         scratch_shapes=[pltpu.VMEM((zones, width), BF16), pltpu.SemaphoreType.DMA((tiles,))],
     )[0]

time: 109 us -> 109 us (level)
  local copies, waits for them, and re-layouts: 7.93 us -> 5.75 us
  waiting for transfers between devices: 15.8 us -> 17.9 us
  Pallas kernels: 19.2 us -> 20.3 us
    unnamed x18 -> x14, local copies, waits for them, and re-layouts: 7.81 us -> 5.62 us
    ppermute x11, waiting for transfers between devices: 13.9 us -> 16 us  [from_all(): lax.ppermute(parts(d), axis, [(j, partner(j, d, n)) for j in range(n)])]
    pallas_call x9, Pallas kernels: 19.2 us -> 20.3 us  [kernel_call(): pl.pallas_call(body, out_shape=outs, in_specs=specs or [whole()] * len(in...]
  transfers between devices with their start and end apart: 19 -> 19, of which waited for: 8 -> 8; matrix products, arithmetic and copies ran while one was open for 1% -> 1% of each run, Pallas kernels for 15% -> 16%
where the time goes in v6:
time: 109 us; the launch traced here: 108 us
  starting transfers between devices  62.3 us (57%)
  Pallas kernels  20.3 us (19%)
  waiting for transfers between devices  17.9 us (16%)
  local copies, waits for them, and re-layouts  5.75 us (5%)
    ppermute x8, starting transfers between devices, swapped(): lax.ppermute(x, LINE, swap_pairs(start, across))  35.8 us
    ppermute x11, starting transfers between devices, from_all(): lax.ppermute(parts(d), axis, [(j, partner(j, d, n)) for j in range(n)])  26.5 us
    pallas_call x9, Pallas kernels, kernel_call(): pl.pallas_call(body, out_shape=outs, in_specs=specs or [whole()] * len(in...  20.3 us
    ppermute x11, waiting for transfers between devices, from_all(): lax.ppermute(parts(d), axis, [(j, partner(j, d, n)) for j in range(n)])  16 us
    unnamed x14, local copies, waits for them, and re-layouts  5.62 us
  transfers between devices with their start and end apart: 19, of which 8 were waited for; matrix products, arithmetic and copies ran while one was open for 1% of the time, Pallas kernels for 16%

profile of v6, /device:TPU:0, one launch (start us, length us, event | category | flops | bytes accessed | tf_op | source)
XLA Modules:
  0.0 108.3 jit_solution(12855659356441766039)
XLA Ops:
  0.6 2.3 %shard_map.77 = (bf16[640,512]{1,0:T(8,128)(2,1)}, bf16[640,512]{1,0:T(8,128)(2,1)S(1)}, bf16[256,512]{1,0:T(8,128)(2,1)S(1)}, bf16[256,512]{1,0:T(8,128)(2,1)S(1)}) custom-call(bf16[1024,512]{1,0:T(8,128)(2,1)} %bitcast.15), custom_call_target="tpu_custom_call" | custom-call | tf_op jit(solution)/shard_map/pallas_call | solution.py:252
  2.9 3.1 %collective-permute-start = (bf16[640,512]{1,0:T(8,128)(2,1)}, bf16[640,512]{1,0:T(8,128)(2,1)S(1)}, u32[]{:S(2)}, u32[]{:S(2)}) collective-permute-start(bf16[640,512]{1,0:T(8,128)(2,1)} %get-tuple-element.36), channel_id=1, source_target_pairs={{0,1},{2,3},{4,5},{6,7},{8,9},{10,11},{12,13},{14,15},{1,0},{3,2},... | collective-permute-start | bytes 1966088 | tf_op jit(solution)/shard_map/ppermute | solution.py:271
  6.0 0.7 collective-permute-start.1
  6.7 4.4 %collective-permute-start.2 = (bf16[256,512]{1,0:T(8,128)(2,1)S(1)}, bf16[256,512]{1,0:T(8,128)(2,1)S(1)}, u32[]{:S(2)}, u32[]{:S(2)}) collective-permute-start(bf16[256,512]{1,0:T(8,128)(2,1)S(1)} %get-tuple-element.39), channel_id=1, source_target_pairs={{0,1},{2,3},{4,5},{6,7},{8,9},{10,11},{12,13},{14,15},{1,0},{3,2},... | collective-permute-start | bytes 786440 | tf_op jit(solution)/shard_map/ppermute | solution.py:271
  11.9 1.2 %copy-done.2 = bf16[1,1024,512]{2,1,0:T(8,128)(2,1)S(1)} copy-done((bf16[1,1024,512]{2,1,0:T(8,128)(2,1)S(1)}, bf16[1,1024,512]{2,1,0:T(8,128)(2,1)}, u32[]{:S(2)}) %copy-start.2) | copy-done | bytes 1048600
  13.1 2.1 %copy-done.3 = bf16[1,8,15,128,128]{4,3,2,1,0:T(8,128)(2,1)S(1)} copy-done((bf16[1,8,15,128,128]{4,3,2,1,0:T(8,128)(2,1)S(1)}, bf16[1,8,15,128,128]{4,3,2,1,0:T(8,128)(2,1)}, u32[]{:S(2)}) %copy-start.3) | copy-done | bytes 3932184
  15.2 0.7 copy-done.4
  15.9 8.5 %shard_map.76 = (bf16[4,16,256,128]{3,2,1,0:T(8,128)(2,1)S(1)}, f32[1024,512]{1,0:T(8,128)S(1)}) custom-call(s32[8,15]{1,0:T(8,128)S(1)} %bitcast.22, bf16[8,15,128,128]{3,2,1,0:T(8,128)(2,1)S(1)} %bitcast.21, bf16[1024,512]{1,0:T(8,128)(2,1)S(1)} %bitcast.16), custom_call_target="tpu_custom_call" | custom-call | flops 2147483648 | tf_op jit(solution)/shard_map/pallas_call | solution.py:252
  24.4 1.3 %shard_map.78 = (bf16[512,512]{1,0:T(8,128)(2,1)S(1)}, bf16[512,512]{1,0:T(8,128)(2,1)S(1)}) custom-call(bf16[4,16,256,128]{3,2,1,0:T(8,128)(2,1)S(1)} %get-tuple-element.34.band_ref, f32[1024,512]{1,0:T(8,128)S(1)} %get-tuple-element.35.near_ref, bf16[640,512]{1,0:T(8,128)(2,1)S(1)} %collective-permute-done.first5_ref, ...), custom_call_target="tpu_custom_call" | custom-call | flops 536870912 | tf_op jit(solution)/shard_map/pallas_call | solution.py:252
  25.7 16.4 %collective-permute-start.5 = (bf16[512,512]{1,0:T(8,128)(2,1)S(1)}, bf16[512,512]{1,0:T(8,128)(2,1)S(1)}, u32[]{:S(2)}, u32[]{:S(2)}) collective-permute-start(bf16[512,512]{1,0:T(8,128)(2,1)S(1)} %get-tuple-element.38.mid_ref), channel_id=1, source_target_pairs={{0,1},{2,3},{4,5},{6,7},{8,9},{10,11},{12,13},{14,15},{1,0},{3,2},... | collective-permute-start | bytes 1572872 | tf_op jit(solution)/shard_map/ppermute | solution.py:271
  42.8 1.3 %shard_map.79 = (bf16[512,512]{1,0:T(8,128)(2,1)S(1)}, bf16[512,512]{1,0:T(8,128)(2,1)S(1)}, bf16[384,512]{1,0:T(8,128)(2,1)S(1)}, bf16[384,512]{1,0:T(8,128)(2,1)S(1)}) custom-call(bf16[4,16,256,128]{3,2,1,0:T(8,128)(2,1)S(1)} %get-tuple-element.34.band_ref, f32[1024,512]{1,0:T(8,128)S(1)} %get-tuple-element.35.near_ref, ...), custom_call_target="tpu_custom_call" | custom-call | flops 536870912 | tf_op jit(solution)/shard_map/pallas_call | solution.py:252
  45.2 9.2 %collective-permute-start.13 = (bf16[384,512]{1,0:T(8,128)(2,1)S(1)}, bf16[384,512]{1,0:T(8,128)(2,1)S(1)}, u32[]{:S(2)}, u32[]{:S(2)}) collective-permute-start(bf16[384,512]{1,0:T(8,128)(2,1)S(1)} %get-tuple-element.56), channel_id=1, source_target_pairs={{0,1},{2,3},{4,5},{6,7},{8,9},{10,11},{12,13},{14,15},{1,0},{3,2},... | collective-permute-start | bytes 1179656 | tf_op jit(solution)/shard_map/ppermute | solution.py:271
  55.1 2.8 %shard_map.80 = (f32[1024,512]{1,0:T(8,128)S(1)}, bf16[1024,512]{1,0:T(8,128)(2,1)}) custom-call(bf16[4,16,256,128]{3,2,1,0:T(8,128)(2,1)S(1)} %get-tuple-element.34.band_ref, bf16[512,512]{1,0:T(8,128)(2,1)S(1)} %get-tuple-element.38.mid_ref, bf16[512,512]{1,0:T(8,128)(2,1)S(1)} %get-tuple-element.41.end_ref, ...), custom_call_target="tpu_custom_call" | custom-call | flops 6442450944 | tf_op jit(solution)/shard_map/pallas_call | solution.py:252
  57.9 1.9 %collective-permute-done.5.first_ref = bf16[512,512]{1,0:T(8,128)(2,1)S(1)} collective-permute-done((bf16[512,512]{1,0:T(8,128)(2,1)S(1)}, bf16[512,512]{1,0:T(8,128)(2,1)S(1)}, u32[]{:S(2)}, u32[]{:S(2)}) %collective-permute-start.5) | collective-permute-done | bytes 524320 | tf_op jit(solution)/shard_map/ppermute | solution.py:271
  59.8 0.8 shard_map.81
  60.8 13.9 %collective-permute-start.7 = (bf16[64,512]{1,0:T(8,128)(2,1)S(1)}, bf16[64,512]{1,0:T(8,128)(2,1)S(1)}, u32[]{:S(2)}, u32[]{:S(2)}) collective-permute-start(bf16[64,512]{1,0:T(8,128)(2,1)S(1)} %get-tuple-element.69), channel_id=1, source_target_pairs={{0,4},{4,0},{8,12},{12,8},{1,5},{5,1},{9,13},{13,9},{2,6},{6,2},{1... | collective-permute-start | bytes 196616 | tf_op jit(solution)/shard_map/ppermute | solution.py:281
  74.7 1.5 %collective-permute-start.8 = (bf16[64,512]{1,0:T(8,128)(2,1)S(1)}, bf16[64,512]{1,0:T(8,128)(2,1)S(1)}, u32[]{:S(2)}, u32[]{:S(2)}) collective-permute-start(bf16[64,512]{1,0:T(8,128)(2,1)S(1)} %get-tuple-element.68), channel_id=1, source_target_pairs={{0,8},{4,12},{8,0},{12,4},{1,9},{5,13},{9,1},{13,5},{2,10},{6,14},... | collective-permute-start | bytes 196616 | tf_op jit(solution)/shard_map/ppermute | solution.py:281
  76.2 0.9 collective-permute-start.9
  77.4 1.5 %collective-permute-done.8 = bf16[64,512]{1,0:T(8,128)(2,1)S(1)} collective-permute-done((bf16[64,512]{1,0:T(8,128)(2,1)S(1)}, bf16[64,512]{1,0:T(8,128)(2,1)S(1)}, u32[]{:S(2)}, u32[]{:S(2)}) %collective-permute-start.8) | collective-permute-done | bytes 65568 | tf_op jit(solution)/shard_map/ppermute | solution.py:281
  78.9 2.4 %collective-permute-done.9 = bf16[64,512]{1,0:T(8,128)(2,1)S(1)} collective-permute-done((bf16[64,512]{1,0:T(8,128)(2,1)S(1)}, bf16[64,512]{1,0:T(8,128)(2,1)S(1)}, u32[]{:S(2)}, u32[]{:S(2)}) %collective-permute-start.9) | collective-permute-done | bytes 65568 | tf_op jit(solution)/shard_map/ppermute | solution.py:281
  81.4 1.9 %collective-permute-start.10 = (bf16[64,512]{1,0:T(8,128)(2,1)S(1)}, bf16[64,512]{1,0:T(8,128)(2,1)S(1)}, u32[]{:S(2)}, u32[]{:S(2)}) collective-permute-start(bf16[64,512]{1,0:T(8,128)(2,1)S(1)} %add_convert_fusion.1), channel_id=1, source_target_pairs={{0,1},{1,0},{2,3},{3,2},{4,5},{5,4},{6,7},{7,6},{8,9},{9,8},{10,11... | collective-permute-start | bytes 196616 | tf_op jit(solution)/shard_map/ppermute | solution.py:281
  83.3 2.0 %collective-permute-start.11 = (bf16[64,512]{1,0:T(8,128)(2,1)S(1)}, bf16[64,512]{1,0:T(8,128)(2,1)S(1)}, u32[]{:S(2)}, u32[]{:S(2)}) collective-permute-start(bf16[64,512]{1,0:T(8,128)(2,1)S(1)} %add_convert_fusion.1), channel_id=1, source_target_pairs={{0,2},{1,3},{2,0},{3,1},{4,6},{5,7},{6,4},{7,5},{8,10},{9,11},{10,... | collective-permute-start | bytes 196616 | tf_op jit(solution)/shard_map/ppermute | solution.py:281
  85.3 1.4 %collective-permute-start.12 = (bf16[64,512]{1,0:T(8,128)(2,1)S(1)}, bf16[64,512]{1,0:T(8,128)(2,1)S(1)}, u32[]{:S(2)}, u32[]{:S(2)}) collective-permute-start(bf16[64,512]{1,0:T(8,128)(2,1)S(1)} %add_convert_fusion.1), channel_id=1, source_target_pairs={{0,3},{1,2},{2,1},{3,0},{4,7},{5,6},{6,5},{7,4},{8,11},{9,10},{10,... | collective-permute-start | bytes 196616 | tf_op jit(solution)/shard_map/ppermute | solution.py:281
  86.7 2.5 %collective-permute-done.10 = bf16[64,512]{1,0:T(8,128)(2,1)S(1)} collective-permute-done((bf16[64,512]{1,0:T(8,128)(2,1)S(1)}, bf16[64,512]{1,0:T(8,128)(2,1)S(1)}, u32[]{:S(2)}, u32[]{:S(2)}) %collective-permute-start.10) | collective-permute-done | bytes 65568 | tf_op jit(solution)/shard_map/ppermute | solution.py:281
  89.2 5.3 %collective-permute-done.11 = bf16[64,512]{1,0:T(8,128)(2,1)S(1)} collective-permute-done((bf16[64,512]{1,0:T(8,128)(2,1)S(1)}, bf16[64,512]{1,0:T(8,128)(2,1)S(1)}, u32[]{:S(2)}, u32[]{:S(2)}) %collective-permute-start.11) | collective-permute-done | bytes 65568 | tf_op jit(solution)/shard_map/ppermute | solution.py:281
  94.6 1.2 %collective-permute-done.15 = bf16[64,512]{1,0:T(8,128)(2,1)S(1)} collective-permute-done((bf16[64,512]{1,0:T(8,128)(2,1)S(1)}, bf16[64,512]{1,0:T(8,128)(2,1)S(1)}, u32[]{:S(2)}, u32[]{:S(2)}) %collective-permute-start.15) | collective-permute-done | bytes 65568 | tf_op jit(solution)/shard_map/ppermute | solution.py:281
  95.9 3.3 %collective-permute-start.16 = (bf16[128,512]{1,0:T(8,128)(2,1)S(1)}, bf16[128,512]{1,0:T(8,128)(2,1)S(1)}, u32[]{:S(2)}, u32[]{:S(2)}) collective-permute-start(bf16[128,512]{1,0:T(8,128)(2,1)S(1)} %bitcast.17), channel_id=1, source_target_pairs={{0,4},{4,0},{8,12},{12,8},{1,5},{5,1},{9,13},{13,9},{2,6},{6,2},{1... | collective-permute-start | bytes 393224 | tf_op jit(solution)/shard_map/ppermute | solution.py:281
  99.2 1.5 %collective-permute-start.18 = (bf16[128,512]{1,0:T(8,128)(2,1)S(1)}, bf16[128,512]{1,0:T(8,128)(2,1)S(1)}, u32[]{:S(2)}, u32[]{:S(2)}) collective-permute-start(bf16[128,512]{1,0:T(8,128)(2,1)S(1)} %bitcast.19), channel_id=1, source_target_pairs={{0,12},{4,8},{8,4},{12,0},{1,13},{5,9},{9,5},{13,1},{2,14},{6,10},... | collective-permute-start | bytes 393224 | tf_op jit(solution)/shard_map/ppermute | solution.py:281
  100.7 1.6 %copy-done.6 = f32[1024,512]{1,0:T(8,128)S(1)} copy-done((f32[1024,512]{1,0:T(8,128)S(1)}, f32[1024,512]{1,0:T(8,128)}, u32[]{:S(2)}) %copy-start.6) | copy-done | bytes 2097176
  102.3 2.3 %shard_map.83 = bf16[1024,512]{1,0:T(8,128)(2,1)} custom-call(bf16[4,4,256,128]{3,2,1,0:T(8,128)(2,1)S(1)} %get-tuple-element.47.last_ref, f32[1024,512]{1,0:T(8,128)S(1)} %copy-done.6, bf16[384,512]{1,0:T(8,128)(2,1)S(1)} %collective-permute-done.13.first3_ref, bf16[384,512]{1,0:T(8,128)(2,1)S(1)} %collective-permute-done.14.second3_ref, ...), custom_call_target="tpu_custom_call" | custom-call | flops 6442450944 | tf_op jit(solution)/shard_map/pallas_call | solution.py:252
  104.6 2.6 %collective-permute-done.17.refs_2_ = bf16[128,512]{1,0:T(8,128)(2,1)S(1)} collective-permute-done((bf16[128,512]{1,0:T(8,128)(2,1)S(1)}, bf16[128,512]{1,0:T(8,128)(2,1)S(1)}, u32[]{:S(2)}, u32[]{:S(2)}) %collective-permute-start.17) | collective-permute-done | bytes 131104 | tf_op jit(solution)/shard_map/ppermute | solution.py:281
  107.2 1.1 shard_map.84
  (37 shorter events, 3.8 us)
Async XLA Ops:
  2.9 21.4 %collective-permute-start = (bf16[640,512]{1,0:T(8,128)(2,1)}, bf16[640,512]{1,0:T(8,128)(2,1)S(1)}, u32[]{:S(2)}, u32[]{:S(2)}) collective-permute-start(bf16[640,512]{1,0:T(8,128)(2,1)} %get-tuple-element.36), channel_id=1, source_target_pairs={{0,1},{2,3},{4,5},{6,7},{8,9},{10,11},{12,13},{14,15},{1,0},{3,2},... | collective-permute-start | bytes 1966088 | tf_op jit(solution)/shard_map/ppermute | solution.py:271
  6.0 18.3 %collective-permute-start.1 = (bf16[640,512]{1,0:T(8,128)(2,1)S(1)}, bf16[640,512]{1,0:T(8,128)(2,1)S(1)}, u32[]{:S(2)}, u32[]{:S(2)}) collective-permute-start(bf16[640,512]{1,0:T(8,128)(2,1)S(1)} %get-tuple-element.37), channel_id=1, source_target_pairs={{1,2},{3,4},{5,6},{7,8},{9,10},{11,12},{13,14},{2,1},{4,3},{6,5},{... | collective-permute-start | bytes 1966088 | tf_op jit(solution)/shard_map/ppermute | solution.py:271
  6.7 36.0 %collective-permute-start.2 = (bf16[256,512]{1,0:T(8,128)(2,1)S(1)}, bf16[256,512]{1,0:T(8,128)(2,1)S(1)}, u32[]{:S(2)}, u32[]{:S(2)}) collective-permute-start(bf16[256,512]{1,0:T(8,128)(2,1)S(1)} %get-tuple-element.39), channel_id=1, source_target_pairs={{0,1},{2,3},{4,5},{6,7},{8,9},{10,11},{12,13},{14,15},{1,0},{3,2},... | collective-permute-start | bytes 786440 | tf_op jit(solution)/shard_map/ppermute | solution.py:271
  11.2 31.6 %collective-permute-start.3 = (bf16[256,512]{1,0:T(8,128)(2,1)S(1)}, bf16[256,512]{1,0:T(8,128)(2,1)S(1)}, u32[]{:S(2)}, u32[]{:S(2)}) collective-permute-start(bf16[256,512]{1,0:T(8,128)(2,1)S(1)} %get-tuple-element.40), channel_id=1, source_target_pairs={{1,2},{3,4},{5,6},{7,8},{9,10},{11,12},{13,14},{2,1},{4,3},{6,5},{... | collective-permute-start | bytes 786440 | tf_op jit(solution)/shard_map/ppermute | solution.py:271
  11.9 1.2 %copy-start.2 = (bf16[1,1024,512]{2,1,0:T(8,128)(2,1)S(1)}, bf16[1,1024,512]{2,1,0:T(8,128)(2,1)}, u32[]{:S(2)}) copy-start(bf16[1,1024,512]{2,1,0:T(8,128)(2,1)} %param.5) | copy-start | bytes 3145732
  13.1 2.1 %copy-start.3 = (bf16[1,8,15,128,128]{4,3,2,1,0:T(8,128)(2,1)S(1)}, bf16[1,8,15,128,128]{4,3,2,1,0:T(8,128)(2,1)}, u32[]{:S(2)}) copy-start(bf16[1,8,15,128,128]{4,3,2,1,0:T(8,128)(2,1)} %param.8) | copy-start | bytes 11796484
  15.2 0.7 copy-start.4
  15.9 8.5 %copy-start = (bf16[1,1024,512]{2,1,0:T(8,128)(2,1)S(1)}, bf16[1,1024,512]{2,1,0:T(8,128)(2,1)}, u32[]{:S(2)}) copy-start(bf16[1,1024,512]{2,1,0:T(8,128)(2,1)} %param.9) | copy-start | bytes 3145732
  15.9 8.5 %copy-start.1 = (bf16[512,512]{1,0:T(8,128)(2,1)S(1)}, bf16[512,512]{1,0:T(8,128)(2,1)}, u32[]{:S(2)}) copy-start(bf16[512,512]{1,0:T(8,128)(2,1)} %weight_ref.7) | copy-start | bytes 1572868
  25.7 34.1 %collective-permute-start.5 = (bf16[512,512]{1,0:T(8,128)(2,1)S(1)}, bf16[512,512]{1,0:T(8,128)(2,1)S(1)}, u32[]{:S(2)}, u32[]{:S(2)}) collective-permute-start(bf16[512,512]{1,0:T(8,128)(2,1)S(1)} %get-tuple-element.38.mid_ref), channel_id=1, source_target_pairs={{0,1},{2,3},{4,5},{6,7},{8,9},{10,11},{12,13},{14,15},{1,0},{3,2},... | collective-permute-start | bytes 1572872 | tf_op jit(solution)/shard_map/ppermute | solution.py:271
  42.1 17.7 %collective-permute-start.6 = (bf16[512,512]{1,0:T(8,128)(2,1)S(1)}, bf16[512,512]{1,0:T(8,128)(2,1)S(1)}, u32[]{:S(2)}, u32[]{:S(2)}) collective-permute-start(bf16[512,512]{1,0:T(8,128)(2,1)S(1)} %get-tuple-element.38.mid_ref), channel_id=1, source_target_pairs={{1,2},{3,4},{5,6},{7,8},{9,10},{11,12},{13,14},{2,1},{4,3},{6,5},{... | collective-permute-start | bytes 1572872 | tf_op jit(solution)/shard_map/ppermute | solution.py:271
  45.1 12.8 %collective-permute-start.4 = (f32[256,512]{1,0:T(8,128)S(1)}, f32[256,512]{1,0:T(8,128)S(1)}, u32[]{:S(2)}, u32[]{:S(2)}) collective-permute-start(f32[256,512]{1,0:T(8,128)S(1)} %get-tuple-element.66), channel_id=1, source_target_pairs={{0,16},{16,0},{1,17},{17,1},{2,18},{18,2},{3,19},{19,3},{4,20},{20... | collective-permute-start | bytes 1572872 | tf_op jit(solution)/shard_map/ppermute | solution.py:281
  45.2 41.5 %collective-permute-start.13 = (bf16[384,512]{1,0:T(8,128)(2,1)S(1)}, bf16[384,512]{1,0:T(8,128)(2,1)S(1)}, u32[]{:S(2)}, u32[]{:S(2)}) collective-permute-start(bf16[384,512]{1,0:T(8,128)(2,1)S(1)} %get-tuple-element.56), channel_id=1, source_target_pairs={{0,1},{2,3},{4,5},{6,7},{8,9},{10,11},{12,13},{14,15},{1,0},{3,2},... | collective-permute-start | bytes 1179656 | tf_op jit(solution)/shard_map/ppermute | solution.py:271
  54.4 32.3 %collective-permute-start.14 = (bf16[384,512]{1,0:T(8,128)(2,1)S(1)}, bf16[384,512]{1,0:T(8,128)(2,1)S(1)}, u32[]{:S(2)}, u32[]{:S(2)}) collective-permute-start(bf16[384,512]{1,0:T(8,128)(2,1)S(1)} %get-tuple-element.57), channel_id=1, source_target_pairs={{1,2},{3,4},{5,6},{7,8},{9,10},{11,12},{13,14},{2,1},{4,3},{6,5},{... | collective-permute-start | bytes 1179656 | tf_op jit(solution)/shard_map/ppermute | solution.py:271
  60.6 16.5 %copy-start.5 = (f32[1024,512]{1,0:T(8,128)}, f32[1024,512]{1,0:T(8,128)S(1)}, u32[]{:S(2)}) copy-start(f32[1024,512]{1,0:T(8,128)S(1)} %get-tuple-element.50.near_ref) | copy-start | bytes 6291460
  60.8 16.6 %collective-permute-start.7 = (bf16[64,512]{1,0:T(8,128)(2,1)S(1)}, bf16[64,512]{1,0:T(8,128)(2,1)S(1)}, u32[]{:S(2)}, u32[]{:S(2)}) collective-permute-start(bf16[64,512]{1,0:T(8,128)(2,1)S(1)} %get-tuple-element.69), channel_id=1, source_target_pairs={{0,4},{4,0},{8,12},{12,8},{1,5},{5,1},{9,13},{13,9},{2,6},{6,2},{1... | collective-permute-start | bytes 196616 | tf_op jit(solution)/shard_map/ppermute | solution.py:281
  74.7 4.3 %collective-permute-start.8 = (bf16[64,512]{1,0:T(8,128)(2,1)S(1)}, bf16[64,512]{1,0:T(8,128)(2,1)S(1)}, u32[]{:S(2)}, u32[]{:S(2)}) collective-permute-start(bf16[64,512]{1,0:T(8,128)(2,1)S(1)} %get-tuple-element.68), channel_id=1, source_target_pairs={{0,8},{4,12},{8,0},{12,4},{1,9},{5,13},{9,1},{13,5},{2,10},{6,14},... | collective-permute-start | bytes 196616 | tf_op jit(solution)/shard_map/ppermute | solution.py:281
  76.2 5.2 %collective-permute-start.9 = (bf16[64,512]{1,0:T(8,128)(2,1)S(1)}, bf16[64,512]{1,0:T(8,128)(2,1)S(1)}, u32[]{:S(2)}, u32[]{:S(2)}) collective-permute-start(bf16[64,512]{1,0:T(8,128)(2,1)S(1)} %get-tuple-element.67), channel_id=1, source_target_pairs={{0,12},{4,8},{8,4},{12,0},{1,13},{5,9},{9,5},{13,1},{2,14},{6,10},... | collective-permute-start | bytes 196616 | tf_op jit(solution)/shard_map/ppermute | solution.py:281
  81.4 7.8 %collective-permute-start.10 = (bf16[64,512]{1,0:T(8,128)(2,1)S(1)}, bf16[64,512]{1,0:T(8,128)(2,1)S(1)}, u32[]{:S(2)}, u32[]{:S(2)}) collective-permute-start(bf16[64,512]{1,0:T(8,128)(2,1)S(1)} %add_convert_fusion.1), channel_id=1, source_target_pairs={{0,1},{1,0},{2,3},{3,2},{4,5},{5,4},{6,7},{7,6},{8,9},{9,8},{10,11... | collective-permute-start | bytes 196616 | tf_op jit(solution)/shard_map/ppermute | solution.py:281
  83.3 11.2 %collective-permute-start.11 = (bf16[64,512]{1,0:T(8,128)(2,1)S(1)}, bf16[64,512]{1,0:T(8,128)(2,1)S(1)}, u32[]{:S(2)}, u32[]{:S(2)}) collective-permute-start(bf16[64,512]{1,0:T(8,128)(2,1)S(1)} %add_convert_fusion.1), channel_id=1, source_target_pairs={{0,2},{1,3},{2,0},{3,1},{4,6},{5,7},{6,4},{7,5},{8,10},{9,11},{10,... | collective-permute-start | bytes 196616 | tf_op jit(solution)/shard_map/ppermute | solution.py:281
  85.3 9.2 %collective-permute-start.12 = (bf16[64,512]{1,0:T(8,128)(2,1)S(1)}, bf16[64,512]{1,0:T(8,128)(2,1)S(1)}, u32[]{:S(2)}, u32[]{:S(2)}) collective-permute-start(bf16[64,512]{1,0:T(8,128)(2,1)S(1)} %add_convert_fusion.1), channel_id=1, source_target_pairs={{0,3},{1,2},{2,1},{3,0},{4,7},{5,6},{6,5},{7,4},{8,11},{9,10},{10,... | collective-permute-start | bytes 196616 | tf_op jit(solution)/shard_map/ppermute | solution.py:281
  94.5 1.3 %collective-permute-start.15 = (bf16[64,512]{1,0:T(8,128)(2,1)S(1)}, bf16[64,512]{1,0:T(8,128)(2,1)S(1)}, u32[]{:S(2)}, u32[]{:S(2)}) collective-permute-start(bf16[64,512]{1,0:T(8,128)(2,1)S(1)} %add_convert_fusion), channel_id=1, source_target_pairs={{0,16},{16,0},{1,17},{17,1},{2,18},{18,2},{3,19},{19,3},{4,20},{20... | collective-permute-start | bytes 196616 | tf_op jit(solution)/shard_map/ppermute | solution.py:281
  95.9 8.7 %collective-permute-start.16 = (bf16[128,512]{1,0:T(8,128)(2,1)S(1)}, bf16[128,512]{1,0:T(8,128)(2,1)S(1)}, u32[]{:S(2)}, u32[]{:S(2)}) collective-permute-start(bf16[128,512]{1,0:T(8,128)(2,1)S(1)} %bitcast.17), channel_id=1, source_target_pairs={{0,4},{4,0},{8,12},{12,8},{1,5},{5,1},{9,13},{13,9},{2,6},{6,2},{1... | collective-permute-start | bytes 393224 | tf_op jit(solution)/shard_map/ppermute | solution.py:281
  99.1 8.1 %collective-permute-start.17 = (bf16[128,512]{1,0:T(8,128)(2,1)S(1)}, bf16[128,512]{1,0:T(8,128)(2,1)S(1)}, u32[]{:S(2)}, u32[]{:S(2)}) collective-permute-start(bf16[128,512]{1,0:T(8,128)(2,1)S(1)} %bitcast.18), channel_id=1, source_target_pairs={{0,8},{4,12},{8,0},{12,4},{1,9},{5,13},{9,1},{13,5},{2,10},{6,14},... | collective-permute-start | bytes 393224 | tf_op jit(solution)/shard_map/ppermute | solution.py:281
  99.2 8.0 %collective-permute-start.18 = (bf16[128,512]{1,0:T(8,128)(2,1)S(1)}, bf16[128,512]{1,0:T(8,128)(2,1)S(1)}, u32[]{:S(2)}, u32[]{:S(2)}) collective-permute-start(bf16[128,512]{1,0:T(8,128)(2,1)S(1)} %bitcast.19), channel_id=1, source_target_pairs={{0,12},{4,8},{8,4},{12,0},{1,13},{5,9},{9,5},{13,1},{2,14},{6,10},... | collective-permute-start | bytes 393224 | tf_op jit(solution)/shard_map/ppermute | solution.py:281
  100.7 1.6 %copy-start.6 = (f32[1024,512]{1,0:T(8,128)S(1)}, f32[1024,512]{1,0:T(8,128)}, u32[]{:S(2)}) copy-start(f32[1024,512]{1,0:T(8,128)} %copy-done.5) | copy-start | bytes 6291460

commit v7 on v4

--- a/solution.py
+++ b/solution.py
@@ -353,12 +353,12 @@
     term = jnp.sum(term.astype(F32), axis=0)
     term = term.astype(BF16)
     parts = [term, *from_all(lambda d: term, "rep")]
+    parts, three = lax.optimization_barrier((parts, three))
     feat_grad = kernel_call(
         back_kernel, [*held(last, near), *three, weight], [plain(rows)], 12 * product,
         out_specs=[anywhere()],
         scratch_shapes=[pltpu.VMEM((zones, width), BF16), pltpu.SemaphoreType.DMA((tiles,))],
     )[0]
-    parts, feat_grad = lax.optimization_barrier((parts, feat_grad))
     term = pairwise(parts).astype(BF16)
     other, = from_all(lambda d: term, LEVEL[0])
     term = jnp.where(lax.axis_index(LEVEL[0]) == 0, jnp.stack([term, other]), jnp.stack([other, term]))

time: 108 us -> 107 us (level)
  the two profiles are of different devices: /device:TPU:16 before, /device:TPU:0 now
where the time goes in v7:
time: 107 us; the launch traced here: 106 us
  starting transfers between devices  54 us (50%)
  Pallas kernels  19.9 us (19%)
  waiting for transfers between devices  19.5 us (18%)
  local copies, waits for them, and re-layouts  9.16 us (9%)
  matrix products  1.72 us (2%)
  other arithmetic  1.17 us (1%)
    ppermute x8, starting transfers between devices, swapped(): result.append(lax.ppermute(x, LINE, pairs + [(j, i) for i, j in pairs]))  34.8 us
    pallas_call x8, Pallas kernels, kernel_call(): pl.pallas_call(body, out_shape=outs, in_specs=specs or [whole()] * len(in...  19.9 us
    all_to_all x1, waiting for transfers between devices, shards(): lax.all_to_all(term.astype(BF16).reshape(lax.axis_size(LEVEL), -1, width)...  11.8 us
    all_to_all x1, starting transfers between devices, shards(): lax.all_to_all(term.astype(BF16).reshape(lax.axis_size(LEVEL), -1, width)...  9.61 us
    ppermute x7, starting transfers between devices, from_all(): lax.ppermute(parts(d), axis, [(j, partner(j, d, n)) for j in range(n)])  9.56 us
    unnamed x22, local copies, waits for them, and re-layouts  9.16 us
    ppermute x7, waiting for transfers between devices, from_all(): lax.ppermute(parts(d), axis, [(j, partner(j, d, n)) for j in range(n)])  7.65 us
  transfers between devices with their start and end apart: 16, of which 5 were waited for; matrix products, arithmetic and copies ran while one was open for 3% of the time, Pallas kernels for 16%

profile of v7, /device:TPU:0, one launch (start us, length us, event | category | flops | bytes accessed | tf_op | source)
XLA Modules:
  0.0 106.3 jit_solution(1862804331500673139)
XLA Ops:
  0.6 1.5 %shard_map.77 = (bf16[640,512]{1,0:T(8,128)(2,1)S(1)}, bf16[640,512]{1,0:T(8,128)(2,1)S(1)}, bf16[256,512]{1,0:T(8,128)(2,1)S(1)}, bf16[256,512]{1,0:T(8,128)(2,1)S(1)}) custom-call(bf16[1024,512]{1,0:T(8,128)(2,1)} %bitcast.16), custom_call_target="tpu_custom_call" | custom-call | tf_op jit(solution)/shard_map/pallas_call | solution.py:245
  2.1 3.1 %collective-permute-start = (bf16[640,512]{1,0:T(8,128)(2,1)S(1)}, bf16[640,512]{1,0:T(8,128)(2,1)S(1)}, u32[]{:S(2)}, u32[]{:S(2)}) collective-permute-start(bf16[640,512]{1,0:T(8,128)(2,1)S(1)} %get-tuple-element.29), channel_id=1, source_target_pairs={{0,1},{2,3},{4,5},{6,7},{8,9},{10,11},{12,13},{14,15},{1,0},{3,2},... | collective-permute-start | bytes 1966088 | tf_op jit(solution)/shard_map/ppermute | solution.py:261
  5.2 0.7 collective-permute-start.1
  5.9 4.4 %collective-permute-start.2 = (bf16[256,512]{1,0:T(8,128)(2,1)S(1)}, bf16[256,512]{1,0:T(8,128)(2,1)S(1)}, u32[]{:S(2)}, u32[]{:S(2)}) collective-permute-start(bf16[256,512]{1,0:T(8,128)(2,1)S(1)} %get-tuple-element.32), channel_id=1, source_target_pairs={{0,1},{2,3},{4,5},{6,7},{8,9},{10,11},{12,13},{14,15},{1,0},{3,2},... | collective-permute-start | bytes 786440 | tf_op jit(solution)/shard_map/ppermute | solution.py:261
  11.0 1.2 %copy-done.4 = bf16[1,1024,512]{2,1,0:T(8,128)(2,1)S(1)} copy-done((bf16[1,1024,512]{2,1,0:T(8,128)(2,1)S(1)}, bf16[1,1024,512]{2,1,0:T(8,128)(2,1)}, u32[]{:S(2)}) %copy-start.4) | copy-done | bytes 1048600
  12.2 2.1 %copy-done.5 = bf16[1,8,15,128,128]{4,3,2,1,0:T(8,128)(2,1)S(1)} copy-done((bf16[1,8,15,128,128]{4,3,2,1,0:T(8,128)(2,1)S(1)}, bf16[1,8,15,128,128]{4,3,2,1,0:T(8,128)(2,1)}, u32[]{:S(2)}) %copy-start.5) | copy-done | bytes 3932184
  15.0 6.9 %shard_map.76 = (bf16[4,16,256,128]{3,2,1,0:T(8,128)(2,1)S(1)}, f32[1024,512]{1,0:T(8,128)S(1)}) custom-call(s32[8,15]{1,0:T(8,128)S(1)} %bitcast.23, bf16[8,15,128,128]{3,2,1,0:T(8,128)(2,1)S(1)} %bitcast.22, bf16[1024,512]{1,0:T(8,128)(2,1)S(1)} %bitcast.17), custom_call_target="tpu_custom_call" | custom-call | flops 2147483648 | tf_op jit(solution)/shard_map/pallas_call | solution.py:245
  22.0 1.3 %shard_map.78 = (bf16[512,512]{1,0:T(8,128)(2,1)S(1)}, bf16[512,512]{1,0:T(8,128)(2,1)S(1)}) custom-call(bf16[4,16,256,128]{3,2,1,0:T(8,128)(2,1)S(1)} %get-tuple-element.27.band_ref, f32[1024,512]{1,0:T(8,128)S(1)} %get-tuple-element.28.near_ref, bf16[640,512]{1,0:T(8,128)(2,1)S(1)} %collective-permute-done.first5_ref, ...), custom_call_target="tpu_custom_call" | custom-call | flops 536870912 | tf_op jit(solution)/shard_map/pallas_call | solution.py:245
  23.3 18.0 %collective-permute-start.4 = (bf16[512,512]{1,0:T(8,128)(2,1)S(1)}, bf16[512,512]{1,0:T(8,128)(2,1)S(1)}, u32[]{:S(2)}, u32[]{:S(2)}) collective-permute-start(bf16[512,512]{1,0:T(8,128)(2,1)S(1)} %get-tuple-element.31.mid_ref), channel_id=1, source_target_pairs={{0,1},{2,3},{4,5},{6,7},{8,9},{10,11},{12,13},{14,15},{1,0},{3,2},... | collective-permute-start | bytes 1572872 | tf_op jit(solution)/shard_map/ppermute | solution.py:261
  41.2 1.5 %collective-permute-start.5 = (bf16[512,512]{1,0:T(8,128)(2,1)S(1)}, bf16[512,512]{1,0:T(8,128)(2,1)}, u32[]{:S(2)}, u32[]{:S(2)}) collective-permute-start(bf16[512,512]{1,0:T(8,128)(2,1)S(1)} %get-tuple-element.31.mid_ref), channel_id=1, source_target_pairs={{1,2},{3,4},{5,6},{7,8},{9,10},{11,12},{13,14},{2,1},{4,3},{6,5},{... | collective-permute-start | bytes 1572872 | tf_op jit(solution)/shard_map/ppermute | solution.py:261
  42.7 1.3 %shard_map.79 = (bf16[512,512]{1,0:T(8,128)(2,1)S(1)}, bf16[512,512]{1,0:T(8,128)(2,1)S(1)}, bf16[384,512]{1,0:T(8,128)(2,1)S(1)}, bf16[384,512]{1,0:T(8,128)(2,1)S(1)}) custom-call(bf16[4,16,256,128]{3,2,1,0:T(8,128)(2,1)S(1)} %get-tuple-element.27.band_ref, f32[1024,512]{1,0:T(8,128)S(1)} %get-tuple-element.28.near_ref, ...), custom_call_target="tpu_custom_call" | custom-call | flops 536870912 | tf_op jit(solution)/shard_map/pallas_call | solution.py:245
  44.5 1.3 %fusion = bf16[512,512]{1,0:T(8,128)(2,1)} fusion(f32[512,512]{1,0:T(8,128)S(1)} %fusion.1, bf16[512,512]{1,0:T(8,128)(2,1)S(1)} %get-tuple-element.35.mixed_mid_ref, bf16[512,512]{1,0:T(8,128)(2,1)S(1)} %get-tuple-element.31.mid_ref), kind=kOutput, calls=%fused_computation.1 | convolution fusion | flops 268959744 | bytes 2621440 | tf_op jit(solution)/shard_map/dot_general | solution.py:297
  45.8 9.6 %all-to-all-start = ((bf16[8,64,512]{2,1,0:T(8,128)(2,1)}), bf16[8,64,512]{2,1,0:T(8,128)(2,1)}, u32[]{:S(2)}, u32[]{:S(2)}) async-start(bf16[8,64,512]{2,1,0:T(8,128)(2,1)} %bitcast.24), calls=%async_computation | async-start | bytes 1048576 | tf_op jit(solution)/shard_map/all_to_all | solution.py:349
  56.1 5.9 %collective-permute-start.9 = (bf16[384,512]{1,0:T(8,128)(2,1)}, bf16[384,512]{1,0:T(8,128)(2,1)}, u32[]{:S(2)}, u32[]{:S(2)}) collective-permute-start(bf16[384,512]{1,0:T(8,128)(2,1)} %copy-done.6), channel_id=1, source_target_pairs={{0,1},{2,3},{4,5},{6,7},{8,9},{10,11},{12,13},{14,15},{1,0},{3,2},... | collective-permute-start | bytes 1179656 | tf_op jit(solution)/shard_map/ppermute | solution.py:261
  61.9 2.2 %copy-done.1 = bf16[4,16,256,128]{3,2,1,0:T(8,128)(2,1)S(1)} copy-done((bf16[4,16,256,128]{3,2,1,0:T(8,128)(2,1)S(1)}, bf16[4,16,256,128]{3,2,1,0:T(8,128)(2,1)}, u32[]{:S(2)}) %copy-start.1) | copy-done | bytes 4194328
  64.1 2.8 %shard_map.80 = (f32[1024,512]{1,0:T(8,128)S(1)}, bf16[1024,512]{1,0:T(8,128)(2,1)}) custom-call(bf16[4,16,256,128]{3,2,1,0:T(8,128)(2,1)S(1)} %copy-done.1, bf16[512,512]{1,0:T(8,128)(2,1)S(1)} %get-tuple-element.31.mid_ref, bf16[512,512]{1,0:T(8,128)(2,1)S(1)} %get-tuple-element.34.end_ref, bf16[512,512]{1,0:T(8,128)(2,1)S(1)} %get-tuple-element.35.mixed_mid_ref, ...), custom_call_target="tpu_custom_call" | custom-call | flops 536870912 | tf_op jit(solution)/shard_map/pallas_call | solution.py:245
  66.9 1.8 %shard_map.81 = (f32[1024,512]{1,0:T(8,128)S(1)}, bf16[4,4,256,128]{3,2,1,0:T(8,128)(2,1)S(1)}) custom-call(bf16[4,16,256,128]{3,2,1,0:T(8,128)(2,1)S(1)} %copy-done.1, f32[1024,512]{1,0:T(8,128)S(1)} %get-tuple-element.38.near_ref, bf16[512,512]{1,0:T(8,128)(2,1)S(1)} %collective-permute-done.4.first4_ref, bf16[512,512]{1,0:T(8,128)(2,1)} %collective-permute-done.5.second4_ref), custom_call_target="tpu_custom_call" | custom-call | flops 6442450944 | tf_op jit(solution)/shard_map/pallas_call | solution.py:245
  68.7 1.3 %copy-done.9 = f32[1024,512]{1,0:T(8,128)} copy-done((f32[1024,512]{1,0:T(8,128)}, f32[1024,512]{1,0:T(8,128)S(1)}, u32[]{:S(2)}) %copy-start.9) | copy-done | bytes 2097176
  70.1 11.8 %all-to-all-done = bf16[8,64,512]{2,1,0:T(8,128)(2,1)} async-done(((bf16[8,64,512]{2,1,0:T(8,128)(2,1)}), bf16[8,64,512]{2,1,0:T(8,128)(2,1)}, u32[]{:S(2)}, u32[]{:S(2)}) %all-to-all-start) | async-done | bytes 524320 | tf_op jit(solution)/shard_map/all_to_all | solution.py:349
  81.9 1.1 %reduce_sum.12 = bf16[64,512]{1,0:T(8,128)(2,1)S(1)} reduce(bf16[8,64,512]{2,1,0:T(8,128)(2,1)} %all-to-all-done, bf16[]{:T(256)} %constant.3.clone.1), dimensions={0}, to_apply=%region_0.0 | reduce | flops 229376 | bytes 589826 | tf_op jit(solution)/shard_map/reduce_sum | solution.py:353
  83.0 3.5 %collective-permute-start.6 = (bf16[64,512]{1,0:T(8,128)(2,1)S(1)}, bf16[64,512]{1,0:T(8,128)(2,1)S(1)}, u32[]{:S(2)}, u32[]{:S(2)}) collective-permute-start(bf16[64,512]{1,0:T(8,128)(2,1)S(1)} %reduce_sum.12), channel_id=1, source_target_pairs={{0,1},{1,0},{2,3},{3,2},{4,5},{5,4},{6,7},{7,6},{8,9},{9,8},{10,11... | collective-permute-start | bytes 196616 | tf_op jit(solution)/shard_map/ppermute | solution.py:272
  86.5 1.8 %collective-permute-start.7 = (bf16[64,512]{1,0:T(8,128)(2,1)S(1)}, bf16[64,512]{1,0:T(8,128)(2,1)S(1)}, u32[]{:S(2)}, u32[]{:S(2)}) collective-permute-start(bf16[64,512]{1,0:T(8,128)(2,1)S(1)} %reduce_sum.12), channel_id=1, source_target_pairs={{0,2},{1,3},{2,0},{3,1},{4,6},{5,7},{6,4},{7,5},{8,10},{9,11},{10,... | collective-permute-start | bytes 196616 | tf_op jit(solution)/shard_map/ppermute | solution.py:272
  88.9 4.5 %collective-permute-done.7 = bf16[64,512]{1,0:T(8,128)(2,1)S(1)} collective-permute-done((bf16[64,512]{1,0:T(8,128)(2,1)S(1)}, bf16[64,512]{1,0:T(8,128)(2,1)S(1)}, u32[]{:S(2)}, u32[]{:S(2)}) %collective-permute-start.7) | collective-permute-done | bytes 65568 | tf_op jit(solution)/shard_map/ppermute | solution.py:272
  93.5 1.0 collective-permute-done.8
  94.6 1.2 %collective-permute-done.11 = bf16[64,512]{1,0:T(8,128)(2,1)S(1)} collective-permute-done((bf16[64,512]{1,0:T(8,128)(2,1)S(1)}, bf16[64,512]{1,0:T(8,128)(2,1)S(1)}, u32[]{:S(2)}, u32[]{:S(2)}) %collective-permute-start.11) | collective-permute-done | bytes 65568 | tf_op jit(solution)/shard_map/ppermute | solution.py:272
  95.9 1.2 %collective-permute-start.12 = (bf16[128,512]{1,0:T(8,128)(2,1)S(1)}, bf16[128,512]{1,0:T(8,128)(2,1)S(1)}, u32[]{:S(2)}, u32[]{:S(2)}) collective-permute-start(bf16[128,512]{1,0:T(8,128)(2,1)S(1)} %bitcast.18), channel_id=1, source_target_pairs={{0,4},{4,0},{8,12},{12,8},{1,5},{5,1},{9,13},{13,9},{2,6},{6,2},{1... | collective-permute-start | bytes 393224 | tf_op jit(solution)/shard_map/ppermute | solution.py:272
  97.1 1.6 %collective-permute-start.13 = (bf16[128,512]{1,0:T(8,128)(2,1)S(1)}, bf16[128,512]{1,0:T(8,128)(2,1)S(1)}, u32[]{:S(2)}, u32[]{:S(2)}) collective-permute-start(bf16[128,512]{1,0:T(8,128)(2,1)S(1)} %bitcast.19), channel_id=1, source_target_pairs={{0,8},{4,12},{8,0},{12,4},{1,9},{5,13},{9,1},{13,5},{2,10},{6,14},... | collective-permute-start | bytes 393224 | tf_op jit(solution)/shard_map/ppermute | solution.py:272
  98.7 0.8 collective-permute-start.14
  99.4 1.6 %copy-done.10 = f32[1024,512]{1,0:T(8,128)S(1)} copy-done((f32[1024,512]{1,0:T(8,128)S(1)}, f32[1024,512]{1,0:T(8,128)}, u32[]{:S(2)}) %copy-start.10) | copy-done | bytes 2097176
  101.0 3.3 %shard_map.82 = bf16[1024,512]{1,0:T(8,128)(2,1)} custom-call(bf16[4,4,256,128]{3,2,1,0:T(8,128)(2,1)S(1)} %get-tuple-element.39.last_ref, f32[1024,512]{1,0:T(8,128)S(1)} %copy-done.10, bf16[384,512]{1,0:T(8,128)(2,1)} %collective-permute-done.9.first3_ref, bf16[384,512]{1,0:T(8,128)(2,1)S(1)} %collective-permute-done.10.second3_ref, ...), custom_call_target="tpu_custom_call" | custom-call | flops 6442450944 | tf_op jit(solution)/shard_map/pallas_call | solution.py:245
  104.4 0.8 collective-permute-done.13.refs_2_
  105.2 1.1 shard_map.83
  (35 shorter events, 3.3 us)
Async XLA Ops:
  2.1 19.8 %collective-permute-start = (bf16[640,512]{1,0:T(8,128)(2,1)S(1)}, bf16[640,512]{1,0:T(8,128)(2,1)S(1)}, u32[]{:S(2)}, u32[]{:S(2)}) collective-permute-start(bf16[640,512]{1,0:T(8,128)(2,1)S(1)} %get-tuple-element.29), channel_id=1, source_target_pairs={{0,1},{2,3},{4,5},{6,7},{8,9},{10,11},{12,13},{14,15},{1,0},{3,2},... | collective-permute-start | bytes 1966088 | tf_op jit(solution)/shard_map/ppermute | solution.py:261
  5.2 16.7 %collective-permute-start.1 = (bf16[640,512]{1,0:T(8,128)(2,1)S(1)}, bf16[640,512]{1,0:T(8,128)(2,1)S(1)}, u32[]{:S(2)}, u32[]{:S(2)}) collective-permute-start(bf16[640,512]{1,0:T(8,128)(2,1)S(1)} %get-tuple-element.30), channel_id=1, source_target_pairs={{1,2},{3,4},{5,6},{7,8},{9,10},{11,12},{13,14},{2,1},{4,3},{6,5},{... | collective-permute-start | bytes 1966088 | tf_op jit(solution)/shard_map/ppermute | solution.py:261
  5.9 36.8 %collective-permute-start.2 = (bf16[256,512]{1,0:T(8,128)(2,1)S(1)}, bf16[256,512]{1,0:T(8,128)(2,1)S(1)}, u32[]{:S(2)}, u32[]{:S(2)}) collective-permute-start(bf16[256,512]{1,0:T(8,128)(2,1)S(1)} %get-tuple-element.32), channel_id=1, source_target_pairs={{0,1},{2,3},{4,5},{6,7},{8,9},{10,11},{12,13},{14,15},{1,0},{3,2},... | collective-permute-start | bytes 786440 | tf_op jit(solution)/shard_map/ppermute | solution.py:261
  10.3 32.4 %collective-permute-start.3 = (bf16[256,512]{1,0:T(8,128)(2,1)S(1)}, bf16[256,512]{1,0:T(8,128)(2,1)S(1)}, u32[]{:S(2)}, u32[]{:S(2)}) collective-permute-start(bf16[256,512]{1,0:T(8,128)(2,1)S(1)} %get-tuple-element.33), channel_id=1, source_target_pairs={{1,2},{3,4},{5,6},{7,8},{9,10},{11,12},{13,14},{2,1},{4,3},{6,5},{... | collective-permute-start | bytes 786440 | tf_op jit(solution)/shard_map/ppermute | solution.py:261
  11.0 1.2 %copy-start.4 = (bf16[1,1024,512]{2,1,0:T(8,128)(2,1)S(1)}, bf16[1,1024,512]{2,1,0:T(8,128)(2,1)}, u32[]{:S(2)}) copy-start(bf16[1,1024,512]{2,1,0:T(8,128)(2,1)} %param.5) | copy-start | bytes 3145732
  12.2 2.1 %copy-start.5 = (bf16[1,8,15,128,128]{4,3,2,1,0:T(8,128)(2,1)S(1)}, bf16[1,8,15,128,128]{4,3,2,1,0:T(8,128)(2,1)}, u32[]{:S(2)}) copy-start(bf16[1,8,15,128,128]{4,3,2,1,0:T(8,128)(2,1)} %param.8) | copy-start | bytes 11796484
  14.3 0.7 copy-start.8
  15.0 6.9 %copy-start.2 = (bf16[512,512]{1,0:T(8,128)(2,1)S(1)}, bf16[512,512]{1,0:T(8,128)(2,1)}, u32[]{:S(2)}) copy-start(bf16[512,512]{1,0:T(8,128)(2,1)} %weight_ref.7) | copy-start | bytes 1572868
  15.0 6.9 %copy-start.3 = (bf16[1,1024,512]{2,1,0:T(8,128)(2,1)S(1)}, bf16[1,1024,512]{2,1,0:T(8,128)(2,1)}, u32[]{:S(2)}) copy-start(bf16[1,1024,512]{2,1,0:T(8,128)(2,1)} %param.9) | copy-start | bytes 3145732
  21.9 20.8 %copy-start = (bf16[4,16,256,128]{3,2,1,0:T(8,128)(2,1)}, bf16[4,16,256,128]{3,2,1,0:T(8,128)(2,1)S(1)}, u32[]{:S(2)}) copy-start(bf16[4,16,256,128]{3,2,1,0:T(8,128)(2,1)S(1)} %get-tuple-element.27.band_ref) | copy-start | bytes 12582916
  23.3 43.6 %collective-permute-start.4 = (bf16[512,512]{1,0:T(8,128)(2,1)S(1)}, bf16[512,512]{1,0:T(8,128)(2,1)S(1)}, u32[]{:S(2)}, u32[]{:S(2)}) collective-permute-start(bf16[512,512]{1,0:T(8,128)(2,1)S(1)} %get-tuple-element.31.mid_ref), channel_id=1, source_target_pairs={{0,1},{2,3},{4,5},{6,7},{8,9},{10,11},{12,13},{14,15},{1,0},{3,2},... | collective-permute-start | bytes 1572872 | tf_op jit(solution)/shard_map/ppermute | solution.py:261
  41.2 25.6 %collective-permute-start.5 = (bf16[512,512]{1,0:T(8,128)(2,1)S(1)}, bf16[512,512]{1,0:T(8,128)(2,1)}, u32[]{:S(2)}, u32[]{:S(2)}) collective-permute-start(bf16[512,512]{1,0:T(8,128)(2,1)S(1)} %get-tuple-element.31.mid_ref), channel_id=1, source_target_pairs={{1,2},{3,4},{5,6},{7,8},{9,10},{11,12},{13,14},{2,1},{4,3},{6,5},{... | collective-permute-start | bytes 1572872 | tf_op jit(solution)/shard_map/ppermute | solution.py:261
  44.0 1.7 %copy-start.6 = (bf16[384,512]{1,0:T(8,128)(2,1)}, bf16[384,512]{1,0:T(8,128)(2,1)S(1)}, u32[]{:S(2)}) copy-start(bf16[384,512]{1,0:T(8,128)(2,1)S(1)} %get-tuple-element.43) | copy-start | bytes 1179652
  44.0 1.7 %copy-start.7 = (bf16[384,512]{1,0:T(8,128)(2,1)}, bf16[384,512]{1,0:T(8,128)(2,1)S(1)}, u32[]{:S(2)}) copy-start(bf16[384,512]{1,0:T(8,128)(2,1)S(1)} %get-tuple-element.44) | copy-start | bytes 1179652
  45.8 36.1 %all-to-all-start = ((bf16[8,64,512]{2,1,0:T(8,128)(2,1)}), bf16[8,64,512]{2,1,0:T(8,128)(2,1)}, u32[]{:S(2)}, u32[]{:S(2)}) async-start(bf16[8,64,512]{2,1,0:T(8,128)(2,1)} %bitcast.24), calls=%async_computation | async-start | bytes 1048576 | tf_op jit(solution)/shard_map/all_to_all | solution.py:349
  55.4 33.6 %collective-permute-start.10 = (bf16[384,512]{1,0:T(8,128)(2,1)}, bf16[384,512]{1,0:T(8,128)(2,1)S(1)}, u32[]{:S(2)}, u32[]{:S(2)}) collective-permute-start(bf16[384,512]{1,0:T(8,128)(2,1)} %copy-done.7), channel_id=1, source_target_pairs={{1,2},{3,4},{5,6},{7,8},{9,10},{11,12},{13,14},{2,1},{4,3},{6,5},{... | collective-permute-start | bytes 1179656 | tf_op jit(solution)/shard_map/ppermute | solution.py:261
  56.1 32.9 %collective-permute-start.9 = (bf16[384,512]{1,0:T(8,128)(2,1)}, bf16[384,512]{1,0:T(8,128)(2,1)}, u32[]{:S(2)}, u32[]{:S(2)}) collective-permute-start(bf16[384,512]{1,0:T(8,128)(2,1)} %copy-done.6), channel_id=1, source_target_pairs={{0,1},{2,3},{4,5},{6,7},{8,9},{10,11},{12,13},{14,15},{1,0},{3,2},... | collective-permute-start | bytes 1179656 | tf_op jit(solution)/shard_map/ppermute | solution.py:261
  61.9 2.2 %copy-start.1 = (bf16[4,16,256,128]{3,2,1,0:T(8,128)(2,1)S(1)}, bf16[4,16,256,128]{3,2,1,0:T(8,128)(2,1)}, u32[]{:S(2)}) copy-start(bf16[4,16,256,128]{3,2,1,0:T(8,128)(2,1)} %copy-done) | copy-start | bytes 12582916
  68.7 1.3 %copy-start.9 = (f32[1024,512]{1,0:T(8,128)}, f32[1024,512]{1,0:T(8,128)S(1)}, u32[]{:S(2)}) copy-start(f32[1024,512]{1,0:T(8,128)S(1)} %get-tuple-element.41.near_ref) | copy-start | bytes 6291460
  83.0 6.0 %collective-permute-start.6 = (bf16[64,512]{1,0:T(8,128)(2,1)S(1)}, bf16[64,512]{1,0:T(8,128)(2,1)S(1)}, u32[]{:S(2)}, u32[]{:S(2)}) collective-permute-start(bf16[64,512]{1,0:T(8,128)(2,1)S(1)} %reduce_sum.12), channel_id=1, source_target_pairs={{0,1},{1,0},{2,3},{3,2},{4,5},{5,4},{6,7},{7,6},{8,9},{9,8},{10,11... | collective-permute-start | bytes 196616 | tf_op jit(solution)/shard_map/ppermute | solution.py:272
  86.5 7.0 %collective-permute-start.7 = (bf16[64,512]{1,0:T(8,128)(2,1)S(1)}, bf16[64,512]{1,0:T(8,128)(2,1)S(1)}, u32[]{:S(2)}, u32[]{:S(2)}) collective-permute-start(bf16[64,512]{1,0:T(8,128)(2,1)S(1)} %reduce_sum.12), channel_id=1, source_target_pairs={{0,2},{1,3},{2,0},{3,1},{4,6},{5,7},{6,4},{7,5},{8,10},{9,11},{10,... | collective-permute-start | bytes 196616 | tf_op jit(solution)/shard_map/ppermute | solution.py:272
  88.3 6.2 %collective-permute-start.8 = (bf16[64,512]{1,0:T(8,128)(2,1)S(1)}, bf16[64,512]{1,0:T(8,128)(2,1)S(1)}, u32[]{:S(2)}, u32[]{:S(2)}) collective-permute-start(bf16[64,512]{1,0:T(8,128)(2,1)S(1)} %reduce_sum.12), channel_id=1, source_target_pairs={{0,3},{1,2},{2,1},{3,0},{4,7},{5,6},{6,5},{7,4},{8,11},{9,10},{10,... | collective-permute-start | bytes 196616 | tf_op jit(solution)/shard_map/ppermute | solution.py:272
  94.5 1.3 %collective-permute-start.11 = (bf16[64,512]{1,0:T(8,128)(2,1)S(1)}, bf16[64,512]{1,0:T(8,128)(2,1)S(1)}, u32[]{:S(2)}, u32[]{:S(2)}) collective-permute-start(bf16[64,512]{1,0:T(8,128)(2,1)S(1)} %add_convert_fusion), channel_id=1, source_target_pairs={{0,16},{16,0},{1,17},{17,1},{2,18},{18,2},{3,19},{19,3},{4,20},{20... | collective-permute-start | bytes 196616 | tf_op jit(solution)/shard_map/ppermute | solution.py:272
  95.9 8.5 %collective-permute-start.12 = (bf16[128,512]{1,0:T(8,128)(2,1)S(1)}, bf16[128,512]{1,0:T(8,128)(2,1)S(1)}, u32[]{:S(2)}, u32[]{:S(2)}) collective-permute-start(bf16[128,512]{1,0:T(8,128)(2,1)S(1)} %bitcast.18), channel_id=1, source_target_pairs={{0,4},{4,0},{8,12},{12,8},{1,5},{5,1},{9,13},{13,9},{2,6},{6,2},{1... | collective-permute-start | bytes 393224 | tf_op jit(solution)/shard_map/ppermute | solution.py:272
  97.1 8.1 %collective-permute-start.13 = (bf16[128,512]{1,0:T(8,128)(2,1)S(1)}, bf16[128,512]{1,0:T(8,128)(2,1)S(1)}, u32[]{:S(2)}, u32[]{:S(2)}) collective-permute-start(bf16[128,512]{1,0:T(8,128)(2,1)S(1)} %bitcast.19), channel_id=1, source_target_pairs={{0,8},{4,12},{8,0},{12,4},{1,9},{5,13},{9,1},{13,5},{2,10},{6,14},... | collective-permute-start | bytes 393224 | tf_op jit(solution)/shard_map/ppermute | solution.py:272
  98.7 6.5 %collective-permute-start.14 = (bf16[128,512]{1,0:T(8,128)(2,1)S(1)}, bf16[128,512]{1,0:T(8,128)(2,1)S(1)}, u32[]{:S(2)}, u32[]{:S(2)}) collective-permute-start(bf16[128,512]{1,0:T(8,128)(2,1)S(1)} %bitcast.20), channel_id=1, source_target_pairs={{0,12},{4,8},{8,4},{12,0},{1,13},{5,9},{9,5},{13,1},{2,14},{6,10},... | collective-permute-start | bytes 393224 | tf_op jit(solution)/shard_map/ppermute | solution.py:272
  99.4 1.6 %copy-start.10 = (f32[1024,512]{1,0:T(8,128)S(1)}, f32[1024,512]{1,0:T(8,128)}, u32[]{:S(2)}) copy-start(f32[1024,512]{1,0:T(8,128)} %copy-done.9) | copy-start | bytes 6291460
